TPU v7x, 32 devices: a whole 2x2x4 slice. The times are simulated.
32 devices in a mesh: grp: 2 (over core), ctx: 4 (over z), wsh: 4 (over y, x).
Axes of the slice: x: 2, y: 2, z: 4, core: 2. Of those that a mesh axis runs over, the one named last changes fastest.
Arguments:
- tokens: bfloat16 [6144, 1152], P(('grp', 'ctx', 'wsh')), may hold values from -6 to 6
- segment_ids: int32 [6144], P(('grp', 'ctx', 'wsh')), may hold values from 0 to 1, as said below
- positions: int32 [6144], P(('grp', 'ctx', 'wsh')), may hold values from 0 to 3071, as said below
- attend_gain: float32 [1152], replicated, may hold values from 0.5 to 1.5
- query_key_value: bfloat16 [1152, 1920], P('wsh'), may hold values from -0.25 to 0.25
- attend_out: bfloat16 [1152, 1152], P('wsh'), may hold values from -2 to 2
- feed_gain: float32 [1152], replicated, may hold values from 0.5 to 1.5
- gate_up: bfloat16 [1152, 6144], P('wsh'), may hold values from -0.1875 to 0.1875
- down_weight: bfloat16 [3072, 1152], P('wsh'), may hold values from -0.4375 to 0.4375
- upstream: bfloat16 [6144, 1152], P(('grp', 'ctx', 'wsh')), may hold values from -6 to 6
Outputs:
- activations: bfloat16 [6144, 1152], P(('grp', 'ctx', 'wsh'))
- input_grad: float32 [6144, 1152], P(('grp', 'ctx', 'wsh'))
- query_key_value_grad: float32 [1152, 1920], P(('ctx', 'wsh'))
- attend_out_grad: float32 [1152, 1152], P(('ctx', 'wsh'))
- gate_up_grad: float32 [1152, 6144], P(('ctx', 'wsh'))
- down_weight_grad: float32 [3072, 1152], P(('ctx', 'wsh'))
- attend_gain_grad: float32 [1152], P(('ctx', 'wsh'))
- feed_gain_grad: float32 [1152], P(('ctx', 'wsh'))
Inputs may be any that keep to these rules, and one draw needn't show every extreme that they name: `segment_ids`: in each group of 3072 rows the aligned runs of 96 rows are the runs of 96 consecutive tokens of that group's token stream, in some order, each once; the stream is the prompt of 2048 tokens (segment 0) followed by 1 continuations of 1024 tokens (segments 1 to 1). `positions`: matching segment_ids: a prompt token's position is its index in the prompt; a continuation token's position is 2048 plus its index in its continuation.
All inputs are finite; a program needn't handle non-finite values.
Results may differ from a plain program's by a relative error of at most 0.02.
Values may be sent and summed in bfloat16 or wider, within the bound.
A program may use at most 256 MiB of HBM per device.

v0:
```python
import math

import jax
import jax.numpy as jnp
from jax import lax
from jax.sharding import PartitionSpec as P

HEADS = 18
KV_HEADS = 6
HEAD_DIM = 64
FF = 3072
KTILE = 1024
QW = 1152
KW = 384


EPSILON = 1e-05


def rope_angles(positions):
    halfway = HEAD_DIM // 2
    frequency = jnp.exp(jnp.arange(halfway, dtype=jnp.float32) * (-math.log(10000.0) / halfway))
    angles = positions.astype(jnp.float32)[:, None] * frequency[None, :]
    return (jnp.cos(angles), jnp.sin(angles))


def rotate(tensor, cosine, sine_table):
    halfway = tensor.shape[-1] // 2
    first_half = tensor[..., :halfway]
    second_half = tensor[..., halfway:]
    cos_wide = cosine[:, None, :]
    sin_wide = sine_table[:, None, :]
    return jnp.concatenate(
        [
            first_half * cos_wide - second_half * sin_wide,
            second_half * cos_wide + first_half * sin_wide,
        ],
        axis=-1,
    )


def unrotate(gradient, cosine, sine_table):
    halfway = gradient.shape[-1] // 2
    first_half = gradient[..., :halfway]
    second_half = gradient[..., halfway:]
    cos_wide = cosine[:, None, :]
    sin_wide = sine_table[:, None, :]
    return jnp.concatenate(
        [
            first_half * cos_wide + second_half * sin_wide,
            second_half * cos_wide - first_half * sin_wide,
        ],
        axis=-1,
    )


def rms_factor(values):
    return lax.rsqrt(jnp.mean(values * values, axis=-1, keepdims=True) + EPSILON)


def norm_back(grad_normed, inputs, factor, gain):
    weighted = grad_normed * gain
    inner_mean = jnp.mean(weighted * inputs, axis=-1, keepdims=True)
    input_part = factor * weighted - inputs * (factor * factor * factor) * inner_mean
    return (input_part, jnp.sum(grad_normed * inputs * factor, axis=0))


def rounded(values):
    return lax.optimization_barrier(values.astype(jnp.bfloat16)).astype(jnp.float32)


def tile_mask(segment_ids, positions, seg_key, pos_key):
    return (pos_key[None, :] <= positions[:, None]) & (
        (seg_key[None, :] == 0) | (seg_key[None, :] == segment_ids[:, None])
    )


def tile_scores(queries, key_tile, allowed):
    raw_scores = jnp.einsum(
        "nhjd,khd->hjnk", queries, key_tile, preferred_element_type=jnp.float32
    ) * HEAD_DIM ** (-0.5)
    return jnp.where(allowed, raw_scores, -1e30)


def split_tiles(key_all, value_all, seg_all, pos_all):
    tile_count = key_all.shape[0] // KTILE
    key_tiles = key_all.reshape(tile_count, KTILE, KV_HEADS, HEAD_DIM)
    value_tiles = value_all.reshape(tile_count, KTILE, KV_HEADS, HEAD_DIM)
    return (
        key_tiles,
        value_tiles,
        seg_all.reshape(tile_count, KTILE),
        pos_all.reshape(tile_count, KTILE),
    )


def attend_forward(queries, key_all, value_all, seg_all, pos_all, segment_ids, positions):
    local_rows = queries.shape[0]
    head_ratio = HEADS // KV_HEADS
    key_tiles, value_tiles, seg_tiles, pos_tiles = split_tiles(key_all, value_all, seg_all, pos_all)

    def stats_step(state_pair, pieces):
        running_max, running_sum = state_pair
        key_tile, seg_key, pos_key = pieces
        allowed = tile_mask(segment_ids, positions, seg_key, pos_key)
        scores = tile_scores(queries, key_tile, allowed)
        new_max = jnp.maximum(running_max, jnp.max(scores, axis=-1))
        expons = jnp.where(allowed, jnp.exp(scores - new_max[..., None]), 0.0)
        new_sum = running_sum * jnp.exp(running_max - new_max) + jnp.sum(expons, axis=-1)
        return ((new_max, new_sum), None)

    start_max = jnp.full((KV_HEADS, head_ratio, local_rows), -1e30, jnp.float32)
    start_sum = jnp.zeros((KV_HEADS, head_ratio, local_rows), jnp.float32)
    (row_max, row_sum), _ = lax.scan(
        stats_step, (start_max, start_sum), (key_tiles, seg_tiles, pos_tiles)
    )
    log_total = row_max + jnp.log(row_sum)

    def value_step(running, pieces):
        key_tile, value_tile, seg_key, pos_key = pieces
        allowed = tile_mask(segment_ids, positions, seg_key, pos_key)
        scores = tile_scores(queries, key_tile, allowed)
        weights_tile = jnp.where(allowed, jnp.exp(scores - log_total[..., None]), 0.0).astype(
            jnp.bfloat16
        )
        return (
            running
            + jnp.einsum(
                "hjnk,khd->nhjd", weights_tile, value_tile, preferred_element_type=jnp.float32
            ),
            None,
        )

    start_out = jnp.zeros((local_rows, KV_HEADS, head_ratio, HEAD_DIM), jnp.float32)
    output, _ = lax.scan(value_step, start_out, (key_tiles, value_tiles, seg_tiles, pos_tiles))
    return (output, log_total)


def attend_backward(
    queries,
    key_all,
    value_all,
    seg_all,
    pos_all,
    segment_ids,
    positions,
    log_total,
    output_grad,
    output,
):
    key_count = key_all.shape[0]
    key_tiles, value_tiles, seg_tiles, pos_tiles = split_tiles(key_all, value_all, seg_all, pos_all)
    row_delta = jnp.einsum("nhjd,nhjd->hjn", output_grad.astype(jnp.float32), output)

    def grad_step(query_sum, pieces):
        key_tile, value_tile, seg_key, pos_key = pieces
        allowed = tile_mask(segment_ids, positions, seg_key, pos_key)
        scores = tile_scores(queries, key_tile, allowed)
        weights_tile = jnp.where(allowed, jnp.exp(scores - log_total[..., None]), 0.0)
        value_grad = jnp.einsum(
            "hjnk,nhjd->khd",
            weights_tile.astype(jnp.bfloat16),
            output_grad,
            preferred_element_type=jnp.float32,
        )
        weight_grad = jnp.einsum(
            "nhjd,khd->hjnk", output_grad, value_tile, preferred_element_type=jnp.float32
        )
        score_grad = (weights_tile * (weight_grad - row_delta[..., None])).astype(jnp.bfloat16)
        query_sum = query_sum + jnp.einsum(
            "hjnk,khd->nhjd", score_grad, key_tile, preferred_element_type=jnp.float32
        )
        key_grad = jnp.einsum(
            "hjnk,nhjd->khd", score_grad, queries, preferred_element_type=jnp.float32
        )
        return (query_sum, (key_grad, value_grad))

    start_query = jnp.zeros(queries.shape, jnp.float32)
    query_sum, (key_grads, value_grads) = lax.scan(
        grad_step, start_query, (key_tiles, value_tiles, seg_tiles, pos_tiles)
    )
    scale_factor = HEAD_DIM ** (-0.5)
    return (
        query_sum * scale_factor,
        key_grads.reshape(key_count, KW) * scale_factor,
        value_grads.reshape(key_count, KW),
    )


def local(
    tokens,
    segment_ids,
    positions,
    attend_gain,
    query_key_value,
    attend_out,
    feed_gain,
    gate_up,
    down_weight,
    upstream,
):
    local_rows = tokens.shape[0]
    head_ratio = HEADS // KV_HEADS
    inputs = tokens.astype(jnp.float32)
    factor_one = rms_factor(inputs)
    normed_one = (inputs * factor_one * attend_gain).astype(jnp.bfloat16)
    full_qkv, full_out, full_gate_up, full_down = (
        lax.all_gather(query_key_value, "wsh", axis=0, tiled=True),
        lax.all_gather(attend_out, "wsh", axis=0, tiled=True),
        lax.all_gather(gate_up, "wsh", axis=0, tiled=True),
        lax.all_gather(down_weight, "wsh", axis=0, tiled=True),
    )
    projected = jnp.dot(normed_one, full_qkv, preferred_element_type=jnp.float32)
    cosine, sine_table = rope_angles(positions)
    queries = rotate(
        projected[:, :QW].reshape(local_rows, HEADS, HEAD_DIM), cosine, sine_table
    ).astype(jnp.bfloat16)
    queries = queries.reshape(local_rows, KV_HEADS, head_ratio, HEAD_DIM)
    key_local = (
        rotate(
            projected[:, QW : QW + KW].reshape(local_rows, KV_HEADS, HEAD_DIM), cosine, sine_table
        )
        .astype(jnp.bfloat16)
        .reshape(local_rows, KW)
    )
    value_local = projected[:, QW + KW :].astype(jnp.bfloat16)
    key_all, value_all, seg_all, pos_all = (
        lax.all_gather(key_local, ("ctx", "wsh"), axis=0, tiled=True),
        lax.all_gather(value_local, ("ctx", "wsh"), axis=0, tiled=True),
        lax.all_gather(segment_ids, ("ctx", "wsh"), axis=0, tiled=True),
        lax.all_gather(positions, ("ctx", "wsh"), axis=0, tiled=True),
    )
    output, log_total = attend_forward(
        queries, key_all, value_all, seg_all, pos_all, segment_ids, positions
    )
    attended = output.reshape(local_rows, QW).astype(jnp.bfloat16)
    middle = inputs + jnp.dot(attended, full_out, preferred_element_type=jnp.float32)
    factor_two = rms_factor(middle)
    normed_two = (middle * factor_two * feed_gain).astype(jnp.bfloat16)
    gate_value = jnp.dot(normed_two, full_gate_up, preferred_element_type=jnp.float32)
    gate_part = gate_value[:, :FF]
    up_part = gate_value[:, FF:]
    sigmoid_gate = jax.nn.sigmoid(gate_part)
    silu_gate = gate_part * sigmoid_gate
    hidden = (silu_gate * up_part).astype(jnp.bfloat16)
    activations = (middle + jnp.dot(hidden, full_down, preferred_element_type=jnp.float32)).astype(
        jnp.bfloat16
    )
    back_qkv, back_out, back_gate_up, back_down = (
        lax.all_gather(query_key_value, "wsh", axis=0, tiled=True),
        lax.all_gather(attend_out, "wsh", axis=0, tiled=True),
        lax.all_gather(gate_up, "wsh", axis=0, tiled=True),
        lax.all_gather(down_weight, "wsh", axis=0, tiled=True),
    )
    down_grad = jnp.dot(hidden.T, upstream, preferred_element_type=jnp.float32)
    hidden_grad = jnp.dot(upstream, back_down.T, preferred_element_type=jnp.float32)
    gate_grad = hidden_grad * up_part * sigmoid_gate * (1.0 + gate_part * (1.0 - sigmoid_gate))
    up_grad = hidden_grad * silu_gate
    joint_grad = jnp.concatenate([gate_grad, up_grad], axis=1).astype(jnp.bfloat16)
    gate_up_grad = jnp.dot(normed_two.T, joint_grad, preferred_element_type=jnp.float32)
    normed_two_grad = jnp.dot(joint_grad, back_gate_up.T, preferred_element_type=jnp.float32)
    middle_part, feed_gain_grad = norm_back(normed_two_grad, middle, factor_two, feed_gain)
    middle_grad = upstream.astype(jnp.float32) + middle_part
    branch_grad = middle_grad.astype(jnp.bfloat16)
    out_weight_grad = jnp.dot(attended.T, branch_grad, preferred_element_type=jnp.float32)
    attended_grad = jnp.dot(branch_grad, back_out.T, preferred_element_type=jnp.float32).astype(
        jnp.bfloat16
    )
    attended_grad = attended_grad.reshape(local_rows, KV_HEADS, head_ratio, HEAD_DIM)
    query_grad, key_grad_all, value_grad_all = attend_backward(
        queries,
        key_all,
        value_all,
        seg_all,
        pos_all,
        segment_ids,
        positions,
        log_total,
        attended_grad,
        output,
    )
    key_grad, value_grad = (
        lax.psum_scatter(key_grad_all, ("ctx", "wsh"), scatter_dimension=0, tiled=True),
        lax.psum_scatter(value_grad_all, ("ctx", "wsh"), scatter_dimension=0, tiled=True),
    )
    query_back = unrotate(
        rounded(query_grad).reshape(local_rows, HEADS, HEAD_DIM), cosine, sine_table
    ).reshape(local_rows, QW)
    key_back = unrotate(
        rounded(key_grad).reshape(local_rows, KV_HEADS, HEAD_DIM), cosine, sine_table
    ).reshape(local_rows, KW)
    projected_grad = jnp.concatenate(
        [
            query_back.astype(jnp.bfloat16),
            key_back.astype(jnp.bfloat16),
            value_grad.astype(jnp.bfloat16),
        ],
        axis=1,
    )
    qkv_grad = jnp.dot(normed_one.T, projected_grad, preferred_element_type=jnp.float32)
    normed_one_grad = jnp.dot(projected_grad, back_qkv.T, preferred_element_type=jnp.float32)
    input_part, attend_gain_grad = norm_back(normed_one_grad, inputs, factor_one, attend_gain)
    input_grad = middle_grad + input_part
    shares = (
        lax.psum_scatter(qkv_grad, ("ctx", "wsh"), scatter_dimension=0, tiled=True),
        lax.psum_scatter(out_weight_grad, ("ctx", "wsh"), scatter_dimension=0, tiled=True),
        lax.psum_scatter(gate_up_grad, ("ctx", "wsh"), scatter_dimension=0, tiled=True),
        lax.psum_scatter(down_grad, ("ctx", "wsh"), scatter_dimension=0, tiled=True),
        lax.psum_scatter(attend_gain_grad, ("ctx", "wsh"), scatter_dimension=0, tiled=True),
        lax.psum_scatter(feed_gain_grad, ("ctx", "wsh"), scatter_dimension=0, tiled=True),
    )
    shares = (
        lax.psum(shares[0].astype(jnp.bfloat16), "grp").astype(jnp.float32),
        lax.psum(shares[1].astype(jnp.bfloat16), "grp").astype(jnp.float32),
        lax.psum(shares[2].astype(jnp.bfloat16), "grp").astype(jnp.float32),
        lax.psum(shares[3].astype(jnp.bfloat16), "grp").astype(jnp.float32),
        lax.psum(shares[4].astype(jnp.bfloat16), "grp").astype(jnp.float32),
        lax.psum(shares[5].astype(jnp.bfloat16), "grp").astype(jnp.float32),
    )
    return (
        activations,
        input_grad,
        shares[0],
        shares[1],
        shares[2],
        shares[3],
        shares[4],
        shares[5],
    )


def solution(mesh):
    in_specs = (
        P(("grp", "ctx", "wsh"), None),
        P(("grp", "ctx", "wsh")),
        P(("grp", "ctx", "wsh")),
        P(),
        P("wsh", None),
        P("wsh", None),
        P(),
        P("wsh", None),
        P("wsh", None),
        P(("grp", "ctx", "wsh"), None),
    )
    out_specs = (
        P(("grp", "ctx", "wsh"), None),
        P(("grp", "ctx", "wsh"), None),
        P(("ctx", "wsh"), None),
        P(("ctx", "wsh"), None),
        P(("ctx", "wsh"), None),
        P(("ctx", "wsh"), None),
        P(("ctx", "wsh")),
        P(("ctx", "wsh")),
    )
    return jax.shard_map(local, mesh=mesh, in_specs=in_specs, out_specs=out_specs, check_vma=False)
```

profile of v0, /device:TPU:0, one launch (start us, length us, event | category | flops | bytes accessed | tf_op | source)
XLA Modules:
  0.0 1910.0 jit_solution(1182851010017177751)
XLA Ops:
  10.6 56.6 %all-gather.7.cloned.1.call-done = bf16[1152,1920]{1,0:T(8,128)(2,1)} async-done(((bf16[288,1920]{1,0:T(8,128)(2,1)}), bf16[1152,1920]{1,0:T(8,128)(2,1)}) %all-gather.7.cloned.1.call-update) | async-done | bytes 4423696 | tf_op jit(solution)/shard_map/all_gather | solution.py:208
  67.2 3.7 fusion.69
  77.2 76.3 %all-reduce.6 = (s32[3072]{0:T(1024)S(1)}, s32[3072]{0:T(1024)S(1)}) all-reduce(s32[3072]{0:T(1024)S(1)} %dynamic-update-slice, s32[3072]{0:T(1024)S(1)} %dynamic-update-slice.1), channel_id=1, replica_groups=mesh['grp'=2,'ctx'=4,'wsh'=4] {'ctx','wsh'}, use_global_device_ids=true, to_apply=%add | all-reduce | flops 6144 | bytes 49152
  154.3 8.1 reshape.216
  162.4 6.0 copy.46
  168.4 31.3 %all-gather.9.cloned.1.call-done = bf16[3072,384]{1,0:T(8,128)(2,1)} async-done(((bf16[192,384]{1,0:T(8,128)(2,1)}), bf16[3072,384]{1,0:T(8,128)(2,1)}) %all-gather.9.cloned.1.call-update) | async-done | bytes 2359312 | tf_op jit(solution)/shard_map/all_gather | solution.py:229
  199.8 8.1 reshape.215
  207.9 7.2 copy.45
  215.0 24.5 %while.39 = (s32[]{:T(128)}, f32[6,3,192]{2,1,0:T(4,128)S(1)}, f32[6,3,192]{2,1,0:T(4,128)S(1)}, s32[3,1024]{1,0:T(4,128)S(1)}, s32[192]{0:T(256)S(1)}, /*index=...) while((s32[]{:T(128)}, f32[6,3,192]{2,1,0:T(4,128)S(1)}, ...), condition=%wide.region_4.5_spmd.clone, body=%wide.region_1.4_spmd.clone.sunk | while | flops 482101120 | bytes 30485644 | solution.py:114
  218.6 4.6 select_reduce_fusion.2
  226.8 4.5 select_reduce_fusion.2
  235.0 4.6 select_reduce_fusion.2
  240.2 40.5 %while.40 = (s32[]{:T(128)}, f32[192,6,3,64]{0,3,2,1:T(8,128)}, bf16[3,1024,6,64]{1,3,2,0:T(8,128)(2,1)}, s32[3,1024]{1,0:T(4,128)S(1)}, s32[192]{0:T(256)S(1)},...) while((s32[]{:T(128)}, f32[192,6,3,64]{0,3,2,1:T(8,128)}, ...), condition=%wide.region_6.7_spmd.clone, body=%wide.region_5.6_spmd.clone.sunk | while | flops 924894208 | bytes 4674702 | solution.py:135
  253.1 7.9 fusion.126
  262.7 8.2 fusion.126
  272.5 8.2 fusion.126
  282.9 3.7 multiply_reduce_fusion.2
  286.6 90.9 %all-gather.15.cloned.1.call-done = bf16[1152,6144]{1,0:T(8,128)(2,1)} async-done(((bf16[288,6144]{1,0:T(8,128)(2,1)}), bf16[1152,6144]{1,0:T(8,128)(2,1)}) %all-gather.15.cloned.1.call-update) | async-done | bytes 14155792 | tf_op jit(solution)/shard_map/all_gather | solution.py:210
  377.5 11.0 fusion.75
  388.5 67.5 %all-gather.17.cloned.1.call-done = bf16[3072,1152]{1,0:T(8,128)(2,1)} async-done(((bf16[768,1152]{1,0:T(8,128)(2,1)}), bf16[3072,1152]{1,0:T(8,128)(2,1)}) %all-gather.17.cloned.1.call-update) | async-done | bytes 7077904 | tf_op jit(solution)/shard_map/all_gather | solution.py:211
  456.0 8.8 multiply_convert_fusion.1
  464.8 11.3 multiply_reduce_fusion
  483.2 67.5 %while.41 = (s32[]{:T(128)}, f32[192,6,3,64]{0,3,2,1:T(8,128)}, f32[3,1024,6,64]{1,3,2,0:T(8,128)}, f32[3,1024,6,64]{1,3,2,0:T(8,128)}, bf16[3,1024,6,64]{1,3,2,...) while((s32[]{:T(128)}, f32[192,6,3,64]{0,3,2,1:T(8,128)}, ...), condition=%wide.region_10.11_spmd.clone, body=%wide.region_9.10_spmd.clone.sunk | while | flops 2308621312 | bytes 81001752 | solution.py:179
  487.4 6.0 bitcast_dynamic-update-slice_fusion.5
  493.5 7.3 fusion.138
  509.8 6.1 bitcast_dynamic-update-slice_fusion.5
  515.8 7.3 fusion.138
  532.1 6.0 bitcast_dynamic-update-slice_fusion.5
  538.2 7.4 fusion.138
  548.1 2.7 bitcast_dynamic-update-slice_fusion.4
  550.8 5.5 broadcast_multiply_fusion
  556.3 9.2 copy.76
  565.5 10.3 reshape.207
  575.9 9.2 copy.77
  585.2 10.4 reshape.209
  596.9 3.3 fusion.65
  602.1 111.5 %reduce-scatter.19.cloned.1.call-done = f32[192,384]{1,0:T(8,128)} async-done(((f32[3072,384]{1,0:T(8,128)}), f32[192,384]{1,0:T(8,128)}) %reduce-scatter.19.cloned.1.call-update) | async-done | bytes 294928
  714.7 141.0 %reduce-scatter.21.cloned.1.call-done = f32[192,384]{1,0:T(8,128)} async-done(((f32[3072,384]{1,0:T(8,128)}), f32[192,384]{1,0:T(8,128)}) %reduce-scatter.21.cloned.1.call-update) | async-done | bytes 294928
  857.0 5.0 fusion.63
  863.0 8.6 fusion.77
  872.7 12.6 fusion.51
  886.1 114.8 %reduce-scatter.25.cloned.1.call-done = f32[72,1152]{1,0:T(8,128)} async-done(((f32[1152,1152]{1,0:T(8,128)}), f32[72,1152]{1,0:T(8,128)}) %reduce-scatter.25.cloned.1.call-update) | async-done | bytes 331792
  1002.5 170.1 %reduce-scatter.23.cloned.1.call-done = f32[72,1920]{1,0:T(8,128)} async-done(((f32[1152,1920]{1,0:T(8,128)}), f32[72,1920]{1,0:T(8,128)}) %reduce-scatter.23.cloned.1.call-update) | async-done | bytes 552976
  1174.4 224.2 %reduce-scatter.17.cloned.1.call-done = f32[192,1152]{1,0:T(8,128)} async-done(((f32[3072,1152]{1,0:T(8,128)}), f32[192,1152]{1,0:T(8,128)}) %reduce-scatter.17.cloned.1.call-update) | async-done | bytes 884752 | tf_op jit(solution)/shard_map/reduce_scatter | solution.py:308
  1400.6 402.7 %reduce-scatter.15.cloned.1.call-done = f32[72,6144]{1,0:T(8,128)} async-done(((f32[1152,6144]{1,0:T(8,128)}), f32[72,6144]{1,0:T(8,128)}) %reduce-scatter.15.cloned.1.call-update) | async-done | bytes 1769488 | tf_op jit(solution)/shard_map/reduce_scatter | solution.py:307
  1805.8 5.9 fusion.49
  1811.7 4.1 fusion.62
  1815.8 74.7 %all-reduce.7 = (bf16[1152]{0:T(1024)(128)(2,1)S(1)}, bf16[1152]{0:T(1024)(128)(2,1)S(1)}) all-reduce(f32[1152]{0:T(1024)S(1)} %get-tuple-element.388, f32[1152]{0:T(1024)S(1)} %copy-done.29), channel_id=8, replica_groups=mesh['grp'=2,'ctx'=4,'wsh'=4] {'ctx','wsh'}, use_global_device_ids=true, to_apply=%region_23.24.clone | all-reduce | flops 2304 | bytes 13824
  (212 shorter events, 87.9 us)
Async XLA Ops:
  7.2 60.0 %all-gather.7.cloned.1.call-start = ((), (), s32[]{:S(2)}) async-start(), calls=%async_computation.6 | async-start | bytes 5529600 | tf_op jit(solution)/shard_map/all_gather | solution.py:208
  7.9 146.4 %all-gather.11.cloned.1.call-start = ((), (), s32[]{:S(2)}) async-start(), calls=%async_computation.8 | async-start | bytes 2506752 | tf_op jit(solution)/shard_map/all_gather | solution.py:228
  10.4 60.5 %copy-start.26 = (f32[192]{0:T(256)}, f32[192]{0:T(256)S(1)}, u32[]{:S(2)}) copy-start(f32[192]{0:T(256)S(1)} %get-tuple-element.488) | copy-start | bytes 2308
  10.6 143.4 %copy-start.14 = (f32[192,32]{0,1:T(8,128)}, f32[192,32]{0,1:T(8,128)S(1)}, u32[]{:S(2)}) copy-start(f32[192,32]{0,1:T(8,128)S(1)} %get-tuple-element.485) | copy-start | bytes 73732
  10.6 143.4 %copy-start.16 = (f32[192,32]{0,1:T(8,128)}, f32[192,32]{0,1:T(8,128)S(1)}, u32[]{:S(2)}) copy-start(f32[192,32]{0,1:T(8,128)S(1)} %get-tuple-element.486) | copy-start | bytes 73732
  71.2 3.5 copy-start.31
  71.2 4.8 copy-start.19
  72.0 127.7 %all-gather.9.cloned.1.call-start = ((), (), s32[]{:S(2)}) async-start(), calls=%async_computation.7 | async-start | bytes 2506752 | tf_op jit(solution)/shard_map/all_gather | solution.py:229
  72.8 210.1 %all-gather.13.cloned.1.call-start = ((), (), s32[]{:S(2)}) async-start(), calls=%async_computation.9 | async-start | bytes 3317760 | tf_op jit(solution)/shard_map/all_gather | solution.py:209
  73.3 304.2 %all-gather.15.cloned.1.call-start = ((), (), s32[]{:S(2)}) async-start(), calls=%async_computation.10 | async-start | bytes 17694720 | tf_op jit(solution)/shard_map/all_gather | solution.py:210
  73.9 382.0 %all-gather.17.cloned.1.call-start = ((), (), s32[]{:S(2)}) async-start(), calls=%async_computation.11 | async-start | bytes 8847360 | tf_op jit(solution)/shard_map/all_gather | solution.py:211
  74.5 639.0 %reduce-scatter.19.cloned.1.call-start = ((), (), s32[]{:S(2)}) async-start(), calls=%async_computation.14 | async-start | bytes 5013504
  240.2 42.7 %copy-start.7 = (bf16[192,1152]{1,0:T(8,128)(2,1)S(1)}, bf16[192,1152]{1,0:T(8,128)(2,1)}, u32[]{:S(2)}) copy-start(bf16[192,1152]{1,0:T(8,128)(2,1)} %param.16) | copy-start | bytes 1327108
  280.7 107.8 %copy-start.18 = (s32[3,1024]{1,0:T(4,128)}, s32[3,1024]{1,0:T(4,128)S(1)}, u32[]{:S(2)}) copy-start(s32[3,1024]{1,0:T(4,128)S(1)} %get-tuple-element.899) | copy-start | bytes 36868
  280.7 107.8 %copy-start.20 = (s32[192]{0:T(256)}, s32[192]{0:T(256)S(1)}, u32[]{:S(2)}) copy-start(s32[192]{0:T(256)S(1)} %get-tuple-element.902) | copy-start | bytes 2308
  280.7 96.8 %copy-start.21 = (f32[1152]{0:T(1024)S(1)}, f32[1152]{0:T(1024)}, u32[]{:S(2)}) copy-start(f32[1152]{0:T(1024)} %param.22) | copy-start | bytes 13828
  286.6 189.4 %copy-start.24 = (f32[192]{0:T(256)}, f32[192]{0:T(256)S(1)}, u32[]{:S(2)}) copy-start(f32[192]{0:T(256)S(1)} %get-tuple-element.490) | copy-start | bytes 2308
  377.5 78.4 %copy-start.11 = (bf16[192,1152]{1,0:T(8,128)(2,1)S(1)}, bf16[192,1152]{1,0:T(8,128)(2,1)}, u32[]{:S(2)}) copy-start(bf16[192,1152]{1,0:T(8,128)(2,1)} %param.25) | copy-start | bytes 1327108
  456.0 8.8 copy-start.3
  464.7 11.3 copy-start.13
  476.0 2.1 copy-start.9
  487.4 6.1 copy-start.28
  493.5 7.4 copy-start
  503.3 2.7 copy-start.1
  509.8 6.1 copy-start.28
  515.8 7.4 copy-start
  525.7 2.6 copy-start.1
  532.1 6.1 copy-start.28
  538.2 7.4 copy-start
  548.0 2.7 copy-start.1
  575.9 279.8 %reduce-scatter.21.cloned.1.call-start = ((), (), s32[]{:S(2)}) async-start(), calls=%async_computation.15 | async-start | bytes 5013504
  595.6 1.2 copy-start.6
  595.6 1.4 copy-start.10
  595.6 405.3 %reduce-scatter.25.cloned.1.call-start = ((), (), s32[]{:S(2)}) async-start(), calls=%async_computation.17 | async-start | bytes 5640192
  600.2 1.3 copy-start.2
  600.2 1.6 copy-start.15
  600.2 1.6 copy-start.17
  600.2 572.4 %reduce-scatter.23.cloned.1.call-start = ((), (), s32[]{:S(2)}) async-start(), calls=%async_computation.16 | async-start | bytes 9400320
  601.6 255.4 %copy-start.8 = (bf16[192,1152]{1,0:T(8,128)(2,1)S(1)}, bf16[192,1152]{1,0:T(8,128)(2,1)}, u32[]{:S(2)}) copy-start(bf16[192,1152]{1,0:T(8,128)(2,1)} %param.16) | copy-start | bytes 1327108
  601.6 255.4 %copy-start.23 = (f32[1152]{0:T(1024)S(1)}, f32[1152]{0:T(1024)}, u32[]{:S(2)}) copy-start(f32[1152]{0:T(1024)} %param.19) | copy-start | bytes 13828
  601.6 255.4 %copy-start.27 = (f32[192]{0:T(256)S(1)}, f32[192]{0:T(256)}, u32[]{:S(2)}) copy-start(f32[192]{0:T(256)} %copy-done.26) | copy-start | bytes 2308
  862.0 536.7 %reduce-scatter.17.cloned.1.call-start = ((), (), s32[]{:S(2)}) async-start(), calls=%async_computation.13 | async-start | bytes 15040512 | tf_op jit(solution)/shard_map/reduce_scatter | solution.py:308
  871.6 1.2 copy-start.22
  871.6 1.2 copy-start.25
  871.6 931.7 %reduce-scatter.15.cloned.1.call-start = ((), (), s32[]{:S(2)}) async-start(), calls=%async_computation.12 | async-start | bytes 30081024 | tf_op jit(solution)/shard_map/reduce_scatter | solution.py:307
  885.3 1010.0 %all-reduce.12.cloned.1.call-start = ((), (), s32[]{:S(2)}) async-start(), calls=%async_computation.18 | async-start | bytes 3538944 | tf_op jit(solution)/shard_map/psum | solution.py:313
  1811.7 4.1 copy-start.29
  1811.7 82.5 %copy-start.30 = (f32[192]{0:T(256)S(1)}, f32[192]{0:T(256)}, u32[]{:S(2)}) copy-start(f32[192]{0:T(256)} %get-tuple-element.487) | copy-start | bytes 2308
  (3 other events, 3.1 us)
Sparse Core Ops, SparseCore 0:
  9.8 57.3 all-gather.6
  72.1 62.8 all-gather.10
  138.4 61.3 all-gather.8
  201.4 38.7 all-gather.12
  241.9 135.5 all-gather.14
  379.2 76.6 all-gather.16
  576.0 137.4 reduce-scatter.18
  719.6 136.1 reduce-scatter.20
  861.0 139.7 reduce-scatter.24
  1006.4 166.1 reduce-scatter.22
  1178.4 220.1 reduce-scatter.16
  1405.2 398.0 reduce-scatter.14
  1806.6 19.9 all-reduce.11
where the time goes:
time: 1920 us; the launch traced here: 1910 us
  waiting for transfers between devices  1410 us (73%)
  matrix products  173 us (9%)
  blocking collectives  154 us (8%)
  local copies, waits for them, and re-layouts  82.4 us (4%)
  other arithmetic  59.4 us (3%)
    unnamed x17, waiting for transfers between devices  540 us
    reduce_scatter x1, waiting for transfers between devices, local(): lax.psum_scatter(gate_up_grad, ('ctx', 'wsh'), scatter_dimension=0, tiled...  403 us
    reduce_scatter x1, waiting for transfers between devices, local(): lax.psum_scatter(down_grad, ('ctx', 'wsh'), scatter_dimension=0, tiled=True)  224 us
    unnamed x2, blocking collectives  151 us
    all_gather x1, waiting for transfers between devices, local(): lax.all_gather(gate_up, 'wsh', axis=0, tiled=True)  90.9 us
    all_gather x1, waiting for transfers between devices, local(): lax.all_gather(down_weight, 'wsh', axis=0, tiled=True)  67.5 us
    unnamed x73, local copies, waits for them, and re-layouts  62.7 us
    all_gather x1, waiting for transfers between devices, local(): lax.all_gather(query_key_value, 'wsh', axis=0, tiled=True)  56.6 us
  transfers between devices with their start and end apart: 13, of which 10 were waited for; matrix products, arithmetic and copies ran while one was open for 9% of the time, Pallas kernels for 0%

commit v1 on v0

v1 whole, which is shorter than its diff:
```python
import itertools
import math

import jax
import jax.numpy as jnp
from jax import lax
from jax.experimental import pallas as pl
from jax.experimental.pallas import tpu as pltpu
from jax.sharding import PartitionSpec as P

HEADS = 18
KV_HEADS = 6
HEAD_DIM = 64
FF = 3072
D = 1152
QW = 1152
KW = 384
EPSILON = 1e-05
MESH = pl.DeviceIdType.MESH
F32 = jnp.float32
BF = jnp.bfloat16
VMEM_LIMIT = 56 << 20


def dot_general(a, b, ca, cb):
    return lax.dot_general(a, b, (((ca,), (cb,)), ((), ())), preferred_element_type=F32)


class Exchange:
    def __init__(self, sizes):
        self.sizes = sizes

    def place(self, axes, offset):
        where, index = {}, 0
        for axis, step in zip(axes, offset):
            size = self.sizes[axis]
            spot = lax.axis_index(axis)
            if step:
                spot = lax.rem(spot + step, size)
            where[axis] = spot
            index = index * size + spot
        return where, index

    def offsets(self, axes):
        return list(itertools.product(*[range(self.sizes[axis]) for axis in axes]))

    def gather(self, x, axes):
        count = math.prod(self.sizes[axis] for axis in axes)
        return ("peer", x, axes, lambda ref, p: ref, (count,) + x.shape, x.shape)

    def swap(self, x, axes):
        return ("peer", x, axes, lambda ref, p: ref.at[p], x.shape, x.shape[1:])

    def columns(self, x, axes, start, width):
        count = math.prod(self.sizes[axis] for axis in axes)
        source = lambda ref, p: ref.at[:, pl.ds(pl.multiple_of(start + p * width, 128), width)]
        return ("peer", x, axes, source, (count, x.shape[0], width), (x.shape[0], width))

    def owners(self, x):
        return ("owner", x, None, None, x.shape, x.shape[1:])

    def run(self, name, number, ops):
        ctx, wsh = self.sizes["ctx"], self.sizes["wsh"]
        total = 0
        for kind, x, axes, *_ in ops:
            total += ctx if kind == "owner" else math.prod(self.sizes[a] for a in axes)
        peers = {}
        for kind, x, axes, *_ in ops:
            for offset in self.offsets(axes if kind == "peer" else ("ctx", "wsh")):
                axes_of = axes if kind == "peer" else ("ctx", "wsh")
                key = tuple(sorted((a, o) for a, o in zip(axes_of, offset) if o))
                if key:
                    peers[key] = (axes_of, offset)
        count = len(ops)

        def kernel(*refs):
            ins, outs = refs[:count], refs[count : 2 * count]
            bounce = refs[2 * count : 3 * count]
            send, recv, near = refs[3 * count :]
            barrier = pltpu.get_barrier_semaphore()
            for axes, offset in peers.values():
                where, _ = self.place(axes, offset)
                pl.semaphore_signal(barrier, 1, device_id=where, device_id_type=MESH)
            pl.semaphore_wait(barrier, len(peers))
            first, second, remote, late = [], [], [], []
            slot = 0
            for op, (kind, x, axes, source, _, _) in enumerate(ops):
                if kind == "peer":
                    none = tuple(0 for _ in axes)
                    _, me = self.place(axes, none)
                    for offset in self.offsets(axes):
                        where, index = self.place(axes, offset)
                        if any(offset):
                            copy = pltpu.make_async_remote_copy(
                                source(ins[op], index),
                                outs[op].at[me],
                                send.at[slot],
                                recv.at[slot],
                                device_id=where,
                                device_id_type=MESH,
                            )
                            copy.start()
                            remote.append(copy)
                        else:
                            copy = pltpu.make_async_copy(
                                source(ins[op], me), bounce[op], near.at[op]
                            )
                            copy.start()
                            first.append(copy)
                            second.append(
                                pltpu.make_async_copy(bounce[op], outs[op].at[me], near.at[op])
                            )
                        slot += 1
                else:
                    my_c, my_w = lax.axis_index("ctx"), lax.axis_index("wsh")
                    base = slot
                    for k in range(ctx):
                        shard = my_w * ctx + k
                        to_c, to_w = shard // wsh, lax.rem(shard, wsh)
                        own = jnp.logical_and(to_c == my_c, to_w == my_w)
                        copy = pltpu.make_async_remote_copy(
                            ins[op].at[k],
                            outs[op].at[my_c],
                            send.at[base + k],
                            recv.at[base + my_c],
                            device_id={"ctx": to_c, "wsh": to_w},
                            device_id_type=MESH,
                        )
                        inward = pltpu.make_async_copy(ins[op].at[k], bounce[op], near.at[op])
                        outward = pltpu.make_async_copy(
                            bounce[op], outs[op].at[my_c], near.at[op]
                        )

                        @pl.when(jnp.logical_not(own))
                        def _():
                            copy.start()

                        late.append((own, copy, inward, outward))
                    mine = my_c * wsh + my_w
                    from_w = mine // ctx
                    for c in range(ctx):
                        own = jnp.logical_and(my_c == c, from_w == my_w)
                        arrival = pltpu.make_async_remote_copy(
                            ins[op].at[0],
                            outs[op].at[c],
                            send.at[base + c],
                            recv.at[base + c],
                            device_id={"ctx": my_c, "wsh": my_w},
                            device_id_type=MESH,
                        )
                        late.append((own, arrival, None, None))
                    slot += ctx
            for one, two in zip(first, second):
                one.wait()
                two.start()
            for own, copy, inward, outward in late:
                if inward is not None:

                    @pl.when(own)
                    def _():
                        inward.start()
                        inward.wait()
                        outward.start()
                        outward.wait()

            for copy in second:
                copy.wait()
            for own, copy, inward, outward in late:

                @pl.when(jnp.logical_not(own))
                def _():
                    if inward is None:
                        copy.wait_recv()
                    else:
                        copy.wait_send()

            for copy in remote:
                copy.wait()

        return pl.pallas_call(
            kernel,
            name=name,
            out_shape=[jax.ShapeDtypeStruct(op[4], op[1].dtype) for op in ops],
            in_specs=[pl.BlockSpec(memory_space=pl.ANY)] * count,
            out_specs=[pl.BlockSpec(memory_space=pl.ANY)] * count,
            scratch_shapes=[pltpu.VMEM(op[5], op[1].dtype) for op in ops]
            + [
                pltpu.SemaphoreType.DMA((total,)),
                pltpu.SemaphoreType.DMA((total,)),
                pltpu.SemaphoreType.DMA((count,)),
            ],
            compiler_params=pltpu.CompilerParams(
                collective_id=number, has_side_effects=True, vmem_limit_bytes=VMEM_LIMIT
            ),
        )(*[op[1] for op in ops])


def head_plan(w):
    pair, odd = w // 2, w % 2
    start = 9 * pair + 4 * odd
    if odd:
        f_heads, h_heads = [start + 2, start + 3, start + 4], [start, start + 1]
        f_kv, h_kv = 3 * pair + 2, 3 * pair + 1
    else:
        f_heads, h_heads = [start, start + 1, start + 2], [start + 3, start + 4]
        f_kv, h_kv = 3 * pair, 3 * pair + 1
    q_order = [f_heads[0], h_heads[0], f_heads[1], h_heads[1], f_heads[2], None]
    return q_order, [f_kv, h_kv]


def qkv_columns(weight):
    blank = jnp.zeros((weight.shape[0], HEAD_DIM), weight.dtype)
    parts = []
    for w in range(4):
        q_order, kv_order = head_plan(w)
        pieces = [
            blank if h is None else weight[:, h * HEAD_DIM : (h + 1) * HEAD_DIM] for h in q_order
        ]
        for base in (QW, QW + KW):
            pieces += [
                weight[:, base + h * HEAD_DIM : base + (h + 1) * HEAD_DIM] for h in kv_order
            ]
        parts.append(jnp.concatenate(pieces, axis=1))
    return jnp.stack(parts)


def qkv_restore(parts):
    found = {}
    for w in range(4):
        q_order, kv_order = head_plan(w)
        slots = list(q_order) + [HEADS + h for h in kv_order]
        slots += [HEADS + KV_HEADS + h for h in kv_order]
        for at, head in enumerate(slots):
            if head is not None:
                found.setdefault(head, []).append(
                    parts[w][:, at * HEAD_DIM : (at + 1) * HEAD_DIM]
                )
    pieces = []
    for head in range(HEADS + 2 * KV_HEADS):
        term = found[head][0]
        for other in found[head][1:]:
            term = term + other
        pieces.append(term)
    return jnp.concatenate(pieces, axis=1)


def spread_rows(rows, odd):
    n = rows.shape[1]
    half = jnp.zeros((32, n), rows.dtype)
    blank = jnp.zeros((64, n), rows.dtype)
    even_rows = jnp.concatenate(
        [rows[0:64], rows[192:256], rows[64:128], rows[256:288], half, rows[128:192], blank]
    )
    odd_rows = jnp.concatenate(
        [rows[96:160], half, rows[0:32], rows[160:224], rows[32:96], rows[224:288], blank]
    )
    return jnp.where(odd, odd_rows, even_rows)


def collect_rows(wide, odd):
    f0, h0, f1, h1, f2 = (wide[64 * i : 64 * i + 64] for i in range(5))
    even_rows = jnp.concatenate([f0, f1, f2, h0, h1[:32]])
    odd_rows = jnp.concatenate([h0[32:], h1, f0, f1, f2])
    return jnp.where(odd, odd_rows, even_rows)


def turn(x, cos, sin, lanes):
    swapped = jnp.where(lanes, pltpu.roll(x, 96, 1), pltpu.roll(x, 32, 1))
    return x * cos + swapped * sin


def project(normed, weight, cos, sin):
    rows = normed.shape[0]
    tile = 256

    def kernel(n_ref, w_ref, c_ref, s_ref, q_ref, kv_ref):
        full = jnp.dot(n_ref[...], w_ref[...], preferred_element_type=F32)
        cos_t, sin_t = c_ref[...], s_ref[...]
        low = lax.rem(lax.broadcasted_iota(jnp.int32, (tile, 128), 1), 64) < 32
        for b in range(3):
            block = turn(full[:, 128 * b : 128 * b + 128], cos_t, sin_t, low)
            q_ref[:, 128 * b : 128 * b + 128] = (block.astype(BF).astype(F32) * 0.125).astype(BF)
        kv_ref[:, :128] = turn(full[:, 384:512], cos_t, sin_t, low).astype(BF)
        kv_ref[:, 128:] = full[:, 512:].astype(BF)

    return pl.pallas_call(
        kernel,
        name="project",
        grid=(rows // tile,),
        in_specs=[
            pl.BlockSpec((tile, D), lambda i: (i, 0)),
            pl.BlockSpec((D, 640), lambda i: (0, 0)),
            pl.BlockSpec((tile, 128), lambda i: (i, 0)),
            pl.BlockSpec((tile, 128), lambda i: (i, 0)),
        ],
        out_specs=[
            pl.BlockSpec((tile, 384), lambda i: (i, 0)),
            pl.BlockSpec((tile, 256), lambda i: (i, 0)),
        ],
        out_shape=[
            jax.ShapeDtypeStruct((rows, 384), BF),
            jax.ShapeDtypeStruct((rows, 256), BF),
        ],
        compiler_params=pltpu.CompilerParams(vmem_limit_bytes=VMEM_LIMIT),
    )(normed, weight, cos, sin)


def unproject(q_grad, kv_grad, weight, cos, sin):
    rows = q_grad.shape[0]
    tile = 256

    def kernel(q_ref, kv_ref, w_ref, c_ref, s_ref, pg_ref, dn_ref):
        cos_t, sin_t = c_ref[...], -s_ref[...]
        low = lax.rem(lax.broadcasted_iota(jnp.int32, (tile, 128), 1), 64) < 32
        total = kv_ref[0].astype(F32)
        for c in range(1, kv_ref.shape[0]):
            total += kv_ref[c].astype(F32)
        for b in range(3):
            block = q_ref[:, 128 * b : 128 * b + 128].astype(BF).astype(F32)
            pg_ref[:, 128 * b : 128 * b + 128] = turn(block, cos_t, sin_t, low).astype(BF)
        block = total[:, :128].astype(BF).astype(F32)
        pg_ref[:, 384:512] = turn(block, cos_t, sin_t, low).astype(BF)
        pg_ref[:, 512:] = total[:, 128:].astype(BF)
        dn_ref[...] = dot_general(pg_ref[...], w_ref[...], 1, 1).astype(BF)

    return pl.pallas_call(
        kernel,
        name="unproject",
        grid=(rows // tile,),
        in_specs=[
            pl.BlockSpec((tile, 384), lambda i: (i, 0)),
            pl.BlockSpec((kv_grad.shape[0], tile, 256), lambda i: (0, i, 0)),
            pl.BlockSpec((D, 640), lambda i: (0, 0)),
            pl.BlockSpec((tile, 128), lambda i: (i, 0)),
            pl.BlockSpec((tile, 128), lambda i: (i, 0)),
        ],
        out_specs=[
            pl.BlockSpec((tile, 640), lambda i: (i, 0)),
            pl.BlockSpec((tile, D), lambda i: (i, 0)),
        ],
        out_shape=[
            jax.ShapeDtypeStruct((rows, 640), BF),
            jax.ShapeDtypeStruct((rows, D), BF),
        ],
        compiler_params=pltpu.CompilerParams(vmem_limit_bytes=VMEM_LIMIT),
    )(q_grad, kv_grad, weight, cos, sin)


TQ = 256
TK = 512


def head_block(block, head):
    low = lax.broadcasted_iota(jnp.int32, block.shape, 1) < 64
    return jnp.where(low if head == 0 else jnp.logical_not(low), block, jnp.zeros_like(block))


def visible(kp_ref, ks_ref, qp_ref, qs_ref, start):
    key_pos = kp_ref[pl.ds(start, TK), :]
    key_seg = ks_ref[pl.ds(start, TK), :]
    return (key_pos <= qp_ref[...]) & ((key_seg == 0) | (key_seg == qs_ref[...]))


HEAD_SLOTS = [(0, 0), (0, 1), (1, 0), (1, 1), (2, 0)]


def attend_forward(q, kv, q_pos, q_seg, k_pos, k_seg):
    rows, keys = q.shape[0], kv.shape[0]

    def kernel(q_ref, kv_ref, qp_ref, qs_ref, kp_ref, ks_ref, a_ref, o_ref, lse_ref, acc, top, tot):
        acc[...] = jnp.zeros_like(acc)
        top[...] = jnp.full_like(top, -1e30)
        tot[...] = jnp.zeros_like(tot)
        heads = [head_block(q_ref[:, 128 * b : 128 * b + 128], h) for b, h in HEAD_SLOTS]

        @pl.loop(0, keys // TK)
        def _(t):
            start = pl.multiple_of(t * TK, TK)
            k_tile = kv_ref[pl.ds(start, TK), :128]
            v_tile = kv_ref[pl.ds(start, TK), 128:]
            seen = visible(kp_ref, ks_ref, qp_ref, qs_ref, start)
            for j in range(5):
                scores = dot_general(k_tile, heads[j], 1, 1)
                scores = jnp.where(seen, scores, -1e30)
                old = top[j : j + 1, :]
                new = jnp.maximum(old, jnp.max(scores, axis=0, keepdims=True))
                expons = jnp.exp(scores - new)
                shrink = jnp.exp(old - new)
                tot[j : j + 1, :] = tot[j : j + 1, :] * shrink + jnp.sum(
                    expons, axis=0, keepdims=True
                )
                acc[j] = acc[j] * shrink + dot_general(v_tile, expons.astype(BF), 0, 0)
                top[j : j + 1, :] = new

        for j, (b, h) in enumerate(HEAD_SLOTS):
            out = acc[j] / tot[j : j + 1, :]
            acc[j] = out
        lse_ref[...] = top[...] + jnp.log(jnp.maximum(tot[...], 1e-37))
        low = lax.broadcasted_iota(jnp.int32, (TQ, 128), 1) < 64
        for b in range(3):
            first = acc[2 * b].T
            if b < 2:
                block = jnp.where(low, first, acc[2 * b + 1].T)
            else:
                block = jnp.where(low, first, 0.0)
            o_ref[:, 128 * b : 128 * b + 128] = block
            a_ref[:, 128 * b : 128 * b + 128] = block.astype(BF)

    return pl.pallas_call(
        kernel,
        name="attend_forward",
        grid=(rows // TQ,),
        in_specs=[
            pl.BlockSpec((TQ, 384), lambda i: (i, 0)),
            pl.BlockSpec((keys, 256), lambda i: (0, 0)),
            pl.BlockSpec((1, TQ), lambda i: (0, i)),
            pl.BlockSpec((1, TQ), lambda i: (0, i)),
            pl.BlockSpec((keys, 1), lambda i: (0, 0)),
            pl.BlockSpec((keys, 1), lambda i: (0, 0)),
        ],
        out_specs=[
            pl.BlockSpec((TQ, 384), lambda i: (i, 0)),
            pl.BlockSpec((TQ, 384), lambda i: (i, 0)),
            pl.BlockSpec((8, TQ), lambda i: (0, i)),
        ],
        out_shape=[
            jax.ShapeDtypeStruct((rows, 384), BF),
            jax.ShapeDtypeStruct((rows, 384), F32),
            jax.ShapeDtypeStruct((8, rows), F32),
        ],
        scratch_shapes=[
            pltpu.VMEM((5, 128, TQ), F32),
            pltpu.VMEM((8, TQ), F32),
            pltpu.VMEM((8, TQ), F32),
        ],
        compiler_params=pltpu.CompilerParams(vmem_limit_bytes=VMEM_LIMIT),
    )(q, kv, q_pos, q_seg, k_pos, k_seg)


def attend_backward(q, kv, q_pos, q_seg, k_pos, k_seg, lse, out, out_grad):
    rows, keys = q.shape[0], kv.shape[0]
    steps = rows // TQ

    def kernel(
        q_ref, kv_ref, qp_ref, qs_ref, kp_ref, ks_ref, lse_ref, o_ref, do_ref, dq_ref, dkv_ref,
        acc, kv_acc,
    ):
        @pl.when(pl.program_id(0) == 0)
        def _():
            kv_acc[...] = jnp.zeros_like(kv_acc)

        acc[...] = jnp.zeros_like(acc)
        heads = [head_block(q_ref[:, 128 * b : 128 * b + 128], h) for b, h in HEAD_SLOTS]
        grads = [head_block(do_ref[:, 128 * b : 128 * b + 128], h) for b, h in HEAD_SLOTS]
        delta = []
        for j, (b, h) in enumerate(HEAD_SLOTS):
            product = grads[j].astype(F32) * o_ref[:, 128 * b : 128 * b + 128]
            delta.append(jnp.sum(product.T, axis=0, keepdims=True))

        @pl.loop(0, keys // TK)
        def _(t):
            start = pl.multiple_of(t * TK, TK)
            k_tile = kv_ref[pl.ds(start, TK), :128]
            v_tile = kv_ref[pl.ds(start, TK), 128:]
            seen = visible(kp_ref, ks_ref, qp_ref, qs_ref, start)
            k_sum = jnp.zeros((TK, 128), F32)
            v_sum = jnp.zeros((TK, 128), F32)
            for j in range(5):
                scores = dot_general(k_tile, heads[j], 1, 1)
                probs = jnp.where(seen, jnp.exp(scores - lse_ref[j : j + 1, :]), 0.0)
                prob_grad = dot_general(v_tile, grads[j], 1, 1)
                score_grad = (probs * (prob_grad - delta[j])).astype(BF)
                v_sum += jnp.dot(probs.astype(BF), grads[j], preferred_element_type=F32)
                k_sum += jnp.dot(score_grad, heads[j], preferred_element_type=F32)
                acc[j] += dot_general(k_tile, score_grad, 0, 0)
            kv_acc[pl.ds(start, TK), :128] += k_sum
            kv_acc[pl.ds(start, TK), 128:] += v_sum

        low = lax.broadcasted_iota(jnp.int32, (TQ, 128), 1) < 64
        for b in range(3):
            first = acc[2 * b].T * 0.125
            if b < 2:
                block = jnp.where(low, first, acc[2 * b + 1].T * 0.125)
            else:
                block = jnp.where(low, first, 0.0)
            dq_ref[:, 128 * b : 128 * b + 128] = block.astype(BF)

        @pl.when(pl.program_id(0) == steps - 1)
        def _():
            dkv_ref[...] = kv_acc[...].astype(BF)

    return pl.pallas_call(
        kernel,
        name="attend_backward",
        grid=(steps,),
        in_specs=[
            pl.BlockSpec((TQ, 384), lambda i: (i, 0)),
            pl.BlockSpec((keys, 256), lambda i: (0, 0)),
            pl.BlockSpec((1, TQ), lambda i: (0, i)),
            pl.BlockSpec((1, TQ), lambda i: (0, i)),
            pl.BlockSpec((keys, 1), lambda i: (0, 0)),
            pl.BlockSpec((keys, 1), lambda i: (0, 0)),
            pl.BlockSpec((8, TQ), lambda i: (0, i)),
            pl.BlockSpec((TQ, 384), lambda i: (i, 0)),
            pl.BlockSpec((TQ, 384), lambda i: (i, 0)),
        ],
        out_specs=[
            pl.BlockSpec((TQ, 384), lambda i: (i, 0)),
            pl.BlockSpec((keys, 256), lambda i: (0, 0)),
        ],
        out_shape=[
            jax.ShapeDtypeStruct((rows, 384), BF),
            jax.ShapeDtypeStruct((keys, 256), BF),
        ],
        scratch_shapes=[pltpu.VMEM((5, 128, TQ), F32), pltpu.VMEM((keys, 256), F32)],
        compiler_params=pltpu.CompilerParams(vmem_limit_bytes=VMEM_LIMIT),
    )(q, kv, q_pos, q_seg, k_pos, k_seg, lse, out, out_grad)


def rms_factor(values):
    return lax.rsqrt(jnp.mean(values * values, axis=-1, keepdims=True) + EPSILON)


def norm_back(grad_normed, inputs, factor, gain):
    weighted = grad_normed * gain
    inner_mean = jnp.mean(weighted * inputs, axis=-1, keepdims=True)
    input_part = factor * weighted - inputs * (factor * factor * factor) * inner_mean
    return (input_part, jnp.sum(grad_normed * inputs * factor, axis=0))


def rope_tables(positions):
    frequency = jnp.exp(jnp.arange(32, dtype=F32) * (-math.log(10000.0) / 32))
    angles = positions.astype(F32)[:, None] * jnp.tile(frequency, 4)[None, :]
    sign = jnp.where(jnp.arange(128) % 64 < 32, -1.0, 1.0).astype(F32)
    return jnp.cos(angles), jnp.sin(angles) * sign[None, :]


def build(sizes):
    ctx, wsh = sizes["ctx"], sizes["wsh"]
    shards = ctx * wsh
    link = Exchange(sizes)

    def local(
        tokens,
        segment_ids,
        positions,
        attend_gain,
        query_key_value,
        attend_out,
        feed_gain,
        gate_up,
        down_weight,
        upstream,
    ):
        own = tokens.shape[0]
        plane = own * wsh
        group = plane * ctx
        core = lax.axis_index("grp")
        odd = lax.rem(lax.axis_index("wsh"), 2) == 1
        inputs = tokens.astype(F32)
        factor_one = rms_factor(inputs)
        normed_one = (inputs * factor_one * attend_gain).astype(BF)
        marks = jnp.pad(segment_ids * 65536 + positions, (0, 1024 - own)).reshape(8, 128)

        normed_all, w_qkv, marks_plane = link.run(
            "gather_one",
            1,
            [
                link.gather(normed_one, ("wsh",)),
                link.swap(qkv_columns(query_key_value), ("wsh",)),
                link.gather(marks, ("wsh",)),
            ],
        )
        normed_all = normed_all.reshape(plane, D)
        w_qkv = w_qkv.reshape(D, 640)
        plane_marks = marks_plane.reshape(wsh, 1024)[:, :own].reshape(plane)
        q_pos, q_seg = plane_marks % 65536, plane_marks // 65536
        cos, sin = rope_tables(q_pos)
        queries, kv_own = project(normed_all, w_qkv, cos, sin)

        kv_all, marks_all, dy_all, w_gate, w_up = link.run(
            "gather_keys",
            2,
            [
                link.gather(kv_own, ("ctx",)),
                link.gather(marks_plane, ("ctx",)),
                link.gather(upstream, ("wsh",)),
                link.columns(gate_up, ("wsh",), 0, FF // wsh),
                link.columns(gate_up, ("wsh",), FF, FF // wsh),
            ],
        )
        kv_all = kv_all.reshape(group, 256)
        dy_all = dy_all.reshape(plane, D)
        w_gate, w_up = w_gate.reshape(D, FF // wsh), w_up.reshape(D, FF // wsh)
        marks_all = marks_all.reshape(shards, 1024)[:, :own].reshape(group, 1)
        k_pos, k_seg = marks_all % 65536, marks_all // 65536
        q_pos, q_seg = q_pos.reshape(1, plane), q_seg.reshape(1, plane)
        attended, attended_wide, lse = attend_forward(queries, kv_all, q_pos, q_seg, k_pos, k_seg)

        w_out = spread_rows(attend_out, odd)
        out_part = jnp.dot(attended, w_out, preferred_element_type=F32).astype(BF)
        (out_parts,) = link.run(
            "scatter_out", 3, [link.swap(out_part.reshape(wsh, own, D), ("wsh",))]
        )
        middle = inputs + jnp.sum(out_parts.astype(F32), axis=0)
        factor_two = rms_factor(middle)
        normed_two = (middle * factor_two * feed_gain).astype(BF)
        (normed_two_all,) = link.run("gather_two", 4, [link.gather(normed_two, ("wsh",))])
        normed_two_all = normed_two_all.reshape(plane, D)

        gate_part = jnp.dot(normed_two_all, w_gate, preferred_element_type=F32)
        up_part = jnp.dot(normed_two_all, w_up, preferred_element_type=F32)
        hidden_grad = dot_general(dy_all, down_weight, 1, 1)
        sigmoid_gate = jax.nn.sigmoid(gate_part)
        silu_gate = gate_part * sigmoid_gate
        hidden = (silu_gate * up_part).astype(BF)
        gate_grad = (
            hidden_grad * up_part * sigmoid_gate * (1.0 + gate_part * (1.0 - sigmoid_gate))
        ).astype(BF)
        up_grad = (hidden_grad * silu_gate).astype(BF)
        down_part = jnp.dot(hidden, down_weight, preferred_element_type=F32).astype(BF)
        two_part = (dot_general(gate_grad, w_gate, 1, 1) + dot_general(up_grad, w_up, 1, 1)).astype(
            BF
        )
        two_parts, down_parts = link.run(
            "scatter_feed",
            5,
            [
                link.swap(two_part.reshape(wsh, own, D), ("wsh",)),
                link.swap(down_part.reshape(wsh, own, D), ("wsh",)),
            ],
        )
        activations = (middle + jnp.sum(down_parts.astype(F32), axis=0)).astype(BF)
        normed_two_grad = jnp.sum(two_parts.astype(F32), axis=0)
        middle_part, feed_gain_grad = norm_back(normed_two_grad, middle, factor_two, feed_gain)
        middle_grad = upstream.astype(F32) + middle_part
        branch_grad = middle_grad.astype(BF)

        down_grad = dot_general(hidden, dy_all, 0, 0).astype(BF)
        gate_w_grad = dot_general(normed_two_all, gate_grad, 0, 0).astype(BF)
        up_w_grad = dot_general(normed_two_all, up_grad, 0, 0).astype(BF)
        ffn_rows = FF // shards // 2
        down_halves = down_grad.reshape(ctx, 2, ffn_rows, D).transpose(1, 0, 2, 3)
        gate_halves = jnp.stack([gate_w_grad, up_w_grad]).reshape(2, shards, D // shards, FF // wsh)

        branch_all, down_pair, gate_pair = link.run(
            "gather_branch",
            6,
            [
                link.gather(branch_grad, ("wsh",)),
                link.swap(down_halves, ("grp",)),
                link.swap(gate_halves, ("grp",)),
            ],
        )
        branch_all = branch_all.reshape(plane, D)
        down_send = (down_pair[0].astype(F32) + down_pair[1].astype(F32)).astype(BF)
        gate_send = (gate_pair[0].astype(F32) + gate_pair[1].astype(F32)).astype(BF)
        attended_grad = dot_general(branch_all, w_out, 1, 1).astype(BF)
        q_grad, kv_grad = attend_backward(
            queries, kv_all, q_pos, q_seg, k_pos, k_seg, lse, attended_wide, attended_grad
        )
        kv_parts, down_got, gate_got = link.run(
            "scatter_keys",
            7,
            [
                link.swap(kv_grad.reshape(ctx, plane, 256), ("ctx",)),
                link.owners(down_send),
                link.swap(gate_send, ("ctx", "wsh")),
            ],
        )
        projected_grad, one_part = unproject(q_grad, kv_parts, w_qkv, cos, sin)
        qkv_grad = dot_general(normed_all, projected_grad, 0, 0).astype(BF)
        out_grad = collect_rows(dot_general(attended, branch_all, 0, 0), odd).astype(BF)
        qkv_halves = qkv_grad.reshape(shards, D // shards, 2, 320).transpose(2, 0, 1, 3)
        out_halves = out_grad.reshape(ctx, D // shards, 2, 576).transpose(2, 0, 1, 3)
        one_parts, qkv_pair, out_pair = link.run(
            "scatter_one",
            8,
            [
                link.swap(one_part.reshape(wsh, own, D), ("wsh",)),
                link.swap(qkv_halves, ("grp",)),
                link.swap(out_halves, ("grp",)),
            ],
        )
        normed_one_grad = jnp.sum(one_parts.astype(F32), axis=0)
        input_part, attend_gain_grad = norm_back(normed_one_grad, inputs, factor_one, attend_gain)
        input_grad = middle_grad + input_part
        qkv_send = (qkv_pair[0].astype(F32) + qkv_pair[1].astype(F32)).astype(BF)
        out_send = (out_pair[0].astype(F32) + out_pair[1].astype(F32)).astype(BF)
        gains = jnp.stack([attend_gain_grad, feed_gain_grad]).reshape(2, shards, D // shards)
        gains = jnp.pad(gains.transpose(1, 0, 2), ((0, 0), (0, 6), (0, 128 - D // shards)))
        qkv_got, out_got, gains_got = link.run(
            "scatter_weights",
            9,
            [
                link.swap(qkv_send, ("ctx", "wsh")),
                link.owners(out_send),
                link.swap(gains, ("ctx", "wsh")),
            ],
        )

        def over_ctx(x):
            return jnp.sum(x.reshape((ctx, wsh) + x.shape[1:]).astype(F32), axis=0)

        down_half = jnp.sum(down_got.astype(F32), axis=0).astype(BF)
        out_half = jnp.sum(out_got.astype(F32), axis=0).astype(BF)
        gate_half = over_ctx(gate_got).astype(BF)
        qkv_half = over_ctx(qkv_got).astype(BF)
        gain_half = jnp.sum(gains_got, axis=0)
        down_two, out_two, gate_two, qkv_two, gain_two = link.run(
            "swap_cores",
            10,
            [
                link.gather(down_half, ("grp",)),
                link.gather(out_half, ("grp",)),
                link.gather(gate_half, ("grp",)),
                link.gather(qkv_half, ("grp",)),
                link.gather(gain_half, ("grp",)),
            ],
        )
        rows = D // shards
        down_out = down_two.reshape(FF // shards, D).astype(F32)
        out_out = out_two.transpose(1, 0, 2).reshape(rows, D).astype(F32)
        gate_out = gate_two.transpose(2, 0, 1, 3).reshape(rows, 2 * FF).astype(F32)
        qkv_out = qkv_restore(
            qkv_two.transpose(1, 2, 0, 3).reshape(wsh, rows, 640).astype(F32)
        )
        gain_out = gain_two[0] + gain_two[1]
        return (
            activations,
            input_grad,
            qkv_out,
            out_out,
            gate_out,
            down_out,
            gain_out[0, :rows],
            gain_out[1, :rows],
        )

    return local


def solution(mesh):
    whole = ("grp", "ctx", "wsh")
    in_specs = (
        P(whole, None),
        P(whole),
        P(whole),
        P(),
        P("wsh", None),
        P("wsh", None),
        P(),
        P("wsh", None),
        P("wsh", None),
        P(whole, None),
    )
    out_specs = (
        P(whole, None),
        P(whole, None),
        P(("ctx", "wsh"), None),
        P(("ctx", "wsh"), None),
        P(("ctx", "wsh"), None),
        P(("ctx", "wsh"), None),
        P(("ctx", "wsh")),
        P(("ctx", "wsh")),
    )
    return jax.shard_map(
        build(dict(mesh.shape)), mesh=mesh, in_specs=in_specs, out_specs=out_specs, check_vma=False
    )
```

time: 1920 us -> 602 us (0.31)
  waiting for transfers between devices: 1410 us -> 0 us
  Pallas kernels: 0 us -> 490 us
  blocking collectives: 154 us -> 0 us
  matrix products: 173 us -> 32.3 us
  local copies, waits for them, and re-layouts: 82.4 us -> 31.9 us
  other arithmetic: 59.4 us -> 38.4 us
    reduce_scatter x2 -> x0, waiting for transfers between devices: 627 us -> none  [the longest x1 403 us: local(): lax.psum_scatter(gate_up_grad, ('ctx', 'wsh'), scatter_dimension=0, tiled...]
    unnamed x17 -> x0, waiting for transfers between devices: 540 us -> none
    pallas_call x0 -> x14, Pallas kernels: none -> 490 us  [the longest x10 393 us: run(): pl.pallas_call(kernel, name=name, out_shape=[jax.ShapeDtypeStruct(op[4],...]
    all_gather x6 -> x0, waiting for transfers between devices: 246 us -> none  [the longest x1 90.9 us: local(): lax.all_gather(gate_up, 'wsh', axis=0, tiled=True)]
    unnamed x2 -> x0, blocking collectives: 151 us -> none
    dot_general x33 -> x13, matrix products: 173 us -> 32.3 us  [the longest x9 19.9 us: dot_general(): lax.dot_general(a, b, (((ca,), (cb,)), ((), ())), preferred_element_type=...]
    unnamed x73 -> x98, local copies, waits for them, and re-layouts: 62.7 us -> 5.58 us
  transfers between devices with their start and end apart: 13 -> 0, of which waited for: 10 -> 0; matrix products, arithmetic and copies ran while one was open for 9% -> 0% of each run, Pallas kernels for 0% -> 0%
where the time goes in v1:
time: 602 us; the launch traced here: 595 us
  Pallas kernels  490 us (81%)
  other arithmetic  38.4 us (6%)
  matrix products  32.3 us (5%)
  local copies, waits for them, and re-layouts  31.9 us (5%)
    pallas_call x10, Pallas kernels, run(): pl.pallas_call(kernel, name=name, out_shape=[jax.ShapeDtypeStruct(op[4],...  393 us
    pallas_call x1, Pallas kernels, attend_forward(): pl.pallas_call(kernel, name='attend_forward', grid=(rows // TQ,), in_spec...  44.7 us
    pallas_call x1, Pallas kernels, attend_backward(): pl.pallas_call(kernel, name='attend_backward', grid=(steps,), in_specs=[p...  41.3 us
    dot_general x9, matrix products, dot_general(): lax.dot_general(a, b, (((ca,), (cb,)), ((), ())), preferred_element_type=...  19.9 us

profile of v1, /device:TPU:0, one launch (start us, length us, event | category | flops | bytes accessed | tf_op | source)
XLA Modules:
  0.0 594.9 jit_solution(7906923155286961926)
XLA Ops:
  0.7 1.3 fusion.7
  2.0 2.0 fusion.9.refs_0_
  6.0 1.2 concatenate.34
  8.1 1.3 concatenate.33
  10.6 1.3 concatenate.31
  11.9 1.3 pad_maximum_fusion.1.refs_1_
  13.8 40.5 %gather_one.1 = (bf16[4,192,1152]{2,1,0:T(8,128)(2,1)}, bf16[4,288,640]{2,1,0:T(8,128)(2,1)}, s32[4,8,128]{2,1,0:T(8,128)}) custom-call(bf16[192,1152]{1,0:T(8,128)(2,1)} %fusion.9.refs_0_, bf16[4,288,640]{2,1,0:T(8,128)(2,1)} %pad_maximum_fusion.1.refs_1_, s32[8,128]{1,0:T(8,128)} %pad_bitcast_fusion.refs_2_), custom_call_target="tpu_custom_call" | custom-call | tf_op jit(solution)/shard_map/gather_one/pallas_call | solution.py:180
  55.2 2.5 fusion.16
  57.7 5.3 project.1
  63.0 63.1 %gather_keys.1 = (bf16[4,768,256]{2,1,0:T(8,128)(2,1)}, s32[4,4,8,128]{3,2,1,0:T(8,128)}, bf16[4,192,1152]{2,1,0:T(8,128)(2,1)}, bf16[4,288,768]{2,1,0:T(8,128)(2,1)}, bf16[4,288,768]{2,1,0:T(8,128)(2,1)}) custom-call(bf16[768,256]{1,0:T(8,128)(2,1)} %get-tuple-element.48.refs_0_, s32[4,8,128]{2,1,0:T(8,128)} %get-tuple-element.46.refs_1_, ...), custom_call_target="tpu_custom_call" | custom-call | tf_op jit(solution)/shard_map/gather_keys/pallas_call | solution.py:180
  128.2 1.4 reshape.483
  129.7 2.9 add_select_fusion
  132.6 44.7 %attend_forward.1 = (bf16[768,384]{1,0:T(8,128)(2,1)}, f32[768,384]{1,0:T(8,128)}, f32[8,768]{1,0:T(8,128)}) custom-call(bf16[768,384]{1,0:T(8,128)(2,1)} %get-tuple-element.47.q_ref, bf16[3072,256]{1,0:T(8,128)(2,1)} %bitcast.93, s32[1,768]{1,0:T(1,128)} %and_select_fusion.1.qp_ref, s32[1,768]{1,0:T(1,128)} %get-tuple-element.88.qs_ref, ...), custom_call_target="tpu_custom_call" | custom-call | tf_op jit(solution)/shard_map/attend_forward/pallas_call | solution.py:409
  177.6 3.8 convolution_convert_fusion
  181.4 22.1 %scatter_out.1 = bf16[4,192,1152]{2,1,0:T(8,128)(2,1)} custom-call(bf16[4,192,1152]{2,1,0:T(8,128)(2,1)} %bitcast.104), custom_call_target="tpu_custom_call" | custom-call | tf_op jit(solution)/shard_map/scatter_out/pallas_call | solution.py:180
  203.5 1.9 convert_reduce_fusion.3
  207.0 21.9 %gather_two.1 = bf16[4,192,1152]{2,1,0:T(8,128)(2,1)} custom-call(bf16[192,1152]{1,0:T(8,128)(2,1)} %multiply_convert_fusion.3.refs_0_), custom_call_target="tpu_custom_call" | custom-call | tf_op jit(solution)/shard_map/gather_two/pallas_call | solution.py:180
  228.9 3.3 fusion.26
  232.2 1.7 fusion.25
  234.2 2.4 multiply_convert_fusion
  236.7 1.7 fusion.27
  238.4 3.0 fusion
  241.4 2.9 convolution_convert_fusion.4
  244.3 40.2 %scatter_feed.1 = (bf16[4,192,1152]{2,1,0:T(8,128)(2,1)}, bf16[4,192,1152]{2,1,0:T(8,128)(2,1)}) custom-call(bf16[4,192,1152]{2,1,0:T(8,128)(2,1)} %bitcast.101, bf16[4,192,1152]{2,1,0:T(8,128)(2,1)} %bitcast.102), custom_call_target="tpu_custom_call" | custom-call | tf_op jit(solution)/shard_map/scatter_feed/pallas_call | solution.py:180
  284.5 1.9 convert_reduce_fusion.1
  287.7 1.3 fusion.20
  289.9 2.0 convolution_convert_fusion.3
  291.9 1.3 copy.39
  293.6 1.6 convolution_convert_fusion.1
  295.2 1.6 convolution_convert_fusion.2
  296.8 2.1 pad_maximum_fusion.refs_2_
  298.9 21.6 %gather_branch.1 = (bf16[4,192,1152]{2,1,0:T(8,128)(2,1)}, bf16[2,4,96,1152]{3,2,1,0:T(8,128)(2,1)}, bf16[2,16,72,768]{3,2,1,0:T(8,128)(2,1)}) custom-call(bf16[192,1152]{1,0:T(8,128)(2,1)} %get-tuple-element.84.refs_0_, bf16[2,4,96,1152]{3,2,1,0:T(8,128)(2,1)} %bitcast.91, bf16[2,16,72,768]{3,2,1,0:T(8,128)(2,1)} %pad_maximum_fusion.refs_2_), custom_call_target="tpu_custom_call" | custom-call | tf_op jit(solution)/shard_map/gather_branch/pallas_call | solution.py:180
  320.6 3.4 convolution_convert_fusion.6.do_ref
  324.0 41.3 %attend_backward.1 = (bf16[768,384]{1,0:T(8,128)(2,1)}, bf16[3072,256]{1,0:T(8,128)(2,1)}) custom-call(bf16[768,384]{1,0:T(8,128)(2,1)} %get-tuple-element.47.q_ref, bf16[3072,256]{1,0:T(8,128)(2,1)} %bitcast.94, s32[1,768]{1,0:T(1,128)} %and_select_fusion.1.qp_ref, s32[1,768]{1,0:T(1,128)} %get-tuple-element.88.qs_ref, s32[3072,1]{1,0:T(8,128)} %get-tuple-element.94.kp_ref, ...), custom_call_target="tpu_custom_call" | custom-call | tf_op jit(solution)/shard_map/attend_backward/pallas_call | solution.py:492
  366.4 1.6 fusion.2.refs_2_
  368.1 108.6 %scatter_keys.1 = (bf16[4,768,256]{2,1,0:T(8,128)(2,1)}, bf16[4,96,1152]{2,1,0:T(8,128)(2,1)}, bf16[16,72,768]{2,1,0:T(8,128)(2,1)}) custom-call(bf16[4,768,256]{2,1,0:T(8,128)(2,1)} %bitcast.112, bf16[4,96,1152]{2,1,0:T(8,128)(2,1)} %fusion.5.refs_1_, bf16[16,72,768]{2,1,0:T(8,128)(2,1)} %fusion.2.refs_2_), custom_call_target="tpu_custom_call" | custom-call | tf_op jit(solution)/shard_map/scatter_keys/pallas_call | solution.py:180
  476.7 6.0 %unproject.1 = (bf16[768,640]{1,0:T(8,128)(2,1)}, bf16[768,1152]{1,0:T(8,128)(2,1)}) custom-call(bf16[768,384]{1,0:T(8,128)(2,1)} %get-tuple-element.60.q_ref, bf16[4,768,256]{2,1,0:T(8,128)(2,1)} %get-tuple-element.64.kv_ref, bf16[1152,640]{1,0:T(8,128)(2,1)} %bitcast.96, f32[768,128]{1,0:T(8,128)} %get-tuple-element.169.c_ref, ...), custom_call_target="tpu_custom_call" | custom-call | tf_op jit(solution)/shard_map/unproject/pallas_call | solution.py:326
  482.7 3.9 convolution_convert_fusion.5
  486.6 4.1 reshape.477
  490.7 1.4 copy.38
  495.9 28.1 %scatter_one.1 = (bf16[4,192,1152]{2,1,0:T(8,128)(2,1)}, bf16[2,16,72,320]{3,2,1,0:T(8,128)(2,1)}, bf16[2,4,72,576]{3,2,1,0:T(8,128)(2,1)}) custom-call(bf16[4,192,1152]{2,1,0:T(8,128)(2,1)} %bitcast.111, bf16[2,16,72,320]{3,2,1,0:T(8,128)(2,1)} %bitcast.92, bf16[2,4,72,576]{3,2,1,0:T(8,128)(2,1)} %bitcast.97), custom_call_target="tpu_custom_call" | custom-call | tf_op jit(solution)/shard_map/scatter_one/pallas_call | solution.py:180
  524.0 1.8 convert_reduce_fusion
  528.2 2.6 fusion.6.refs_0_
  532.4 44.0 %scatter_weights.1 = (bf16[16,72,320]{2,1,0:T(8,128)(2,1)}, bf16[4,72,576]{2,1,0:T(8,128)(2,1)}, f32[16,8,128]{2,1,0:T(8,128)}) custom-call(bf16[16,72,320]{2,1,0:T(8,128)(2,1)} %fusion.6.refs_0_, bf16[4,72,576]{2,1,0:T(8,128)(2,1)} %fusion.17.refs_1_, f32[16,8,128]{2,1,0:T(8,128)} %pad.9.refs_2_), custom_call_target="tpu_custom_call" | custom-call | tf_op jit(solution)/shard_map/scatter_weights/pallas_call | solution.py:180
  576.5 1.8 reduce_sum.158.refs_1_
  580.9 3.1 swap_cores.1
  589.8 2.1 reshape.481
  591.9 2.0 bitcast_convert_fusion
  (163 shorter events, 30.0 us)
Async XLA Ops:
  0.6 231.6 %copy-start = (bf16[768,1152]{1,0:T(8,128)(2,1)S(1)}, bf16[768,1152]{1,0:T(8,128)(2,1)}, u32[]{:S(2)}) copy-start(bf16[768,1152]{1,0:T(8,128)(2,1)} %param.18) | copy-start | bytes 5308420
  0.6 3.3 copy-start.3
  10.6 2.6 copy-start.25
  10.6 2.6 copy-start.26
  132.6 44.7 %copy-start.5 = (bf16[288,1152]{1,0:T(8,128)(2,1)S(1)}, bf16[288,1152]{1,0:T(8,128)(2,1)}, u32[]{:S(2)}) copy-start(bf16[288,1152]{1,0:T(8,128)(2,1)} %param.15) | copy-start | bytes 1990660
  177.5 3.9 copy-start.20
  177.5 3.9 copy-start.22
  203.5 1.9 copy-start.2
  205.4 0.7 copy-start.17
  206.1 22.8 %copy-start.30 = (bf16[4,288,768]{2,1,0:T(8,128)(2,1)S(1)}, bf16[4,288,768]{2,1,0:T(8,128)(2,1)}, u32[]{:S(2)}) copy-start(bf16[4,288,768]{2,1,0:T(8,128)(2,1)} %get-tuple-element.54) | copy-start | bytes 5308420
  228.9 3.3 copy-start.27
  232.2 1.7 copy-start.8
  232.2 2.0 copy-start.29
  234.2 2.5 copy-start.31
  236.7 1.8 copy-start.36
  236.7 1.8 copy-start.34
  236.7 4.8 copy-start.38
  284.5 2.3 copy-start.10
  286.7 1.0 copy-start.11
  287.7 1.8 copy-start.28
  287.7 2.1 copy-start.39
  291.9 1.7 copy-start.35
  293.6 1.6 copy-start.37
  298.9 21.6 %copy-start.21 = (bf16[384,1152]{1,0:T(8,128)(2,1)S(1)}, bf16[384,1152]{1,0:T(8,128)(2,1)}, u32[]{:S(2)}) copy-start(bf16[384,1152]{1,0:T(8,128)(2,1)} %copy-done.20) | copy-start | bytes 2654212
  298.9 21.6 %copy-start.23 = (bf16[384,1152]{1,0:T(8,128)(2,1)S(1)}, bf16[384,1152]{1,0:T(8,128)(2,1)}, u32[]{:S(2)}) copy-start(bf16[384,1152]{1,0:T(8,128)(2,1)} %copy-done.22) | copy-start | bytes 2654212
  324.0 41.3 %copy-start.9 = (bf16[2,4,96,1152]{3,2,1,0:T(8,128)(2,1)S(1)}, bf16[2,4,96,1152]{3,2,1,0:T(8,128)(2,1)}, u32[]{:S(2)}) copy-start(bf16[2,4,96,1152]{3,2,1,0:T(8,128)(2,1)} %get-tuple-element.62) | copy-start | bytes 5308420
  324.0 42.4 %copy-start.4 = (bf16[2,16,72,768]{3,2,1,0:T(8,128)(2,1)S(1)}, bf16[2,16,72,768]{3,2,1,0:T(8,128)(2,1)}, u32[]{:S(2)}) copy-start(bf16[2,16,72,768]{3,2,1,0:T(8,128)(2,1)} %get-tuple-element.63) | copy-start | bytes 10616836
  476.7 6.0 %copy-start.7 = (bf16[4,192,1152]{2,1,0:T(8,128)(2,1)S(1)}, bf16[4,192,1152]{2,1,0:T(8,128)(2,1)}, u32[]{:S(2)}) copy-start(bf16[4,192,1152]{2,1,0:T(8,128)(2,1)} %get-tuple-element.44) | copy-start | bytes 5308420
  490.7 2.1 copy-start.32
  490.7 2.2 copy-start.33
  524.0 1.8 copy-start.18
  526.1 1.2 copy-start.12
  527.3 3.4 copy-start.15
  530.7 47.5 %copy-start.6 = (bf16[16,72,768]{2,1,0:T(8,128)(2,1)S(1)}, bf16[16,72,768]{2,1,0:T(8,128)(2,1)}, u32[]{:S(2)}) copy-start(bf16[16,72,768]{2,1,0:T(8,128)(2,1)} %get-tuple-element.72) | copy-start | bytes 5308420
  576.5 2.9 copy-start.13
  578.3 2.0 copy-start.19
  586.3 1.4 copy-start.16
  586.7 2.3 copy-start.14
  589.1 5.3 copy-start.1
  589.8 4.1 copy-start.24

commit v2 on v1

--- a/solution.py
+++ b/solution.py
@@ -53,17 +53,19 @@
 
     def columns(self, x, axes, start, width):
         count = math.prod(self.sizes[axis] for axis in axes)
-        source = lambda ref, p: ref.at[:, pl.ds(pl.multiple_of(start + p * width, 128), width)]
+        source = lambda ref, p: ref.at[
+            :, pl.ds(pl.multiple_of(lax.axis_index("grp") * start + p * width, 128), width)
+        ]
         return ("peer", x, axes, source, (count, x.shape[0], width), (x.shape[0], width))
 
-    def owners(self, x):
-        return ("owner", x, None, None, x.shape, x.shape[1:])
+    def turn_over(self, x):
+        return ("owner", x, None, None, x.shape, x.shape)
 
     def run(self, name, number, ops):
         ctx, wsh = self.sizes["ctx"], self.sizes["wsh"]
         total = 0
         for kind, x, axes, *_ in ops:
-            total += ctx if kind == "owner" else math.prod(self.sizes[a] for a in axes)
+            total += 1 if kind == "owner" else math.prod(self.sizes[a] for a in axes)
         peers = {}
         for kind, x, axes, *_ in ops:
             for offset in self.offsets(axes if kind == "peer" else ("ctx", "wsh")):
@@ -113,55 +115,37 @@
                         slot += 1
                 else:
                     my_c, my_w = lax.axis_index("ctx"), lax.axis_index("wsh")
-                    base = slot
-                    for k in range(ctx):
-                        shard = my_w * ctx + k
-                        to_c, to_w = shard // wsh, lax.rem(shard, wsh)
-                        own = jnp.logical_and(to_c == my_c, to_w == my_w)
-                        copy = pltpu.make_async_remote_copy(
-                            ins[op].at[k],
-                            outs[op].at[my_c],
-                            send.at[base + k],
-                            recv.at[base + my_c],
-                            device_id={"ctx": to_c, "wsh": to_w},
-                            device_id_type=MESH,
-                        )
-                        inward = pltpu.make_async_copy(ins[op].at[k], bounce[op], near.at[op])
-                        outward = pltpu.make_async_copy(
-                            bounce[op], outs[op].at[my_c], near.at[op]
-                        )
-
-                        @pl.when(jnp.logical_not(own))
-                        def _():
-                            copy.start()
-
-                        late.append((own, copy, inward, outward))
-                    mine = my_c * wsh + my_w
-                    from_w = mine // ctx
-                    for c in range(ctx):
-                        own = jnp.logical_and(my_c == c, from_w == my_w)
-                        arrival = pltpu.make_async_remote_copy(
-                            ins[op].at[0],
-                            outs[op].at[c],
-                            send.at[base + c],
-                            recv.at[base + c],
-                            device_id={"ctx": my_c, "wsh": my_w},
-                            device_id_type=MESH,
-                        )
-                        late.append((own, arrival, None, None))
-                    slot += ctx
+                    shard = my_w * ctx + my_c
+                    to_c, to_w = shard // wsh, lax.rem(shard, wsh)
+                    own = jnp.logical_and(to_c == my_c, to_w == my_w)
+                    copy = pltpu.make_async_remote_copy(
+                        ins[op],
+                        outs[op],
+                        send.at[slot],
+                        recv.at[slot],
+                        device_id={"ctx": to_c, "wsh": to_w},
+                        device_id_type=MESH,
+                    )
+                    inward = pltpu.make_async_copy(ins[op], bounce[op], near.at[op])
+                    outward = pltpu.make_async_copy(bounce[op], outs[op], near.at[op])
+
+                    @pl.when(jnp.logical_not(own))
+                    def _():
+                        copy.start()
+
+                    late.append((own, copy, inward, outward))
+                    slot += 1
             for one, two in zip(first, second):
                 one.wait()
                 two.start()
             for own, copy, inward, outward in late:
-                if inward is not None:
-
-                    @pl.when(own)
-                    def _():
-                        inward.start()
-                        inward.wait()
-                        outward.start()
-                        outward.wait()
+
+                @pl.when(own)
+                def _():
+                    inward.start()
+                    inward.wait()
+                    outward.start()
+                    outward.wait()
 
             for copy in second:
                 copy.wait()
@@ -169,10 +153,7 @@
 
                 @pl.when(jnp.logical_not(own))
                 def _():
-                    if inward is None:
-                        copy.wait_recv()
-                    else:
-                        copy.wait_send()
+                    copy.wait()
 
             for copy in remote:
                 copy.wait()
@@ -437,16 +418,45 @@
     )(q, kv, q_pos, q_seg, k_pos, k_seg)
 
 
-def attend_backward(q, kv, q_pos, q_seg, k_pos, k_seg, lse, out, out_grad):
+def attend_backward(link, q, kv, q_pos, q_seg, k_pos, k_seg, lse, out, out_grad, send_rows):
     rows, keys = q.shape[0], kv.shape[0]
     steps = rows // TQ
+    axes = ("ctx", "wsh")
+    peers = link.offsets(axes)
 
     def kernel(
-        q_ref, kv_ref, qp_ref, qs_ref, kp_ref, ks_ref, lse_ref, o_ref, do_ref, dq_ref, dkv_ref,
-        acc, kv_acc,
+        q_ref, kv_ref, qp_ref, qs_ref, kp_ref, ks_ref, lse_ref, o_ref, do_ref, rows_ref,
+        dq_ref, dkv_ref, got_ref, acc, kv_acc, bounce, send, recv, near,
     ):
+        _, me = link.place(axes, peers[0])
+        copies = []
+        for at, offset in enumerate(peers[1:]):
+            where, index = link.place(axes, offset)
+            copies.append(
+                pltpu.make_async_remote_copy(
+                    rows_ref.at[index],
+                    got_ref.at[me],
+                    send.at[at],
+                    recv.at[at],
+                    device_id=where,
+                    device_id_type=MESH,
+                )
+            )
+        inward = pltpu.make_async_copy(rows_ref.at[me], bounce, near)
+        outward = pltpu.make_async_copy(bounce, got_ref.at[me], near)
+
         @pl.when(pl.program_id(0) == 0)
         def _():
+            barrier = pltpu.get_barrier_semaphore()
+            for offset in peers[1:]:
+                where, _ = link.place(axes, offset)
+                pl.semaphore_signal(barrier, 1, device_id=where, device_id_type=MESH)
+            pl.semaphore_wait(barrier, len(peers) - 1)
+            for copy in copies:
+                copy.start()
+            inward.start()
+            inward.wait()
+            outward.start()
             kv_acc[...] = jnp.zeros_like(kv_acc)
 
         acc[...] = jnp.zeros_like(acc)
@@ -488,6 +498,9 @@
         @pl.when(pl.program_id(0) == steps - 1)
         def _():
             dkv_ref[...] = kv_acc[...].astype(BF)
+            outward.wait()
+            for copy in copies:
+                copy.wait()
 
     return pl.pallas_call(
         kernel,
@@ -503,18 +516,30 @@
             pl.BlockSpec((8, TQ), lambda i: (0, i)),
             pl.BlockSpec((TQ, 384), lambda i: (i, 0)),
             pl.BlockSpec((TQ, 384), lambda i: (i, 0)),
+            pl.BlockSpec(memory_space=pl.ANY),
         ],
         out_specs=[
             pl.BlockSpec((TQ, 384), lambda i: (i, 0)),
             pl.BlockSpec((keys, 256), lambda i: (0, 0)),
+            pl.BlockSpec(memory_space=pl.ANY),
         ],
         out_shape=[
             jax.ShapeDtypeStruct((rows, 384), BF),
             jax.ShapeDtypeStruct((keys, 256), BF),
-        ],
-        scratch_shapes=[pltpu.VMEM((5, 128, TQ), F32), pltpu.VMEM((keys, 256), F32)],
-        compiler_params=pltpu.CompilerParams(vmem_limit_bytes=VMEM_LIMIT),
-    )(q, kv, q_pos, q_seg, k_pos, k_seg, lse, out, out_grad)
+            jax.ShapeDtypeStruct(send_rows.shape, BF),
+        ],
+        scratch_shapes=[
+            pltpu.VMEM((5, 128, TQ), F32),
+            pltpu.VMEM((keys, 256), F32),
+            pltpu.VMEM(send_rows.shape[1:], BF),
+            pltpu.SemaphoreType.DMA((len(peers),)),
+            pltpu.SemaphoreType.DMA((len(peers),)),
+            pltpu.SemaphoreType.DMA,
+        ],
+        compiler_params=pltpu.CompilerParams(
+            collective_id=11, has_side_effects=True, vmem_limit_bytes=VMEM_LIMIT
+        ),
+    )(q, kv, q_pos, q_seg, k_pos, k_seg, lse, out, out_grad, send_rows)
 
 
 def rms_factor(values):
@@ -578,20 +603,19 @@
         cos, sin = rope_tables(q_pos)
         queries, kv_own = project(normed_all, w_qkv, cos, sin)
 
-        kv_all, marks_all, dy_all, w_gate, w_up = link.run(
+        kv_all, marks_all, dy_all, w_half = link.run(
             "gather_keys",
             2,
             [
                 link.gather(kv_own, ("ctx",)),
                 link.gather(marks_plane, ("ctx",)),
                 link.gather(upstream, ("wsh",)),
-                link.columns(gate_up, ("wsh",), 0, FF // wsh),
                 link.columns(gate_up, ("wsh",), FF, FF // wsh),
             ],
         )
         kv_all = kv_all.reshape(group, 256)
         dy_all = dy_all.reshape(plane, D)
-        w_gate, w_up = w_gate.reshape(D, FF // wsh), w_up.reshape(D, FF // wsh)
+        w_half = w_half.reshape(D, FF // wsh)
         marks_all = marks_all.reshape(shards, 1024)[:, :own].reshape(group, 1)
         k_pos, k_seg = marks_all % 65536, marks_all // 65536
         q_pos, q_seg = q_pos.reshape(1, plane), q_seg.reshape(1, plane)
@@ -599,9 +623,15 @@
 
         w_out = spread_rows(attend_out, odd)
         out_part = jnp.dot(attended, w_out, preferred_element_type=F32).astype(BF)
-        (out_parts,) = link.run(
-            "scatter_out", 3, [link.swap(out_part.reshape(wsh, own, D), ("wsh",))]
-        )
+        out_parts, w_both = link.run(
+            "scatter_out",
+            3,
+            [
+                link.swap(out_part.reshape(wsh, own, D), ("wsh",)),
+                link.gather(w_half, ("grp",)),
+            ],
+        )
+        w_gate, w_up = w_both[0], w_both[1]
         middle = inputs + jnp.sum(out_parts.astype(F32), axis=0)
         factor_two = rms_factor(middle)
         normed_two = (middle * factor_two * feed_gain).astype(BF)
@@ -622,88 +652,89 @@
         two_part = (dot_general(gate_grad, w_gate, 1, 1) + dot_general(up_grad, w_up, 1, 1)).astype(
             BF
         )
-        two_parts, down_parts = link.run(
-            "scatter_feed",
-            5,
-            [
-                link.swap(two_part.reshape(wsh, own, D), ("wsh",)),
-                link.swap(down_part.reshape(wsh, own, D), ("wsh",)),
-            ],
-        )
-        activations = (middle + jnp.sum(down_parts.astype(F32), axis=0)).astype(BF)
-        normed_two_grad = jnp.sum(two_parts.astype(F32), axis=0)
-        middle_part, feed_gain_grad = norm_back(normed_two_grad, middle, factor_two, feed_gain)
-        middle_grad = upstream.astype(F32) + middle_part
-        branch_grad = middle_grad.astype(BF)
-
         down_grad = dot_general(hidden, dy_all, 0, 0).astype(BF)
         gate_w_grad = dot_general(normed_two_all, gate_grad, 0, 0).astype(BF)
         up_w_grad = dot_general(normed_two_all, up_grad, 0, 0).astype(BF)
         ffn_rows = FF // shards // 2
         down_halves = down_grad.reshape(ctx, 2, ffn_rows, D).transpose(1, 0, 2, 3)
         gate_halves = jnp.stack([gate_w_grad, up_w_grad]).reshape(2, shards, D // shards, FF // wsh)
-
-        branch_all, down_pair, gate_pair = link.run(
+        two_parts, down_pair, gate_pair = link.run(
+            "scatter_feed",
+            5,
+            [
+                link.swap(two_part.reshape(wsh, own, D), ("wsh",)),
+                link.swap(down_halves, ("grp",)),
+                link.swap(gate_halves, ("grp",)),
+            ],
+        )
+        normed_two_grad = jnp.sum(two_parts.astype(F32), axis=0)
+        middle_part, feed_gain_grad = norm_back(normed_two_grad, middle, factor_two, feed_gain)
+        middle_grad = upstream.astype(F32) + middle_part
+        branch_grad = middle_grad.astype(BF)
+        down_send = (down_pair[0].astype(F32) + down_pair[1].astype(F32)).astype(BF)
+        gate_send = (gate_pair[0].astype(F32) + gate_pair[1].astype(F32)).astype(BF)
+
+        branch_all, down_got = link.run(
             "gather_branch",
             6,
             [
                 link.gather(branch_grad, ("wsh",)),
-                link.swap(down_halves, ("grp",)),
-                link.swap(gate_halves, ("grp",)),
+                link.swap(down_send, ("ctx",)),
             ],
         )
         branch_all = branch_all.reshape(plane, D)
-        down_send = (down_pair[0].astype(F32) + down_pair[1].astype(F32)).astype(BF)
-        gate_send = (gate_pair[0].astype(F32) + gate_pair[1].astype(F32)).astype(BF)
         attended_grad = dot_general(branch_all, w_out, 1, 1).astype(BF)
-        q_grad, kv_grad = attend_backward(
-            queries, kv_all, q_pos, q_seg, k_pos, k_seg, lse, attended_wide, attended_grad
-        )
-        kv_parts, down_got, gate_got = link.run(
+        q_grad, kv_grad, gate_got = attend_backward(
+            link, queries, kv_all, q_pos, q_seg, k_pos, k_seg, lse, attended_wide, attended_grad,
+            gate_send,
+        )
+        out_grad = collect_rows(dot_general(attended, branch_all, 0, 0), odd).astype(BF)
+        out_halves = out_grad.reshape(ctx, D // shards, 2, 576).transpose(2, 0, 1, 3)
+        kv_parts, down_parts, out_pair = link.run(
             "scatter_keys",
             7,
             [
                 link.swap(kv_grad.reshape(ctx, plane, 256), ("ctx",)),
-                link.owners(down_send),
-                link.swap(gate_send, ("ctx", "wsh")),
-            ],
-        )
+                link.swap(down_part.reshape(wsh, own, D), ("wsh",)),
+                link.swap(out_halves, ("grp",)),
+            ],
+        )
+        activations = (middle + jnp.sum(down_parts.astype(F32), axis=0)).astype(BF)
+        out_send = (out_pair[0].astype(F32) + out_pair[1].astype(F32)).astype(BF)
         projected_grad, one_part = unproject(q_grad, kv_parts, w_qkv, cos, sin)
         qkv_grad = dot_general(normed_all, projected_grad, 0, 0).astype(BF)
-        out_grad = collect_rows(dot_general(attended, branch_all, 0, 0), odd).astype(BF)
         qkv_halves = qkv_grad.reshape(shards, D // shards, 2, 320).transpose(2, 0, 1, 3)
-        out_halves = out_grad.reshape(ctx, D // shards, 2, 576).transpose(2, 0, 1, 3)
-        one_parts, qkv_pair, out_pair = link.run(
+        down_half = jnp.sum(down_got.astype(F32), axis=0).astype(BF)
+        one_parts, qkv_pair, out_got, down_half = link.run(
             "scatter_one",
             8,
             [
                 link.swap(one_part.reshape(wsh, own, D), ("wsh",)),
                 link.swap(qkv_halves, ("grp",)),
-                link.swap(out_halves, ("grp",)),
+                link.swap(out_send, ("ctx",)),
+                link.turn_over(down_half),
             ],
         )
         normed_one_grad = jnp.sum(one_parts.astype(F32), axis=0)
         input_part, attend_gain_grad = norm_back(normed_one_grad, inputs, factor_one, attend_gain)
         input_grad = middle_grad + input_part
         qkv_send = (qkv_pair[0].astype(F32) + qkv_pair[1].astype(F32)).astype(BF)
-        out_send = (out_pair[0].astype(F32) + out_pair[1].astype(F32)).astype(BF)
         gains = jnp.stack([attend_gain_grad, feed_gain_grad]).reshape(2, shards, D // shards)
         gains = jnp.pad(gains.transpose(1, 0, 2), ((0, 0), (0, 6), (0, 128 - D // shards)))
-        qkv_got, out_got, gains_got = link.run(
+        out_half = jnp.sum(out_got.astype(F32), axis=0).astype(BF)
+        qkv_got, gains_got, out_half = link.run(
             "scatter_weights",
             9,
             [
                 link.swap(qkv_send, ("ctx", "wsh")),
-                link.owners(out_send),
                 link.swap(gains, ("ctx", "wsh")),
+                link.turn_over(out_half),
             ],
         )
 
         def over_ctx(x):
             return jnp.sum(x.reshape((ctx, wsh) + x.shape[1:]).astype(F32), axis=0)
 
-        down_half = jnp.sum(down_got.astype(F32), axis=0).astype(BF)
-        out_half = jnp.sum(out_got.astype(F32), axis=0).astype(BF)
         gate_half = over_ctx(gate_got).astype(BF)
         qkv_half = over_ctx(qkv_got).astype(BF)
         gain_half = jnp.sum(gains_got, axis=0)

time: 602 us -> 500 us (0.83)
  Pallas kernels: 490 us -> 374 us
  other arithmetic: 38.4 us -> 45.2 us
  local copies, waits for them, and re-layouts: 31.9 us -> 38.4 us
    pallas_call x10, Pallas kernels: 393 us -> 272 us  [run(): pl.pallas_call(kernel, name=name, out_shape=[jax.ShapeDtypeStruct(op[4],...]
where the time goes in v2:
time: 500 us; the launch traced here: 492 us
  Pallas kernels  374 us (75%)
  other arithmetic  45.2 us (9%)
  local copies, waits for them, and re-layouts  38.4 us (8%)
  matrix products  32.5 us (6%)
    pallas_call x10, Pallas kernels, run(): pl.pallas_call(kernel, name=name, out_shape=[jax.ShapeDtypeStruct(op[4],...  272 us
    pallas_call x1, Pallas kernels, attend_backward(): pl.pallas_call(kernel, name='attend_backward', grid=(steps,), in_specs=[p...  46.2 us
    pallas_call x1, Pallas kernels, attend_forward(): pl.pallas_call(kernel, name='attend_forward', grid=(rows // TQ,), in_spec...  44.7 us
    dot_general x9, matrix products, dot_general(): lax.dot_general(a, b, (((ca,), (cb,)), ((), ())), preferred_element_type=...  20.1 us

profile of v2, /device:TPU:0, one launch (start us, length us, event | category | flops | bytes accessed | tf_op | source)
XLA Modules:
  0.0 491.7 jit_solution(6825420132020789250)
XLA Ops:
  3.1 1.9 fusion.20.refs_0_
  14.9 40.5 %gather_one.1 = (bf16[4,192,1152]{2,1,0:T(8,128)(2,1)}, bf16[4,288,640]{2,1,0:T(8,128)(2,1)}, s32[4,8,128]{2,1,0:T(8,128)}) custom-call(bf16[192,1152]{1,0:T(8,128)(2,1)} %fusion.20.refs_0_, bf16[4,288,640]{2,1,0:T(8,128)(2,1)} %pad_maximum_fusion.1.refs_1_, s32[8,128]{1,0:T(8,128)} %pad_bitcast_fusion.refs_2_), custom_call_target="tpu_custom_call" | custom-call | tf_op jit(solution)/shard_map/gather_one/pallas_call | solution.py:161
  56.3 2.5 fusion.27
  58.8 5.3 %project.1 = (bf16[768,384]{1,0:T(8,128)(2,1)}, bf16[768,256]{1,0:T(8,128)(2,1)}) custom-call(bf16[768,1152]{1,0:T(8,128)(2,1)} %bitcast.112, bf16[1152,640]{1,0:T(8,128)(2,1)} %bitcast.102, f32[768,128]{1,0:T(8,128)} %get-tuple-element.174.c_ref, f32[768,128]{1,0:T(8,128)} %get-tuple-element.173.s_ref), custom_call_target="tpu_custom_call" | custom-call | tf_op jit(solution)/shard_map/project/pallas_call | solution.py:267
  64.1 44.1 %gather_keys.1 = (bf16[4,768,256]{2,1,0:T(8,128)(2,1)}, s32[4,4,8,128]{3,2,1,0:T(8,128)}, bf16[4,192,1152]{2,1,0:T(8,128)(2,1)}, bf16[4,288,768]{2,1,0:T(8,128)(2,1)}) custom-call(bf16[768,256]{1,0:T(8,128)(2,1)} %get-tuple-element.51.refs_0_, s32[4,8,128]{2,1,0:T(8,128)} %get-tuple-element.49.refs_1_, bf16[192,1152]{1,0:T(8,128)(2,1)} %refs_2_.1, ...), custom_call_target="tpu_custom_call" | custom-call | tf_op jit(solution)/shard_map/gather_keys/pallas_call | solution.py:161
  110.3 1.4 reshape.479
  111.7 3.0 add_select_fusion
  114.7 44.7 %attend_forward.1 = (bf16[768,384]{1,0:T(8,128)(2,1)}, f32[768,384]{1,0:T(8,128)}, f32[8,768]{1,0:T(8,128)}) custom-call(bf16[768,384]{1,0:T(8,128)(2,1)} %get-tuple-element.50.q_ref, bf16[3072,256]{1,0:T(8,128)(2,1)} %bitcast.100, s32[1,768]{1,0:T(1,128)} %and_select_fusion.1.qp_ref, s32[1,768]{1,0:T(1,128)} %get-tuple-element.94.qs_ref, ...), custom_call_target="tpu_custom_call" | custom-call | tf_op jit(solution)/shard_map/attend_forward/pallas_call | solution.py:390
  159.7 3.8 convolution_convert_fusion
  163.6 22.4 %scatter_out.1 = (bf16[4,192,1152]{2,1,0:T(8,128)(2,1)}, bf16[2,1152,768]{2,1,0:T(8,128)(2,1)}) custom-call(bf16[4,192,1152]{2,1,0:T(8,128)(2,1)} %bitcast.110, bf16[1152,768]{1,0:T(8,128)(2,1)} %bitcast.109), custom_call_target="tpu_custom_call" | custom-call | tf_op jit(solution)/shard_map/scatter_out/pallas_call | solution.py:161
  185.9 1.9 convert_reduce_fusion.3
  189.5 21.7 %gather_two.1 = bf16[4,192,1152]{2,1,0:T(8,128)(2,1)} custom-call(bf16[192,1152]{1,0:T(8,128)(2,1)} %multiply_convert_fusion.3.refs_0_), custom_call_target="tpu_custom_call" | custom-call | tf_op jit(solution)/shard_map/gather_two/pallas_call | solution.py:161
  211.2 3.3 fusion.5
  214.5 1.7 fusion.36
  216.3 2.4 multiply_convert_fusion
  218.6 1.7 fusion.3
  220.4 3.0 fusion
  223.4 1.7 convolution_convert_fusion.4
  225.1 1.4 copy.39
  226.5 1.8 convolution_convert_fusion.2
  228.3 1.6 convolution_convert_fusion.3
  229.9 2.1 pad_maximum_fusion.refs_2_
  232.0 22.1 %scatter_feed.1 = (bf16[4,192,1152]{2,1,0:T(8,128)(2,1)}, bf16[2,4,96,1152]{3,2,1,0:T(8,128)(2,1)}, bf16[2,16,72,768]{3,2,1,0:T(8,128)(2,1)}) custom-call(bf16[4,192,1152]{2,1,0:T(8,128)(2,1)} %bitcast.105, bf16[2,4,96,1152]{3,2,1,0:T(8,128)(2,1)} %bitcast.98, bf16[2,16,72,768]{3,2,1,0:T(8,128)(2,1)} %pad_maximum_fusion.refs_2_), custom_call_target="tpu_custom_call" | custom-call | tf_op jit(solution)/shard_map/scatter_feed/pallas_call | solution.py:161
  254.1 1.9 convert_reduce_fusion.2
  256.3 1.4 fusion.31
  259.4 22.6 %gather_branch.1 = (bf16[4,192,1152]{2,1,0:T(8,128)(2,1)}, bf16[4,96,1152]{2,1,0:T(8,128)(2,1)}) custom-call(bf16[192,1152]{1,0:T(8,128)(2,1)} %get-tuple-element.90.refs_0_, bf16[4,96,1152]{2,1,0:T(8,128)(2,1)} %fusion.16.refs_1_), custom_call_target="tpu_custom_call" | custom-call | tf_op jit(solution)/shard_map/gather_branch/pallas_call | solution.py:161
  282.1 3.6 convolution_convert_fusion.6.do_ref
  285.7 1.7 fusion.2.rows_ref
  287.4 46.2 %attend_backward.1 = (bf16[768,384]{1,0:T(8,128)(2,1)}, bf16[3072,256]{1,0:T(8,128)(2,1)}, bf16[16,72,768]{2,1,0:T(8,128)(2,1)}) custom-call(bf16[768,384]{1,0:T(8,128)(2,1)} %get-tuple-element.50.q_ref, bf16[3072,256]{1,0:T(8,128)(2,1)} %bitcast.101, s32[1,768]{1,0:T(1,128)} %and_select_fusion.1.qp_ref, s32[1,768]{1,0:T(1,128)} %get-tuple-element.94.qs_ref, ...), custom_call_target="tpu_custom_call" | custom-call | tf_op jit(solution)/shard_map/attend_backward/pallas_call | solution.py:505
  333.6 2.9 convolution_convert_fusion.1
  338.6 3.2 convert_element_type.197
  341.9 2.1 copy.40
  343.9 30.5 %scatter_keys.1 = (bf16[4,768,256]{2,1,0:T(8,128)(2,1)}, bf16[4,192,1152]{2,1,0:T(8,128)(2,1)}, bf16[2,4,72,576]{3,2,1,0:T(8,128)(2,1)}) custom-call(bf16[4,768,256]{2,1,0:T(8,128)(2,1)} %bitcast.120, bf16[4,192,1152]{2,1,0:T(8,128)(2,1)} %bitcast.114, bf16[2,4,72,576]{3,2,1,0:T(8,128)(2,1)} %bitcast.104), custom_call_target="tpu_custom_call" | custom-call | tf_op jit(solution)/shard_map/scatter_keys/pallas_call | solution.py:161
  374.5 1.8 convert_reduce_fusion.1
  377.2 5.7 %unproject.1 = (bf16[768,640]{1,0:T(8,128)(2,1)}, bf16[768,1152]{1,0:T(8,128)(2,1)}) custom-call(bf16[768,384]{1,0:T(8,128)(2,1)} %get-tuple-element.67.q_ref, bf16[4,768,256]{2,1,0:T(8,128)(2,1)} %get-tuple-element.68.kv_ref, bf16[1152,640]{1,0:T(8,128)(2,1)} %bitcast.103, f32[768,128]{1,0:T(8,128)} %get-tuple-element.174.c_ref, ...), custom_call_target="tpu_custom_call" | custom-call | tf_op jit(solution)/shard_map/unproject/pallas_call | solution.py:307
  382.9 3.9 convolution_convert_fusion.5
  386.8 5.0 %reshape.473 = bf16[16,72,2,320]{3,2,1,0:T(2,128)(2,1)} reshape(bf16[1152,640]{1,0:T(8,128)(2,1)} %convolution_convert_fusion.5) | data formatting | bytes 2949120 | tf_op jit(solution)/shard_map/reshape | solution.py:706
  391.9 3.0 copy.38
  396.6 37.1 %scatter_one.1 = (bf16[4,192,1152]{2,1,0:T(8,128)(2,1)}, bf16[2,16,72,320]{3,2,1,0:T(8,128)(2,1)}, bf16[4,72,576]{2,1,0:T(8,128)(2,1)}, bf16[96,1152]{1,0:T(8,128)(2,1)}) custom-call(bf16[4,192,1152]{2,1,0:T(8,128)(2,1)} %bitcast.115, bf16[2,16,72,320]{3,2,1,0:T(8,128)(2,1)} %bitcast.99, bf16[4,72,576]{2,1,0:T(8,128)(2,1)} %fusion.28.refs_2_, ...), custom_call_target="tpu_custom_call" | custom-call | tf_op jit(solution)/shard_map/scatter_one/pallas_call | solution.py:161
  433.8 1.9 convert_reduce_fusion
  441.1 1.7 reduce_sum.158.refs_2_
  442.8 27.7 %scatter_weights.1 = (bf16[16,72,320]{2,1,0:T(8,128)(2,1)}, f32[16,8,128]{2,1,0:T(8,128)}, bf16[72,576]{1,0:T(8,128)(2,1)}) custom-call(bf16[16,72,320]{2,1,0:T(8,128)(2,1)} %fusion.17.refs_0_, f32[16,8,128]{2,1,0:T(8,128)} %pad.9.refs_1_, bf16[72,576]{1,0:T(8,128)(2,1)} %reduce_sum.158.refs_2_), custom_call_target="tpu_custom_call" | custom-call | tf_op jit(solution)/shard_map/scatter_weights/pallas_call | solution.py:161
  471.7 2.1 reduce_sum.160.refs_3_
  473.7 1.4 reduce_sum.161.refs_4_
  475.2 3.1 swap_cores.1
  482.3 2.2 concatenate.39
  486.6 2.1 reshape.477
  488.7 2.0 bitcast_convert_fusion
  (152 shorter events, 36.9 us)
Async XLA Ops:
  0.6 213.9 %copy-start = (bf16[768,1152]{1,0:T(8,128)(2,1)S(1)}, bf16[768,1152]{1,0:T(8,128)(2,1)}, u32[]{:S(2)}) copy-start(bf16[768,1152]{1,0:T(8,128)(2,1)} %param.18) | copy-start | bytes 5308420
  0.6 4.4 copy-start.2
  2.6 0.5 copy-start.22
  11.7 2.6 copy-start.26
  11.7 2.6 copy-start.27
  114.7 44.7 %copy-start.5 = (bf16[288,1152]{1,0:T(8,128)(2,1)S(1)}, bf16[288,1152]{1,0:T(8,128)(2,1)}, u32[]{:S(2)}) copy-start(bf16[288,1152]{1,0:T(8,128)(2,1)} %param.15) | copy-start | bytes 1990660
  159.7 3.9 copy-start.18
  159.7 3.9 copy-start.20
  185.9 1.9 copy-start.1
  187.8 0.7 copy-start.16
  188.5 22.6 %copy-start.28 = (bf16[2,1152,768]{2,1,0:T(8,128)(2,1)S(1)}, bf16[2,1152,768]{2,1,0:T(8,128)(2,1)}, u32[]{:S(2)}) copy-start(bf16[2,1152,768]{2,1,0:T(8,128)(2,1)} %get-tuple-element.60) | copy-start | bytes 10616836
  211.2 3.3 copy-start.29
  214.5 1.7 copy-start.9
  218.6 4.8 copy-start.32
  254.1 2.2 copy-start.6
  256.3 2.0 copy-start.11
  258.3 23.8 %copy-start.19 = (bf16[384,1152]{1,0:T(8,128)(2,1)S(1)}, bf16[384,1152]{1,0:T(8,128)(2,1)}, u32[]{:S(2)}) copy-start(bf16[384,1152]{1,0:T(8,128)(2,1)} %copy-done.18) | copy-start | bytes 2654212
  258.3 23.8 %copy-start.21 = (bf16[384,1152]{1,0:T(8,128)(2,1)S(1)}, bf16[384,1152]{1,0:T(8,128)(2,1)}, u32[]{:S(2)}) copy-start(bf16[384,1152]{1,0:T(8,128)(2,1)} %copy-done.20) | copy-start | bytes 2654212
  282.1 3.6 copy-start.4
  287.4 46.2 %copy-start.33 = (bf16[768,768]{1,0:T(8,128)(2,1)S(1)}, bf16[768,768]{1,0:T(8,128)(2,1)}, u32[]{:S(2)}) copy-start(bf16[768,768]{1,0:T(8,128)(2,1)} %copy-done.32) | copy-start | bytes 3538948
  333.6 2.9 copy-start.30
  333.6 2.9 copy-start.31
  377.2 5.7 %copy-start.8 = (bf16[4,192,1152]{2,1,0:T(8,128)(2,1)S(1)}, bf16[4,192,1152]{2,1,0:T(8,128)(2,1)}, u32[]{:S(2)}) copy-start(bf16[4,192,1152]{2,1,0:T(8,128)(2,1)} %get-tuple-element.47) | copy-start | bytes 5308420
  391.9 3.0 copy-start.14
  391.9 3.9 copy-start.12
  433.7 2.0 copy-start.17
  433.7 2.0 copy-start.23
  433.7 2.3 copy-start.3
  433.7 2.3 copy-start.25
  436.0 1.8 copy-start.10
  437.8 32.7 %copy-start.7 = (bf16[16,72,768]{2,1,0:T(8,128)(2,1)S(1)}, bf16[16,72,768]{2,1,0:T(8,128)(2,1)}, u32[]{:S(2)}) copy-start(bf16[16,72,768]{2,1,0:T(8,128)(2,1)} %get-tuple-element.78) | copy-start | bytes 5308420
  481.2 3.3 copy-start.15
  482.3 3.4 copy-start.13
  486.6 4.1 copy-start.24

commit v3 on v2

--- a/solution.py
+++ b/solution.py
@@ -238,13 +238,6 @@
     return jnp.where(odd, odd_rows, even_rows)
 
 
-def collect_rows(wide, odd):
-    f0, h0, f1, h1, f2 = (wide[64 * i : 64 * i + 64] for i in range(5))
-    even_rows = jnp.concatenate([f0, f1, f2, h0, h1[:32]])
-    odd_rows = jnp.concatenate([h0[32:], h1, f0, f1, f2])
-    return jnp.where(odd, odd_rows, even_rows)
-
-
 def turn(x, cos, sin, lanes):
     swapped = jnp.where(lanes, pltpu.roll(x, 96, 1), pltpu.roll(x, 32, 1))
     return x * cos + swapped * sin
@@ -284,47 +277,6 @@
         ],
         compiler_params=pltpu.CompilerParams(vmem_limit_bytes=VMEM_LIMIT),
     )(normed, weight, cos, sin)
-
-
-def unproject(q_grad, kv_grad, weight, cos, sin):
-    rows = q_grad.shape[0]
-    tile = 256
-
-    def kernel(q_ref, kv_ref, w_ref, c_ref, s_ref, pg_ref, dn_ref):
-        cos_t, sin_t = c_ref[...], -s_ref[...]
-        low = lax.rem(lax.broadcasted_iota(jnp.int32, (tile, 128), 1), 64) < 32
-        total = kv_ref[0].astype(F32)
-        for c in range(1, kv_ref.shape[0]):
-            total += kv_ref[c].astype(F32)
-        for b in range(3):
-            block = q_ref[:, 128 * b : 128 * b + 128].astype(BF).astype(F32)
-            pg_ref[:, 128 * b : 128 * b + 128] = turn(block, cos_t, sin_t, low).astype(BF)
-        block = total[:, :128].astype(BF).astype(F32)
-        pg_ref[:, 384:512] = turn(block, cos_t, sin_t, low).astype(BF)
-        pg_ref[:, 512:] = total[:, 128:].astype(BF)
-        dn_ref[...] = dot_general(pg_ref[...], w_ref[...], 1, 1).astype(BF)
-
-    return pl.pallas_call(
-        kernel,
-        name="unproject",
-        grid=(rows // tile,),
-        in_specs=[
-            pl.BlockSpec((tile, 384), lambda i: (i, 0)),
-            pl.BlockSpec((kv_grad.shape[0], tile, 256), lambda i: (0, i, 0)),
-            pl.BlockSpec((D, 640), lambda i: (0, 0)),
-            pl.BlockSpec((tile, 128), lambda i: (i, 0)),
-            pl.BlockSpec((tile, 128), lambda i: (i, 0)),
-        ],
-        out_specs=[
-            pl.BlockSpec((tile, 640), lambda i: (i, 0)),
-            pl.BlockSpec((tile, D), lambda i: (i, 0)),
-        ],
-        out_shape=[
-            jax.ShapeDtypeStruct((rows, 640), BF),
-            jax.ShapeDtypeStruct((rows, D), BF),
-        ],
-        compiler_params=pltpu.CompilerParams(vmem_limit_bytes=VMEM_LIMIT),
-    )(q_grad, kv_grad, weight, cos, sin)
 
 
 TQ = 256
@@ -418,15 +370,26 @@
     )(q, kv, q_pos, q_seg, k_pos, k_seg)
 
 
-def attend_backward(link, q, kv, q_pos, q_seg, k_pos, k_seg, lse, out, out_grad, send_rows):
+def owner_of(link):
+    ctx, wsh = link.sizes["ctx"], link.sizes["wsh"]
+    my_c, my_w = lax.axis_index("ctx"), lax.axis_index("wsh")
+    shard = my_w * ctx + my_c
+    to_c, to_w = shard // wsh, lax.rem(shard, wsh)
+    return {"ctx": to_c, "wsh": to_w}, jnp.logical_and(to_c == my_c, to_w == my_w)
+
+
+def attend_backward(
+    link, q, kv, q_pos, q_seg, k_pos, k_seg, lse, out, out_grad, send_rows, send_down
+):
     rows, keys = q.shape[0], kv.shape[0]
     steps = rows // TQ
-    axes = ("ctx", "wsh")
+    axes = ("ctx",)
     peers = link.offsets(axes)
+    everyone = link.offsets(("ctx", "wsh"))
 
     def kernel(
-        q_ref, kv_ref, qp_ref, qs_ref, kp_ref, ks_ref, lse_ref, o_ref, do_ref, rows_ref,
-        dq_ref, dkv_ref, got_ref, acc, kv_acc, bounce, send, recv, near,
+        q_ref, kv_ref, qp_ref, qs_ref, kp_ref, ks_ref, lse_ref, o_ref, do_ref, rows_ref, down_ref,
+        dq_ref, dkv_ref, got_ref, down_got, acc, kv_acc, bounce, bounce_two, send, recv, near,
     ):
         _, me = link.place(axes, peers[0])
         copies = []
@@ -442,18 +405,36 @@
                     device_id_type=MESH,
                 )
             )
-        inward = pltpu.make_async_copy(rows_ref.at[me], bounce, near)
-        outward = pltpu.make_async_copy(bounce, got_ref.at[me], near)
+        owner, stays = owner_of(link)
+        move = pltpu.make_async_remote_copy(
+            down_ref,
+            down_got,
+            send.at[len(peers)],
+            recv.at[len(peers)],
+            device_id=owner,
+            device_id_type=MESH,
+        )
+        inward = pltpu.make_async_copy(rows_ref.at[me], bounce, near.at[0])
+        outward = pltpu.make_async_copy(bounce, got_ref.at[me], near.at[0])
+        stay_in = pltpu.make_async_copy(down_ref, bounce_two, near.at[1])
+        stay_out = pltpu.make_async_copy(bounce_two, down_got, near.at[1])
 
         @pl.when(pl.program_id(0) == 0)
         def _():
-            barrier = pltpu.get_barrier_semaphore()
-            for offset in peers[1:]:
-                where, _ = link.place(axes, offset)
-                pl.semaphore_signal(barrier, 1, device_id=where, device_id_type=MESH)
-            pl.semaphore_wait(barrier, len(peers) - 1)
+            greet([link.place(("ctx", "wsh"), offset)[0] for offset in everyone[1:]])
             for copy in copies:
                 copy.start()
+
+            @pl.when(jnp.logical_not(stays))
+            def _():
+                move.start()
+
+            @pl.when(stays)
+            def _():
+                stay_in.start()
+                stay_in.wait()
+                stay_out.start()
+
             inward.start()
             inward.wait()
             outward.start()
@@ -502,6 +483,14 @@
             for copy in copies:
                 copy.wait()
 
+            @pl.when(jnp.logical_not(stays))
+            def _():
+                move.wait()
+
+            @pl.when(stays)
+            def _():
+                stay_out.wait()
+
     return pl.pallas_call(
         kernel,
         name="attend_backward",
@@ -517,29 +506,466 @@
             pl.BlockSpec((TQ, 384), lambda i: (i, 0)),
             pl.BlockSpec((TQ, 384), lambda i: (i, 0)),
             pl.BlockSpec(memory_space=pl.ANY),
+            pl.BlockSpec(memory_space=pl.ANY),
         ],
         out_specs=[
             pl.BlockSpec((TQ, 384), lambda i: (i, 0)),
             pl.BlockSpec((keys, 256), lambda i: (0, 0)),
             pl.BlockSpec(memory_space=pl.ANY),
+            pl.BlockSpec(memory_space=pl.ANY),
         ],
         out_shape=[
             jax.ShapeDtypeStruct((rows, 384), BF),
             jax.ShapeDtypeStruct((keys, 256), BF),
             jax.ShapeDtypeStruct(send_rows.shape, BF),
+            jax.ShapeDtypeStruct(send_down.shape, BF),
         ],
         scratch_shapes=[
             pltpu.VMEM((5, 128, TQ), F32),
             pltpu.VMEM((keys, 256), F32),
             pltpu.VMEM(send_rows.shape[1:], BF),
-            pltpu.SemaphoreType.DMA((len(peers),)),
-            pltpu.SemaphoreType.DMA((len(peers),)),
-            pltpu.SemaphoreType.DMA,
+            pltpu.VMEM(send_down.shape, BF),
+            pltpu.SemaphoreType.DMA((len(peers) + 1,)),
+            pltpu.SemaphoreType.DMA((len(peers) + 1,)),
+            pltpu.SemaphoreType.DMA((2,)),
         ],
         compiler_params=pltpu.CompilerParams(
             collective_id=11, has_side_effects=True, vmem_limit_bytes=VMEM_LIMIT
         ),
-    )(q, kv, q_pos, q_seg, k_pos, k_seg, lse, out, out_grad, send_rows)
+    )(q, kv, q_pos, q_seg, k_pos, k_seg, lse, out, out_grad, send_rows, send_down)
+
+
+class Wires:
+    def __init__(self, send, recv):
+        self.send, self.recv, self.used = send, recv, 0
+
+    def copy(self, source, target, where):
+        at = self.used
+        self.used += 1
+        return pltpu.make_async_remote_copy(
+            source,
+            target,
+            self.send.at[at],
+            self.recv.at[at],
+            device_id=where,
+            device_id_type=MESH,
+        )
+
+    def start(self, source, target, where):
+        copy = self.copy(source, target, where)
+        copy.start()
+        return copy
+
+
+def greet(places):
+    barrier = pltpu.get_barrier_semaphore()
+    for where in places:
+        pl.semaphore_signal(barrier, 1, device_id=where, device_id_type=MESH)
+    pl.semaphore_wait(barrier, len(places))
+
+
+def square():
+    w = lax.axis_index("wsh")
+    return w, w + 1 - 2 * lax.rem(w, 2), w + 2 - 4 * (w // 2), 3 - w
+
+
+class SquareScatter:
+    def __init__(self, wires, parts, near, total):
+        self.wires, self.parts, self.near, self.total = wires, parts, near, total
+        self.half = parts.shape[1] // 2
+        self.a, self.b = pl.ds(0, self.half), pl.ds(self.half, self.half)
+        self.own, self.x, self.y, self.z = square()
+        self.pending = []
+
+    def send_diagonal(self):
+        wires, parts = self.wires, self.parts
+        self.one = wires.start(parts.at[self.z, self.a], self.near.at[0], {"wsh": self.x})
+        self.two = wires.start(parts.at[self.z, self.b], self.near.at[1], {"wsh": self.y})
+
+    def send_x(self):
+        self.pending.append(
+            self.wires.start(
+                self.parts.at[self.x, self.a], self.total.at[0, self.a], {"wsh": self.x}
+            )
+        )
+
+    def send_y(self):
+        self.pending.append(
+            self.wires.start(
+                self.parts.at[self.y, self.b], self.total.at[1, self.b], {"wsh": self.y}
+            )
+        )
+
+    def relay(self):
+        near, parts = self.near, self.parts
+        self.one.wait()
+        near[2] = (near[0].astype(F32) + parts[self.y, self.a].astype(F32)).astype(BF)
+        self.pending.append(
+            self.wires.start(near.at[2], self.total.at[1, self.a], {"wsh": self.y})
+        )
+        self.two.wait()
+        near[3] = (near[1].astype(F32) + parts[self.x, self.b].astype(F32)).astype(BF)
+        self.pending.append(
+            self.wires.start(near.at[3], self.total.at[0, self.b], {"wsh": self.x})
+        )
+
+    def result(self):
+        for copy in self.pending:
+            copy.wait()
+        return (
+            self.parts[self.own].astype(F32)
+            + self.total[0].astype(F32)
+            + self.total[1].astype(F32)
+        )
+
+
+def square_scratch(rows):
+    return [pltpu.VMEM((4, rows // 2, D), BF), pltpu.VMEM((2, rows, D), BF)]
+
+
+def finish(
+    link, q_grad, kv_grad, weight, cos, sin, normed, tokens, gain, middle_grad, gate_got, down_got,
+    attended, branch, feed_sum, down_part, middle,
+):
+    ctx, wsh = link.sizes["ctx"], link.sizes["wsh"]
+    shards = ctx * wsh
+    rows = D // shards
+    chunk = D // ctx
+    fold = ctx // wsh
+    own_rows = tokens.shape[0]
+    plane = normed.shape[0]
+    axes = ("ctx", "wsh")
+    peers = link.offsets(axes)
+    gate_width = gate_got.shape[2]
+    down_rows = down_got.shape[0]
+
+    def kernel(
+        q_ref, kv_send, w_ref, c_ref, s_ref, n_ref, x_ref, g_ref, mg_ref, gate_ref, down_ref,
+        at_ref, br_ref, fs_ref, dp_ref, mid_ref,
+        act_ref, ig_ref, qkv_ref, out_ref, gate_out, down_out, gains_out,
+        kv_ref, pg, parts, near, total, near2, total2, acc, wide, q_own, q_pair, q_send, q_got,
+        q_mid, q_fin, kv_own, kv_pair, kv_go, kv_got, kv_mid, kv_fin, gate_mid, gate_fin, down_fin, out_halves,
+        out_pair, out_send, out_mid, out_got, out_fin, gains, gains_got, gains_fin,
+        send, recv,
+    ):
+        wires = Wires(send, recv)
+        core = lax.axis_index("grp")
+        first, second = core == 0, core == 1
+        sibling = {"grp": 1 - core}
+        my_c, my_w = lax.axis_index("ctx"), lax.axis_index("wsh")
+        odd = lax.rem(my_w, 2) == 1
+        greet([link.place(axes, offset)[0] for offset in peers[1:]] + [sibling])
+        _, me = link.place(axes, peers[0])
+
+        def over_ctx(got, mid):
+            for w in range(wsh):
+                strip = got[0, w * rows : w * rows + rows, :].astype(F32)
+                for c in range(1, ctx):
+                    strip += got[c, w * rows : w * rows + rows, :].astype(F32)
+                mid[w] = strip.astype(BF)
+
+        def in_plane(mid, slot_of):
+            copies = []
+            for offset in link.offsets(("wsh",))[1:]:
+                where, index = link.place(("wsh",), offset)
+                copies.append(wires.copy(mid.at[index], slot_of(my_w), where))
+            return copies
+
+        def begin(cond, *copies):
+            @pl.when(cond)
+            def _():
+                for copy in copies:
+                    copy.start()
+
+        kv_copies = []
+        for offset in link.offsets(("ctx",))[1:]:
+            where, index = link.place(("ctx",), offset)
+            kv_copies.append(wires.start(kv_send.at[index], kv_ref.at[my_c], where))
+        layer = SquareScatter(wires, dp_ref, near2, total2)
+        layer.send_diagonal()
+        layer.send_x()
+        layer.send_y()
+        kv_ref[my_c] = kv_send[my_c]
+
+        wide[...] = dot_general(at_ref[...], br_ref[...], 0, 0)
+
+        def out_strips(pieces):
+            at = 0
+            for start, size in pieces:
+                acc_rows = wide[start : start + size, :].astype(BF)
+                part = jnp.concatenate([acc_rows[:, :576], jnp.zeros((size, 64), BF)], axis=1)
+                out_halves[0, at : at + size, :] = part
+                part = jnp.concatenate([acc_rows[:, 576:], jnp.zeros((size, 64), BF)], axis=1)
+                out_halves[1, at : at + size, :] = part
+                at += size
+
+        @pl.when(odd)
+        def _():
+            out_strips([(96, 32), (192, 64), (0, 64), (128, 64), (256, 64)])
+
+        @pl.when(jnp.logical_not(odd))
+        def _():
+            out_strips([(0, 64), (128, 64), (256, 64), (64, 64), (192, 32)])
+
+        out_swap = wires.start(out_halves.at[1 - core], out_pair, sibling)
+        low = lax.rem(lax.broadcasted_iota(jnp.int32, (own_rows, 128), 1), 64) < 32
+
+        @pl.loop(0, wsh)
+        def _(slot):
+            at = pl.ds(pl.multiple_of(slot * own_rows, 16), own_rows)
+            for b in range(3):
+                block = q_ref[at, 128 * b : 128 * b + 128].astype(F32)
+                pg[at, 128 * b : 128 * b + 128] = turn(
+                    block, c_ref[at, :], -s_ref[at, :], low
+                ).astype(BF)
+
+        layer.relay()
+        for b in range(3):
+            acc[384 * b : 384 * b + 384, :] = dot_general(
+                n_ref[:, 384 * b : 384 * b + 384], pg[:, :384], 0, 0
+            )
+
+        for c in range(ctx):
+            q_own[c] = acc[c * chunk : c * chunk + chunk, :].astype(BF)
+        q_swap = wires.copy(q_own, q_pair, sibling)
+        begin(second, q_swap)
+
+        down_fin[core] = down_ref[...]
+        down_copy = wires.start(down_fin.at[core], down_fin.at[core], sibling)
+
+        over_ctx(gate_ref, gate_mid)
+        gate_moves = in_plane(gate_mid, lambda w: gate_fin.at[core, w])
+        for copy in gate_moves:
+            copy.start()
+        gate_fin[core, my_w] = gate_mid[my_w]
+        act_ref[...] = (mid_ref[...] + layer.result()).astype(BF)
+        out_swap.wait()
+        for k in range(ctx):
+            strip = slice(k * rows, k * rows + rows)
+            out_send[k % wsh, k // wsh] = (
+                out_halves[core, strip, :].astype(F32) + out_pair[strip, :].astype(F32)
+            ).astype(BF)
+        out_moves = in_plane(out_send, lambda w: out_mid.at[w])
+        for copy in out_moves:
+            copy.start()
+        out_mid[my_w] = out_send[my_w]
+
+        @pl.when(first)
+        def _():
+            q_swap.wait_recv()
+
+            @pl.loop(0, ctx)
+            def _(c):
+                q_send[c] = (q_own[c].astype(F32) + q_pair[c].astype(F32)).astype(BF)
+
+        @pl.when(second)
+        def _():
+            q_swap.wait_send()
+
+        for copy in gate_moves:
+            copy.wait()
+        gate_copy = wires.start(gate_fin.at[core], gate_fin.at[core], sibling)
+        down_copy.wait()
+        down_out[:down_rows, :] = down_fin[0].astype(F32)
+        down_out[down_rows:, :] = down_fin[1].astype(F32)
+        gate_copy.wait()
+        for half in range(2):
+            for w in range(wsh):
+                left = (half * wsh + w) * gate_width
+                gate_out[:, left : left + gate_width] = gate_fin[half, w].astype(F32)
+
+        for copy in out_moves:
+            copy.wait()
+
+        for copy in kv_copies:
+            copy.wait()
+        q_copies, kvg_copies, out_copies = [], [], []
+        for offset in link.offsets(("ctx",))[1:]:
+            where, index = link.place(("ctx",), offset)
+            q_copies.append(wires.copy(q_send.at[index], q_got.at[my_c], where))
+            kvg_copies.append(wires.copy(kv_go.at[index], kv_got.at[my_c], where))
+        begin(first, *q_copies)
+        for offset in link.offsets(("ctx",))[1:]:
+            where, index = link.place(("ctx",), offset)
+            part = out_mid.at[index // fold, lax.rem(index, fold)]
+            out_copies.append(wires.start(part, out_got.at[my_c], where))
+        out_got[my_c] = out_mid[my_c // fold, lax.rem(my_c, fold)]
+        scatter = SquareScatter(wires, parts, near, total)
+        gain_sum = jnp.zeros((1, D), F32)
+        for slot in (scatter.z, scatter.x, scatter.y, scatter.own):
+            at = pl.ds(pl.multiple_of(slot * own_rows, 16), own_rows)
+            summed = kv_ref[0, at, :].astype(F32)
+            for c in range(1, ctx):
+                summed += kv_ref[c, at, :].astype(F32)
+            block = summed[:, :128].astype(BF).astype(F32)
+            pg[at, 384:512] = turn(block, c_ref[at, :], -s_ref[at, :], low).astype(BF)
+            pg[at, 512:] = summed[:, 128:].astype(BF)
+            part = dot_general(pg[at, :], w_ref[...], 1, 1)
+            parts[slot] = part.astype(BF)
+            gain_sum += jnp.sum(part * n_ref[at, :].astype(F32), axis=0, keepdims=True)
+            if slot is scatter.z:
+                scatter.send_diagonal()
+            elif slot is scatter.x:
+                scatter.send_x()
+            elif slot is scatter.y:
+                scatter.send_y()
+
+        for b in range(3):
+            acc[384 * b : 384 * b + 384, :256] = dot_general(
+                n_ref[:, 384 * b : 384 * b + 384], pg[:, 384:], 0, 0
+            )
+
+        for c in range(ctx):
+            kv_own[c] = acc[c * chunk : c * chunk + chunk, :256].astype(BF)
+        kv_swap = wires.copy(kv_own, kv_pair, sibling)
+        begin(first, kv_swap)
+        both = jnp.concatenate([gain_sum / g_ref[...], fs_ref[...]], axis=0)
+        gains[...] = jnp.zeros_like(gains)
+        for s in range(shards):
+            gains[s, :2, :rows] = both[:, rows * s : rows * s + rows]
+        gain_copies = []
+        for offset in peers[1:]:
+            where, index = link.place(axes, offset)
+            gain_copies.append(wires.start(gains.at[index], gains_got.at[me], where))
+        gains_got[me] = gains[me]
+        scatter.relay()
+
+        @pl.when(second)
+        def _():
+            kv_swap.wait_recv()
+
+            @pl.loop(0, ctx)
+            def _(c):
+                kv_go[c] = (kv_own[c].astype(F32) + kv_pair[c].astype(F32)).astype(BF)
+
+            for copy in kvg_copies:
+                copy.start()
+            kv_got[my_c] = kv_go[my_c]
+
+        @pl.when(first)
+        def _():
+            kv_swap.wait_send()
+            q_got[my_c] = q_send[my_c]
+            for copy in q_copies:
+                copy.wait()
+            over_ctx(q_got, q_mid)
+
+        q_moves = in_plane(q_mid, lambda w: q_fin.at[w])
+        begin(first, *q_moves)
+        for copy in out_copies:
+            copy.wait()
+        out_fin[core] = jnp.sum(out_got[...].astype(F32), axis=0).astype(BF)
+
+        out_copy = wires.start(out_fin.at[core], out_fin.at[core], sibling)
+
+        grad = scatter.result()
+        x = x_ref[...].astype(F32)
+        factor = lax.rsqrt(jnp.mean(x * x, axis=-1, keepdims=True) + EPSILON)
+        weighted = grad * g_ref[...]
+        inner = jnp.mean(weighted * x, axis=-1, keepdims=True)
+        ig_ref[...] = mg_ref[...] + factor * weighted - x * (factor * factor * factor) * inner
+        q_final = wires.copy(q_fin, q_fin, sibling)
+        kv_final = wires.copy(kv_fin, kv_fin, sibling)
+
+        kv_moves = in_plane(kv_mid, lambda w: kv_fin.at[w])
+
+        @pl.when(first)
+        def _():
+            for copy in q_moves:
+                copy.wait()
+            q_fin[my_w] = q_mid[my_w]
+            q_final.start()
+
+        @pl.when(second)
+        def _():
+            for copy in kvg_copies:
+                copy.wait()
+            over_ctx(kv_got, kv_mid)
+            for copy in kv_moves:
+                copy.start()
+            for copy in kv_moves:
+                copy.wait()
+            kv_fin[my_w] = kv_mid[my_w]
+            kv_final.start()
+
+        for copy in gain_copies:
+            copy.wait()
+        gains_fin[core] = jnp.sum(gains_got[...], axis=0)
+        gain_copy = wires.start(gains_fin.at[core], gains_fin.at[core], sibling)
+        out_copy.wait()
+        out_ref[...] = jnp.concatenate(
+            [out_fin[0, :, :576].astype(F32), out_fin[1, :, :576].astype(F32)], axis=1
+        )
+
+        @pl.when(first)
+        def _():
+            q_final.wait_send()
+            kv_final.wait_recv()
+
+        @pl.when(second)
+        def _():
+            kv_final.wait_send()
+            q_final.wait_recv()
+
+        qkv_ref[...] = qkv_restore(
+            [
+                jnp.concatenate([q_fin[w].astype(F32), kv_fin[w].astype(F32)], axis=1)
+                for w in range(wsh)
+            ]
+        )
+        gain_copy.wait()
+        gains_out[...] = gains_fin[0] + gains_fin[1]
+
+    operands = (
+        q_grad, kv_grad, weight, cos, sin, normed, tokens, gain, middle_grad, gate_got, down_got,
+        attended, branch, feed_sum, down_part, middle,
+    )
+    vmem = pl.BlockSpec(memory_space=pltpu.VMEM)
+    return pl.pallas_call(
+        kernel,
+        name="finish",
+        in_specs=[vmem] * len(operands),
+        out_specs=[vmem] * 7,
+        out_shape=[
+            jax.ShapeDtypeStruct((own_rows, D), BF),
+            jax.ShapeDtypeStruct((own_rows, D), F32),
+            jax.ShapeDtypeStruct((rows, QW + 2 * KW), F32),
+            jax.ShapeDtypeStruct((rows, D), F32),
+            jax.ShapeDtypeStruct((rows, 2 * FF), F32),
+            jax.ShapeDtypeStruct((2 * down_rows, D), F32),
+            jax.ShapeDtypeStruct((8, 128), F32),
+        ],
+        scratch_shapes=[
+            pltpu.VMEM((ctx, plane, 256), BF),
+            pltpu.VMEM((plane, 640), BF),
+            pltpu.VMEM((4, own_rows, D), BF),
+            *square_scratch(own_rows),
+            *square_scratch(own_rows),
+            pltpu.VMEM((D, 384), F32),
+            pltpu.VMEM((384, D), F32),
+            *[pltpu.VMEM((ctx, chunk, 384), BF)] * 4,
+            *[pltpu.VMEM((wsh, rows, 384), BF)] * 2,
+            *[pltpu.VMEM((ctx, chunk, 256), BF)] * 4,
+            *[pltpu.VMEM((wsh, rows, 256), BF)] * 2,
+            pltpu.VMEM((wsh, rows, gate_width), BF),
+            pltpu.VMEM((2, wsh, rows, gate_width), BF),
+            pltpu.VMEM((2, down_rows, D), BF),
+            pltpu.VMEM((2, 288, 640), BF),
+            pltpu.VMEM((288, 640), BF),
+            pltpu.VMEM((wsh, fold, rows, 640), BF),
+            pltpu.VMEM((wsh, fold, rows, 640), BF),
+            pltpu.VMEM((ctx, rows, 640), BF),
+            pltpu.VMEM((2, rows, 640), BF),
+            pltpu.VMEM((shards, 8, 128), F32),
+            pltpu.VMEM((shards, 8, 128), F32),
+            pltpu.VMEM((2, 8, 128), F32),
+            pltpu.SemaphoreType.DMA((3 * shards + 2 * ctx + 32,)),
+            pltpu.SemaphoreType.DMA((3 * shards + 2 * ctx + 32,)),
+        ],
+        compiler_params=pltpu.CompilerParams(
+            collective_id=8, has_side_effects=True, vmem_limit_bytes=VMEM_LIMIT
+        ),
+    )(*operands)
 
 
 def rms_factor(values):
@@ -657,7 +1083,7 @@
         up_w_grad = dot_general(normed_two_all, up_grad, 0, 0).astype(BF)
         ffn_rows = FF // shards // 2
         down_halves = down_grad.reshape(ctx, 2, ffn_rows, D).transpose(1, 0, 2, 3)
-        gate_halves = jnp.stack([gate_w_grad, up_w_grad]).reshape(2, shards, D // shards, FF // wsh)
+        gate_halves = jnp.stack([gate_w_grad, up_w_grad]).reshape(2, ctx, D // ctx, FF // wsh)
         two_parts, down_pair, gate_pair = link.run(
             "scatter_feed",
             5,
@@ -684,79 +1110,17 @@
         )
         branch_all = branch_all.reshape(plane, D)
         attended_grad = dot_general(branch_all, w_out, 1, 1).astype(BF)
-        q_grad, kv_grad, gate_got = attend_backward(
+        down_sum = jnp.sum(down_got.astype(F32), axis=0).astype(BF)
+        q_grad, kv_grad, gate_got, down_got = attend_backward(
             link, queries, kv_all, q_pos, q_seg, k_pos, k_seg, lse, attended_wide, attended_grad,
-            gate_send,
-        )
-        out_grad = collect_rows(dot_general(attended, branch_all, 0, 0), odd).astype(BF)
-        out_halves = out_grad.reshape(ctx, D // shards, 2, 576).transpose(2, 0, 1, 3)
-        kv_parts, down_parts, out_pair = link.run(
-            "scatter_keys",
-            7,
-            [
-                link.swap(kv_grad.reshape(ctx, plane, 256), ("ctx",)),
-                link.swap(down_part.reshape(wsh, own, D), ("wsh",)),
-                link.swap(out_halves, ("grp",)),
-            ],
-        )
-        activations = (middle + jnp.sum(down_parts.astype(F32), axis=0)).astype(BF)
-        out_send = (out_pair[0].astype(F32) + out_pair[1].astype(F32)).astype(BF)
-        projected_grad, one_part = unproject(q_grad, kv_parts, w_qkv, cos, sin)
-        qkv_grad = dot_general(normed_all, projected_grad, 0, 0).astype(BF)
-        qkv_halves = qkv_grad.reshape(shards, D // shards, 2, 320).transpose(2, 0, 1, 3)
-        down_half = jnp.sum(down_got.astype(F32), axis=0).astype(BF)
-        one_parts, qkv_pair, out_got, down_half = link.run(
-            "scatter_one",
-            8,
-            [
-                link.swap(one_part.reshape(wsh, own, D), ("wsh",)),
-                link.swap(qkv_halves, ("grp",)),
-                link.swap(out_send, ("ctx",)),
-                link.turn_over(down_half),
-            ],
-        )
-        normed_one_grad = jnp.sum(one_parts.astype(F32), axis=0)
-        input_part, attend_gain_grad = norm_back(normed_one_grad, inputs, factor_one, attend_gain)
-        input_grad = middle_grad + input_part
-        qkv_send = (qkv_pair[0].astype(F32) + qkv_pair[1].astype(F32)).astype(BF)
-        gains = jnp.stack([attend_gain_grad, feed_gain_grad]).reshape(2, shards, D // shards)
-        gains = jnp.pad(gains.transpose(1, 0, 2), ((0, 0), (0, 6), (0, 128 - D // shards)))
-        out_half = jnp.sum(out_got.astype(F32), axis=0).astype(BF)
-        qkv_got, gains_got, out_half = link.run(
-            "scatter_weights",
-            9,
-            [
-                link.swap(qkv_send, ("ctx", "wsh")),
-                link.swap(gains, ("ctx", "wsh")),
-                link.turn_over(out_half),
-            ],
-        )
-
-        def over_ctx(x):
-            return jnp.sum(x.reshape((ctx, wsh) + x.shape[1:]).astype(F32), axis=0)
-
-        gate_half = over_ctx(gate_got).astype(BF)
-        qkv_half = over_ctx(qkv_got).astype(BF)
-        gain_half = jnp.sum(gains_got, axis=0)
-        down_two, out_two, gate_two, qkv_two, gain_two = link.run(
-            "swap_cores",
-            10,
-            [
-                link.gather(down_half, ("grp",)),
-                link.gather(out_half, ("grp",)),
-                link.gather(gate_half, ("grp",)),
-                link.gather(qkv_half, ("grp",)),
-                link.gather(gain_half, ("grp",)),
-            ],
-        )
-        rows = D // shards
-        down_out = down_two.reshape(FF // shards, D).astype(F32)
-        out_out = out_two.transpose(1, 0, 2).reshape(rows, D).astype(F32)
-        gate_out = gate_two.transpose(2, 0, 1, 3).reshape(rows, 2 * FF).astype(F32)
-        qkv_out = qkv_restore(
-            qkv_two.transpose(1, 2, 0, 3).reshape(wsh, rows, 640).astype(F32)
-        )
-        gain_out = gain_two[0] + gain_two[1]
+            gate_send, down_sum,
+        )
+        (activations, input_grad, qkv_out, out_out, gate_out, down_out, gain_out) = finish(
+            link, q_grad, kv_grad.reshape(ctx, plane, 256), w_qkv, cos, sin, normed_all, tokens,
+            attend_gain[None, :], middle_grad, gate_got, down_got, attended, branch_all,
+            feed_gain_grad[None, :], down_part.reshape(wsh, own, D), middle,
+        )
+        width = D // shards
         return (
             activations,
             input_grad,
@@ -764,8 +1128,8 @@
             out_out,
             gate_out,
             down_out,
-            gain_out[0, :rows],
-            gain_out[1, :rows],
+            gain_out[0, :width],
+            gain_out[1, :width],
         )
 
     return local

time: 500 us -> 445 us (0.89)
  other arithmetic: 45.2 us -> 23.6 us
  Pallas kernels: 374 us -> 361 us
  local copies, waits for them, and re-layouts: 38.4 us -> 26.1 us
  matrix products: 32.5 us -> 26 us
    pallas_call x10 -> x6, Pallas kernels: 272 us -> 174 us  [run(): pl.pallas_call(kernel, name=name, out_shape=[jax.ShapeDtypeStruct(op[4],...]
    pallas_call x1, Pallas kernels: 5.74 us -> 88.7 us  [finish(): pl.pallas_call(kernel, name='finish', in_specs=[vmem] * len(operands), ou...]
    reduce_sum x7 -> x1, other arithmetic: 10.9 us -> 0.85 us  [local(): down_sum = jnp.sum(down_got.astype(F32), axis=0).astype(BF)]
    convert_element_type x6 -> x0, local copies, waits for them, and re-layouts: 9.28 us -> none  [the longest x2 5.29 us: local(): collect_rows(dot_general(attended, branch_all, 0, 0), odd).astype(BF)]
    reshape x2 -> x0, local copies, waits for them, and re-layouts: 8.05 us -> none  [local(): qkv_grad.reshape(shards, D // shards, 2, 320).transpose(2, 0, 1, 3)]
    unnamed x86 -> x67, local copies, waits for them, and re-layouts: 4.17 us -> 12.2 us
    convert_element_type x8 -> x0, other arithmetic: 7.01 us -> none  [the longest x1 1.98 us: local(): down_out = down_two.reshape(FF // shards, D).astype(F32)]
    dot_general x9 -> x7, matrix products: 20.1 us -> 15.1 us  [dot_general(): lax.dot_general(a, b, (((ca,), (cb,)), ((), ())), preferred_element_type=...]
where the time goes in v3:
time: 445 us; the launch traced here: 438 us
  Pallas kernels  361 us (81%)
  local copies, waits for them, and re-layouts  26.1 us (6%)
  matrix products  26 us (6%)
  other arithmetic  23.6 us (5%)
    pallas_call x6, Pallas kernels, run(): pl.pallas_call(kernel, name=name, out_shape=[jax.ShapeDtypeStruct(op[4],...  174 us
    pallas_call x1, Pallas kernels, finish(): pl.pallas_call(kernel, name='finish', in_specs=[vmem] * len(operands), ou...  88.7 us
    pallas_call x1, Pallas kernels, attend_backward(): pl.pallas_call(kernel, name='attend_backward', grid=(steps,), in_specs=[p...  48.1 us
    pallas_call x1, Pallas kernels, attend_forward(): pl.pallas_call(kernel, name='attend_forward', grid=(rows // TQ,), in_spec...  44.7 us
    dot_general x7, matrix products, dot_general(): lax.dot_general(a, b, (((ca,), (cb,)), ((), ())), preferred_element_type=...  15.1 us
    unnamed x67, local copies, waits for them, and re-layouts  12.2 us

profile of v3, /device:TPU:0, one launch (start us, length us, event | category | flops | bytes accessed | tf_op | source)
XLA Modules:
  0.0 438.0 jit_solution(892252270606536681)
XLA Ops:
  0.7 1.3 fusion.16
  2.0 2.0 fusion.18.refs_0_
  4.0 1.2 fusion.25
  6.0 1.2 concatenate.24
  8.1 1.3 concatenate.23
  9.3 1.2 concatenate.22
  10.6 1.3 concatenate.21
  11.9 1.3 pad_maximum_fusion.1.refs_1_
  13.8 40.5 %gather_one.1 = (bf16[4,192,1152]{2,1,0:T(8,128)(2,1)}, bf16[4,288,640]{2,1,0:T(8,128)(2,1)}, s32[4,8,128]{2,1,0:T(8,128)}) custom-call(bf16[192,1152]{1,0:T(8,128)(2,1)} %fusion.18.refs_0_, bf16[4,288,640]{2,1,0:T(8,128)(2,1)} %pad_maximum_fusion.1.refs_1_, s32[8,128]{1,0:T(8,128)} %pad_bitcast_fusion.refs_2_), custom_call_target="tpu_custom_call" | custom-call | tf_op jit(solution)/shard_map/gather_one/pallas_call | solution.py:161
  55.2 2.5 fusion.20
  57.7 5.3 %project.1 = (bf16[768,384]{1,0:T(8,128)(2,1)}, bf16[768,256]{1,0:T(8,128)(2,1)}) custom-call(bf16[768,1152]{1,0:T(8,128)(2,1)} %bitcast.69, bf16[1152,640]{1,0:T(8,128)(2,1)} %bitcast.73, f32[768,128]{1,0:T(8,128)} %get-tuple-element.118.c_ref, f32[768,128]{1,0:T(8,128)} %get-tuple-element.117.s_ref), custom_call_target="tpu_custom_call" | custom-call | tf_op jit(solution)/shard_map/project/pallas_call | solution.py:260
  63.0 44.1 %gather_keys.1 = (bf16[4,768,256]{2,1,0:T(8,128)(2,1)}, s32[4,4,8,128]{3,2,1,0:T(8,128)}, bf16[4,192,1152]{2,1,0:T(8,128)(2,1)}, bf16[4,288,768]{2,1,0:T(8,128)(2,1)}) custom-call(bf16[768,256]{1,0:T(8,128)(2,1)} %get-tuple-element.42.refs_0_, s32[4,8,128]{2,1,0:T(8,128)} %get-tuple-element.40.refs_1_, bf16[192,1152]{1,0:T(8,128)(2,1)} %refs_2_.1, ...), custom_call_target="tpu_custom_call" | custom-call | tf_op jit(solution)/shard_map/gather_keys/pallas_call | solution.py:161
  108.3 0.9 copy.29
  109.2 1.4 reshape.411
  110.6 3.0 add_select_fusion
  113.6 44.7 %attend_forward.1 = (bf16[768,384]{1,0:T(8,128)(2,1)}, f32[768,384]{1,0:T(8,128)}, f32[8,768]{1,0:T(8,128)}) custom-call(bf16[768,384]{1,0:T(8,128)(2,1)} %get-tuple-element.41.q_ref, bf16[3072,256]{1,0:T(8,128)(2,1)} %bitcast.71, s32[1,768]{1,0:T(1,128)} %and_select_fusion.1.qp_ref, s32[1,768]{1,0:T(1,128)} %get-tuple-element.74.qs_ref, ...), custom_call_target="tpu_custom_call" | custom-call | tf_op jit(solution)/shard_map/attend_forward/pallas_call | solution.py:342
  158.6 0.9 copy-done.17
  159.5 2.4 convolution_convert_fusion
  161.9 23.5 %scatter_out.1 = (bf16[4,192,1152]{2,1,0:T(8,128)(2,1)}, bf16[2,1152,768]{2,1,0:T(8,128)(2,1)}) custom-call(bf16[4,192,1152]{2,1,0:T(8,128)(2,1)} %bitcast.79, bf16[1152,768]{1,0:T(8,128)(2,1)} %bitcast.78), custom_call_target="tpu_custom_call" | custom-call | tf_op jit(solution)/shard_map/scatter_out/pallas_call | solution.py:161
  185.4 1.9 convert_reduce_fusion.1
  188.0 0.9 multiply_convert_fusion.3.refs_0_
  188.9 21.5 %gather_two.1 = bf16[4,192,1152]{2,1,0:T(8,128)(2,1)} custom-call(bf16[192,1152]{1,0:T(8,128)(2,1)} %multiply_convert_fusion.3.refs_0_), custom_call_target="tpu_custom_call" | custom-call | tf_op jit(solution)/shard_map/gather_two/pallas_call | solution.py:161
  210.4 3.3 fusion.5
  213.8 1.7 fusion.27
  215.5 2.3 multiply_convert_fusion
  217.8 1.7 fusion.3
  219.6 2.9 fusion
  222.5 1.7 convolution_convert_fusion.4
  224.2 1.4 copy.28
  225.6 1.8 convolution_convert_fusion.2
  227.4 1.6 convolution_convert_fusion.3
  229.0 2.1 pad_maximum_fusion.refs_2_
  231.1 22.3 %scatter_feed.1 = (bf16[4,192,1152]{2,1,0:T(8,128)(2,1)}, bf16[2,4,96,1152]{3,2,1,0:T(8,128)(2,1)}, bf16[2,4,288,768]{3,2,1,0:T(8,128)(2,1)}) custom-call(bf16[4,192,1152]{2,1,0:T(8,128)(2,1)} %bitcast.75, bf16[2,4,96,1152]{3,2,1,0:T(8,128)(2,1)} %bitcast.68, bf16[2,4,288,768]{3,2,1,0:T(8,128)(2,1)} %pad_maximum_fusion.refs_2_), custom_call_target="tpu_custom_call" | custom-call | tf_op jit(solution)/shard_map/scatter_feed/pallas_call | solution.py:161
  253.4 1.9 convert_reduce_fusion
  255.7 1.4 fusion.23
  257.6 1.1 fusion.19.refs_1_
  258.8 22.1 %gather_branch.1 = (bf16[4,192,1152]{2,1,0:T(8,128)(2,1)}, bf16[4,96,1152]{2,1,0:T(8,128)(2,1)}) custom-call(bf16[192,1152]{1,0:T(8,128)(2,1)} %get-tuple-element.70.refs_0_, bf16[4,96,1152]{2,1,0:T(8,128)(2,1)} %fusion.19.refs_1_), custom_call_target="tpu_custom_call" | custom-call | tf_op jit(solution)/shard_map/gather_branch/pallas_call | solution.py:161
  280.9 3.6 convolution_convert_fusion.5.do_ref
  284.5 1.7 fusion.2.rows_ref
  286.1 0.9 reduce_sum.71.down_ref
  287.0 48.1 %attend_backward.1 = (bf16[768,384]{1,0:T(8,128)(2,1)}, bf16[3072,256]{1,0:T(8,128)(2,1)}, bf16[4,288,768]{2,1,0:T(8,128)(2,1)}, bf16[96,1152]{1,0:T(8,128)(2,1)}) custom-call(bf16[768,384]{1,0:T(8,128)(2,1)} %get-tuple-element.41.q_ref, bf16[3072,256]{1,0:T(8,128)(2,1)} %bitcast.72, s32[1,768]{1,0:T(1,128)} %and_select_fusion.1.qp_ref, ...), custom_call_target="tpu_custom_call" | custom-call | tf_op jit(solution)/shard_map/attend_backward/pallas_call | solution.py:494
  336.3 2.9 convolution_convert_fusion.1
  339.2 88.7 %finish.1 = (bf16[192,1152]{1,0:T(8,128)(2,1)}, f32[192,1152]{1,0:T(8,128)}, f32[72,1920]{1,0:T(8,128)}, f32[72,1152]{1,0:T(8,128)}, f32[72,6144]{1,0:T(8,128)}, /*index=5*/f32[192,1152]{1,0:T(8,128)}, f32[8,128]{1,0:T(8,128)}) custom-call(bf16[768,384]{1,0:T(8,128)(2,1)} %get-tuple-element.57.q_ref, bf16[4,768,256]{2,1,0:T(8,128)(2,1)} %bitcast.88, ...), custom_call_target="tpu_custom_call" | custom-call | tf_op jit(solution)/shard_map/finish/pallas_call | solution.py:924
  427.9 1.3 slice_bitcast_fusion
  429.2 1.9 copy.49
  431.1 2.3 copy.50
  434.9 1.2 copy.53
  436.6 0.9 copy.54
  (85 shorter events, 9.6 us)
Async XLA Ops:
  0.6 213.1 %copy-start = (bf16[768,1152]{1,0:T(8,128)(2,1)S(1)}, bf16[768,1152]{1,0:T(8,128)(2,1)}, u32[]{:S(2)}) copy-start(bf16[768,1152]{1,0:T(8,128)(2,1)} %param.18) | copy-start | bytes 5308420
  0.6 3.3 copy-start.3
  10.6 2.6 copy-start.19
  10.6 2.6 copy-start.20
  113.6 44.7 %copy-start.5 = (bf16[288,1152]{1,0:T(8,128)(2,1)S(1)}, bf16[288,1152]{1,0:T(8,128)(2,1)}, u32[]{:S(2)}) copy-start(bf16[288,1152]{1,0:T(8,128)(2,1)} %param.15) | copy-start | bytes 1990660
  158.3 1.2 copy-start.12
  158.6 0.9 copy-start.17
  185.4 1.9 copy-start.2
  187.3 0.7 copy-start.15
  187.5 68.1 %copy-start.1 = (f32[192,1152]{1,0:T(8,128)}, f32[192,1152]{1,0:T(8,128)S(1)}, u32[]{:S(2)}) copy-start(f32[192,1152]{1,0:T(8,128)S(1)} %get-tuple-element.73.mid_ref) | copy-start | bytes 2654212
  188.0 22.4 %copy-start.21 = (bf16[2,1152,768]{2,1,0:T(8,128)(2,1)S(1)}, bf16[2,1152,768]{2,1,0:T(8,128)(2,1)}, u32[]{:S(2)}) copy-start(bf16[2,1152,768]{2,1,0:T(8,128)(2,1)} %get-tuple-element.51) | copy-start | bytes 10616836
  210.4 3.3 copy-start.22
  213.8 1.7 copy-start.8
  217.8 4.7 %copy-start.23 = (bf16[768,768]{1,0:T(8,128)(2,1)}, bf16[768,768]{1,0:T(8,128)(2,1)S(1)}, u32[]{:S(2)}) copy-start(bf16[768,768]{1,0:T(8,128)(2,1)S(1)} %get-tuple-element.76) | copy-start | bytes 3538948
  253.4 2.2 copy-start.6
  255.7 2.0 copy-start.9
  257.6 23.2 %copy-start.18 = (bf16[384,1152]{1,0:T(8,128)(2,1)S(1)}, bf16[384,1152]{1,0:T(8,128)(2,1)}, u32[]{:S(2)}) copy-start(bf16[384,1152]{1,0:T(8,128)(2,1)} %copy-done.17) | copy-start | bytes 2654212
  280.9 3.6 copy-start.4
  284.5 1.7 copy-start.11
  287.0 48.1 %copy-start.16 = (f32[1152]{0:T(1024)S(1)}, f32[1152]{0:T(1024)}, u32[]{:S(2)}) copy-start(f32[1152]{0:T(1024)} %param.13) | copy-start | bytes 13828
  287.0 49.3 %copy-start.24 = (bf16[768,768]{1,0:T(8,128)(2,1)S(1)}, bf16[768,768]{1,0:T(8,128)(2,1)}, u32[]{:S(2)}) copy-start(bf16[768,768]{1,0:T(8,128)(2,1)} %copy-done.23) | copy-start | bytes 3538948
  427.9 5.4 %copy-start.13 = (f32[72,1920]{1,0:T(8,128)S(1)}, f32[72,1920]{1,0:T(8,128)}, u32[]{:S(2)}) copy-start(f32[72,1920]{1,0:T(8,128)} %get-tuple-element.135) | copy-start | bytes 1658884
  429.2 4.9 %copy-start.14 = (f32[72,1152]{1,0:T(8,128)S(1)}, f32[72,1152]{1,0:T(8,128)}, u32[]{:S(2)}) copy-start(f32[72,1152]{1,0:T(8,128)} %get-tuple-element.136) | copy-start | bytes 995332
  431.1 3.8 copy-start.7
  434.9 1.8 copy-start.10

commit v4 on v3

--- a/solution.py
+++ b/solution.py
@@ -623,6 +623,216 @@
     return [pltpu.VMEM((4, rows // 2, D), BF), pltpu.VMEM((2, rows, D), BF)]
 
 
+class SquareGather:
+    def __init__(self, wires, out):
+        self.wires, self.out = wires, out
+        half = out.shape[1] // 2
+        self.a, self.b = pl.ds(0, half), pl.ds(half, half)
+        self.own, self.x, self.y, self.z = square()
+
+    def move(self, slot, part, to):
+        return self.wires.start(self.out.at[slot, part], self.out.at[slot, part], {"wsh": to})
+
+    def begin(self):
+        self.xa = self.move(self.own, self.a, self.x)
+        self.yb = self.move(self.own, self.b, self.y)
+        self.xb = self.move(self.own, self.b, self.x)
+        self.ya = self.move(self.own, self.a, self.y)
+
+    def relay(self):
+        self.xa.wait()
+        self.one = self.move(self.x, self.a, self.y)
+        self.yb.wait()
+        self.two = self.move(self.y, self.b, self.x)
+
+    def wait_x(self):
+        self.xb.wait()
+
+    def wait_y(self):
+        self.ya.wait()
+
+    def wait_z(self):
+        self.one.wait()
+        self.two.wait()
+
+
+def feed(link, attended, w_out, tokens, gain, w_half, down, dy):
+    ctx, wsh = link.sizes["ctx"], link.sizes["wsh"]
+    own_rows = tokens.shape[0]
+    plane = dy.shape[0]
+    units = down.shape[0]
+    chunk = D // ctx
+    pick = units // ctx // 2
+
+    def kernel(
+        at_ref, wo_ref, x_ref, g_ref, wh_ref, dw_ref, dy_ref,
+        mid_ref, mg_ref, br_ref, ag_ref, fs_ref, dp_ref, gs_ref, ds_ref,
+        w_both, parts, near, total, near2, total2, n2, hgrad, hidden, gate_g, up_g,
+        down_h, down_pair, down_send, down_got, gate_h, gate_pair, send, recv, local,
+    ):
+        wires = Wires(send, recv)
+        core = lax.axis_index("grp")
+        sibling = {"grp": 1 - core}
+        my_c = lax.axis_index("ctx")
+        own, x, y, z = square()
+        levels = [link.place(("ctx",), offset) for offset in link.offsets(("ctx",))[1:]]
+        greet([{"wsh": x}, {"wsh": y}, sibling] + [where for where, _ in levels])
+
+        def rows_of(slot):
+            return pl.ds(pl.multiple_of(slot * own_rows, 16), own_rows)
+
+        w_copy = pltpu.make_async_copy(wh_ref, w_both.at[core], local)
+        w_copy.start()
+
+        first = SquareScatter(wires, parts, near, total)
+        for slot in (z, x, y, own):
+            parts[slot] = jnp.dot(
+                at_ref[rows_of(slot), :], wo_ref[...], preferred_element_type=F32
+            ).astype(BF)
+            if slot is z:
+                first.send_diagonal()
+            elif slot is x:
+                first.send_x()
+            elif slot is y:
+                first.send_y()
+        w_swap = wires.start(wh_ref, w_both.at[core], sibling)
+        hgrad[...] = dot_general(dy_ref[...], dw_ref[...], 1, 1)
+        first.relay()
+        middle = x_ref[...].astype(F32) + first.result()
+        mid_ref[...] = middle
+        factor = lax.rsqrt(jnp.mean(middle * middle, axis=-1, keepdims=True) + EPSILON)
+        n2[own] = (middle * factor * g_ref[...]).astype(BF)
+        gather = SquareGather(wires, n2)
+        gather.begin()
+        w_copy.wait()
+        w_swap.wait()
+
+        def block(slot):
+            at = rows_of(slot)
+            gate = jnp.dot(n2[slot], w_both[0], preferred_element_type=F32)
+            up = jnp.dot(n2[slot], w_both[1], preferred_element_type=F32)
+            sigmoid = 1.0 / (1.0 + jnp.exp(-gate))
+            silu = gate * sigmoid
+            hidden[at, :] = (silu * up).astype(BF)
+            back = hgrad[at, :]
+            gate_g[at, :] = (back * up * sigmoid * (1.0 + gate * (1.0 - sigmoid))).astype(BF)
+            up_g[at, :] = (back * silu).astype(BF)
+            parts[slot] = (
+                dot_general(gate_g[at, :], w_both[0], 1, 1)
+                + dot_general(up_g[at, :], w_both[1], 1, 1)
+            ).astype(BF)
+
+        second = SquareScatter(wires, parts, near2, total2)
+        block(own)
+        gather.relay()
+        gather.wait_x()
+        block(x)
+        second.send_x()
+        gather.wait_y()
+        block(y)
+        second.send_y()
+        gather.wait_z()
+        block(z)
+        second.send_diagonal()
+
+        strip = dot_general(hidden[...], dy_ref[...], 0, 0).astype(BF)
+        for k in range(ctx):
+            for g in range(2):
+                top = (2 * k + g) * pick
+                down_h[g, k] = strip[top : top + pick, :]
+        down_swap = wires.start(down_h.at[1 - core], down_pair, sibling)
+        second.relay()
+        tokens_all = n2[...].reshape(plane, D)
+        for g, source in enumerate((gate_g, up_g)):
+            strip = dot_general(tokens_all, source[...], 0, 0).astype(BF)
+            for c in range(ctx):
+                gate_h[g, c] = strip[c * chunk : c * chunk + chunk, :]
+        gate_swap = wires.start(gate_h.at[1 - core], gate_pair, sibling)
+        down_swap.wait()
+        down_send[...] = (down_h[core].astype(F32) + down_pair[...].astype(F32)).astype(BF)
+        down_copies = []
+        for where, index in levels:
+            down_copies.append(wires.start(down_send.at[index], down_got.at[my_c], where))
+        down_got[my_c] = down_send[my_c]
+
+        grad = second.result()
+        middle = mid_ref[...]
+        factor = lax.rsqrt(jnp.mean(middle * middle, axis=-1, keepdims=True) + EPSILON)
+        weighted = grad * g_ref[...]
+        inner = jnp.mean(weighted * middle, axis=-1, keepdims=True)
+        middle_grad = (
+            dy_ref[rows_of(own), :].astype(F32)
+            + factor * weighted
+            - middle * (factor * factor * factor) * inner
+        )
+        mg_ref[...] = middle_grad
+        br_ref[own] = middle_grad.astype(BF)
+        branch = SquareGather(wires, br_ref)
+        branch.begin()
+        fs_ref[...] = jnp.sum(grad * middle * factor, axis=0, keepdims=True)
+
+        def outward(slot):
+            ag_ref[rows_of(slot), :] = dot_general(br_ref[slot], wo_ref[...], 1, 1).astype(BF)
+
+        outward(own)
+        gate_swap.wait()
+        for c in range(ctx):
+            gs_ref[c] = (gate_h[core, c].astype(F32) + gate_pair[c].astype(F32)).astype(BF)
+        branch.relay()
+        for slot in range(wsh):
+            at = slice(slot * own_rows, slot * own_rows + own_rows)
+            dp_ref[slot] = jnp.dot(
+                hidden[at, :], dw_ref[...], preferred_element_type=F32
+            ).astype(BF)
+        branch.wait_x()
+        outward(x)
+        branch.wait_y()
+        outward(y)
+        branch.wait_z()
+        outward(z)
+        for copy in down_copies:
+            copy.wait()
+        ds_ref[...] = jnp.sum(down_got[...].astype(F32), axis=0).astype(BF)
+
+    operands = (attended, w_out, tokens, gain, w_half, down, dy)
+    vmem = pl.BlockSpec(memory_space=pltpu.VMEM)
+    return pl.pallas_call(
+        kernel,
+        name="feed",
+        in_specs=[vmem] * len(operands),
+        out_specs=[vmem] * 8,
+        out_shape=[
+            jax.ShapeDtypeStruct((own_rows, D), F32),
+            jax.ShapeDtypeStruct((own_rows, D), F32),
+            jax.ShapeDtypeStruct((wsh, own_rows, D), BF),
+            jax.ShapeDtypeStruct((plane, 384), BF),
+            jax.ShapeDtypeStruct((1, D), F32),
+            jax.ShapeDtypeStruct((wsh, own_rows, D), BF),
+            jax.ShapeDtypeStruct((ctx, chunk, units), BF),
+            jax.ShapeDtypeStruct((pick, D), BF),
+        ],
+        scratch_shapes=[
+            pltpu.VMEM((2, D, units), BF),
+            pltpu.VMEM((4, own_rows, D), BF),
+            *square_scratch(own_rows),
+            *square_scratch(own_rows),
+            pltpu.VMEM((4, own_rows, D), BF),
+            pltpu.VMEM((plane, units), F32),
+            *[pltpu.VMEM((plane, units), BF)] * 3,
+            pltpu.VMEM((2, ctx, pick, D), BF),
+            *[pltpu.VMEM((ctx, pick, D), BF)] * 3,
+            pltpu.VMEM((2, ctx, chunk, units), BF),
+            pltpu.VMEM((ctx, chunk, units), BF),
+            pltpu.SemaphoreType.DMA((ctx + 28,)),
+            pltpu.SemaphoreType.DMA((ctx + 28,)),
+            pltpu.SemaphoreType.DMA,
+        ],
+        compiler_params=pltpu.CompilerParams(
+            collective_id=3, has_side_effects=True, vmem_limit_bytes=VMEM_LIMIT
+        ),
+    )(*operands)
+
+
 def finish(
     link, q_grad, kv_grad, weight, cos, sin, normed, tokens, gain, middle_grad, gate_got, down_got,
     attended, branch, feed_sum, down_part, middle,
@@ -972,13 +1182,6 @@
     return lax.rsqrt(jnp.mean(values * values, axis=-1, keepdims=True) + EPSILON)
 
 
-def norm_back(grad_normed, inputs, factor, gain):
-    weighted = grad_normed * gain
-    inner_mean = jnp.mean(weighted * inputs, axis=-1, keepdims=True)
-    input_part = factor * weighted - inputs * (factor * factor * factor) * inner_mean
-    return (input_part, jnp.sum(grad_normed * inputs * factor, axis=0))
-
-
 def rope_tables(positions):
     frequency = jnp.exp(jnp.arange(32, dtype=F32) * (-math.log(10000.0) / 32))
     angles = positions.astype(F32)[:, None] * jnp.tile(frequency, 4)[None, :]
@@ -1048,77 +1251,24 @@
         attended, attended_wide, lse = attend_forward(queries, kv_all, q_pos, q_seg, k_pos, k_seg)
 
         w_out = spread_rows(attend_out, odd)
-        out_part = jnp.dot(attended, w_out, preferred_element_type=F32).astype(BF)
-        out_parts, w_both = link.run(
-            "scatter_out",
-            3,
-            [
-                link.swap(out_part.reshape(wsh, own, D), ("wsh",)),
-                link.gather(w_half, ("grp",)),
-            ],
-        )
-        w_gate, w_up = w_both[0], w_both[1]
-        middle = inputs + jnp.sum(out_parts.astype(F32), axis=0)
-        factor_two = rms_factor(middle)
-        normed_two = (middle * factor_two * feed_gain).astype(BF)
-        (normed_two_all,) = link.run("gather_two", 4, [link.gather(normed_two, ("wsh",))])
-        normed_two_all = normed_two_all.reshape(plane, D)
-
-        gate_part = jnp.dot(normed_two_all, w_gate, preferred_element_type=F32)
-        up_part = jnp.dot(normed_two_all, w_up, preferred_element_type=F32)
-        hidden_grad = dot_general(dy_all, down_weight, 1, 1)
-        sigmoid_gate = jax.nn.sigmoid(gate_part)
-        silu_gate = gate_part * sigmoid_gate
-        hidden = (silu_gate * up_part).astype(BF)
-        gate_grad = (
-            hidden_grad * up_part * sigmoid_gate * (1.0 + gate_part * (1.0 - sigmoid_gate))
-        ).astype(BF)
-        up_grad = (hidden_grad * silu_gate).astype(BF)
-        down_part = jnp.dot(hidden, down_weight, preferred_element_type=F32).astype(BF)
-        two_part = (dot_general(gate_grad, w_gate, 1, 1) + dot_general(up_grad, w_up, 1, 1)).astype(
-            BF
-        )
-        down_grad = dot_general(hidden, dy_all, 0, 0).astype(BF)
-        gate_w_grad = dot_general(normed_two_all, gate_grad, 0, 0).astype(BF)
-        up_w_grad = dot_general(normed_two_all, up_grad, 0, 0).astype(BF)
-        ffn_rows = FF // shards // 2
-        down_halves = down_grad.reshape(ctx, 2, ffn_rows, D).transpose(1, 0, 2, 3)
-        gate_halves = jnp.stack([gate_w_grad, up_w_grad]).reshape(2, ctx, D // ctx, FF // wsh)
-        two_parts, down_pair, gate_pair = link.run(
-            "scatter_feed",
-            5,
-            [
-                link.swap(two_part.reshape(wsh, own, D), ("wsh",)),
-                link.swap(down_halves, ("grp",)),
-                link.swap(gate_halves, ("grp",)),
-            ],
-        )
-        normed_two_grad = jnp.sum(two_parts.astype(F32), axis=0)
-        middle_part, feed_gain_grad = norm_back(normed_two_grad, middle, factor_two, feed_gain)
-        middle_grad = upstream.astype(F32) + middle_part
-        branch_grad = middle_grad.astype(BF)
-        down_send = (down_pair[0].astype(F32) + down_pair[1].astype(F32)).astype(BF)
-        gate_send = (gate_pair[0].astype(F32) + gate_pair[1].astype(F32)).astype(BF)
-
-        branch_all, down_got = link.run(
-            "gather_branch",
-            6,
-            [
-                link.gather(branch_grad, ("wsh",)),
-                link.swap(down_send, ("ctx",)),
-            ],
-        )
-        branch_all = branch_all.reshape(plane, D)
-        attended_grad = dot_general(branch_all, w_out, 1, 1).astype(BF)
-        down_sum = jnp.sum(down_got.astype(F32), axis=0).astype(BF)
+        (
+            middle,
+            middle_grad,
+            branch_all,
+            attended_grad,
+            feed_sum,
+            down_part,
+            gate_send,
+            down_sum,
+        ) = feed(link, attended, w_out, tokens, feed_gain[None, :], w_half, down_weight, dy_all)
         q_grad, kv_grad, gate_got, down_got = attend_backward(
             link, queries, kv_all, q_pos, q_seg, k_pos, k_seg, lse, attended_wide, attended_grad,
             gate_send, down_sum,
         )
         (activations, input_grad, qkv_out, out_out, gate_out, down_out, gain_out) = finish(
             link, q_grad, kv_grad.reshape(ctx, plane, 256), w_qkv, cos, sin, normed_all, tokens,
-            attend_gain[None, :], middle_grad, gate_got, down_got, attended, branch_all,
-            feed_gain_grad[None, :], down_part.reshape(wsh, own, D), middle,
+            attend_gain[None, :], middle_grad, gate_got, down_got, attended,
+            branch_all.reshape(plane, D), feed_sum, down_part, middle,
         )
         width = D // shards
         return (

time: 445 us -> 380 us (0.85)
  matrix products: 26 us -> 0 us
  Pallas kernels: 361 us -> 343 us
  other arithmetic: 23.6 us -> 12.3 us
  local copies, waits for them, and re-layouts: 26.1 us -> 16.7 us
    pallas_call x6 -> x2, Pallas kernels: 174 us -> 84.5 us  [run(): pl.pallas_call(kernel, name=name, out_shape=[jax.ShapeDtypeStruct(op[4],...]
    pallas_call x0 -> x1, Pallas kernels: none -> 70.8 us  [feed(): pl.pallas_call(kernel, name='feed', in_specs=[vmem] * len(operands), out_...]
    dot_general x11 -> x0, matrix products: 26 us -> none  [the longest x7 15.1 us: dot_general(): lax.dot_general(a, b, (((ca,), (cb,)), ((), ())), preferred_element_type=...]
    convert_element_type x4 -> x0, other arithmetic: 5.06 us -> none  [the longest x1 1.67 us: local(): gate_send = (gate_pair[0].astype(F32) + gate_pair[1].astype(F32)).astype(BF)]
    reduce_sum x4 -> x0, other arithmetic: 4.93 us -> none  [the longest x1 1.88 us: local(): normed_two_grad = jnp.sum(two_parts.astype(F32), axis=0)]
    unnamed x67 -> x37, local copies, waits for them, and re-layouts: 12.2 us -> 10.1 us
where the time goes in v4:
time: 380 us; the launch traced here: 373 us
  Pallas kernels  343 us (90%)
  local copies, waits for them, and re-layouts  16.7 us (4%)
  other arithmetic  12.3 us (3%)
    pallas_call x1, Pallas kernels, finish(): pl.pallas_call(kernel, name='finish', in_specs=[vmem] * len(operands), ou...  88.9 us
    pallas_call x2, Pallas kernels, run(): pl.pallas_call(kernel, name=name, out_shape=[jax.ShapeDtypeStruct(op[4],...  84.5 us
    pallas_call x1, Pallas kernels, feed(): pl.pallas_call(kernel, name='feed', in_specs=[vmem] * len(operands), out_...  70.8 us
    pallas_call x1, Pallas kernels, attend_backward(): pl.pallas_call(kernel, name='attend_backward', grid=(steps,), in_specs=[p...  48.7 us
    pallas_call x1, Pallas kernels, attend_forward(): pl.pallas_call(kernel, name='attend_forward', grid=(rows // TQ,), in_spec...  44.5 us
    unnamed x37, local copies, waits for them, and re-layouts  10.1 us

profile of v4, /device:TPU:0, one launch (start us, length us, event | category | flops | bytes accessed | tf_op | source)
XLA Modules:
  0.0 373.1 jit_solution(17421462872511849743)
XLA Ops:
  0.6 0.0 copy-start
  0.6 1.3 fusion.2
  1.9 2.0 fusion.4.refs_0_
  3.9 0.0 copy-done
  3.9 0.3 fusion.9
  4.2 0.1 fusion.10
  4.4 0.4 concatenate.23
  4.8 0.1 fusion.8
  4.9 0.2 concatenate.22
  5.1 0.4 concatenate.21
  5.5 0.2 concatenate.20
  5.8 0.0 copy-start.8
  5.8 0.0 copy-start.9
  5.8 1.3 pad_maximum_fusion.refs_1_
  7.1 0.0 copy-done.8
  7.1 0.0 copy-done.9
  7.2 0.6 pad_bitcast_fusion.refs_2_
  7.8 40.5 %gather_one.1 = (bf16[4,192,1152]{2,1,0:T(8,128)(2,1)}, bf16[4,288,640]{2,1,0:T(8,128)(2,1)}, s32[4,8,128]{2,1,0:T(8,128)}) custom-call(bf16[192,1152]{1,0:T(8,128)(2,1)} %fusion.4.refs_0_, bf16[4,288,640]{2,1,0:T(8,128)(2,1)} %pad_maximum_fusion.refs_1_, s32[8,128]{1,0:T(8,128)} %pad_bitcast_fusion.refs_2_), custom_call_target="tpu_custom_call" | custom-call | tf_op jit(solution)/shard_map/gather_one/pallas_call | solution.py:161
  48.3 0.1 mul.68
  48.4 0.7 copy.27
  49.1 0.1 reshape.350
  49.2 2.5 fusion.5
  51.7 5.3 %project.1 = (bf16[768,384]{1,0:T(8,128)(2,1)}, bf16[768,256]{1,0:T(8,128)(2,1)}) custom-call(bf16[768,1152]{1,0:T(8,128)(2,1)} %bitcast.26, bf16[1152,640]{1,0:T(8,128)(2,1)} %bitcast.30, f32[768,128]{1,0:T(8,128)} %get-tuple-element.111.c_ref, f32[768,128]{1,0:T(8,128)} %get-tuple-element.110.s_ref), custom_call_target="tpu_custom_call" | custom-call | tf_op jit(solution)/shard_map/project/pallas_call | solution.py:260
  56.9 44.1 %gather_keys.1 = (bf16[4,768,256]{2,1,0:T(8,128)(2,1)}, s32[4,4,8,128]{3,2,1,0:T(8,128)}, bf16[4,192,1152]{2,1,0:T(8,128)(2,1)}, bf16[4,288,768]{2,1,0:T(8,128)(2,1)}) custom-call(bf16[768,256]{1,0:T(8,128)(2,1)} %get-tuple-element.43.refs_0_, s32[4,8,128]{2,1,0:T(8,128)} %get-tuple-element.41.refs_1_, bf16[192,1152]{1,0:T(8,128)(2,1)} %refs_2_.1, ...), custom_call_target="tpu_custom_call" | custom-call | tf_op jit(solution)/shard_map/gather_keys/pallas_call | solution.py:161
  101.0 0.1 reshape.352
  101.1 0.6 and_select_fusion
  101.7 0.6 and_select_fusion.1.qp_ref
  102.3 0.9 copy.26
  103.2 1.4 reshape.359
  104.6 3.0 add_select_fusion
  107.6 44.5 %attend_forward.1 = (bf16[768,384]{1,0:T(8,128)(2,1)}, f32[768,384]{1,0:T(8,128)}, f32[8,768]{1,0:T(8,128)}) custom-call(bf16[768,384]{1,0:T(8,128)(2,1)} %get-tuple-element.42.q_ref, bf16[3072,256]{1,0:T(8,128)(2,1)} %bitcast.28, s32[1,768]{1,0:T(1,128)} %and_select_fusion.1.qp_ref, s32[1,768]{1,0:T(1,128)} %get-tuple-element.70.qs_ref, ...), custom_call_target="tpu_custom_call" | custom-call | tf_op jit(solution)/shard_map/attend_forward/pallas_call | solution.py:342
  152.3 0.0 copy-start.7
  152.4 1.0 broadcast_select_fusion.wo_ref
  153.4 0.6 broadcast_in_dim.32.g_ref
  154.0 70.8 %feed.1 = (f32[192,1152]{1,0:T(8,128)}, f32[192,1152]{1,0:T(8,128)}, bf16[4,192,1152]{2,1,0:T(8,128)(2,1)}, bf16[768,384]{1,0:T(8,128)(2,1)}, f32[1,1152]{1,0:T(...) custom-call(bf16[768,384]{1,0:T(8,128)(2,1)} %get-tuple-element.48.at_ref, ...), custom_call_target="tpu_custom_call" | custom-call | tf_op jit(solution)/shard_map/feed/pallas_call | solution.py:799
  224.8 0.0 copy-start.6
  224.8 48.7 %attend_backward.1 = (bf16[768,384]{1,0:T(8,128)(2,1)}, bf16[3072,256]{1,0:T(8,128)(2,1)}, bf16[4,288,768]{2,1,0:T(8,128)(2,1)}, bf16[96,1152]{1,0:T(8,128)(2,1)}) custom-call(bf16[768,384]{1,0:T(8,128)(2,1)} %get-tuple-element.42.q_ref, bf16[3072,256]{1,0:T(8,128)(2,1)} %bitcast.29, s32[1,768]{1,0:T(1,128)} %and_select_fusion.1.qp_ref, ...), custom_call_target="tpu_custom_call" | custom-call | tf_op jit(solution)/shard_map/attend_backward/pallas_call | solution.py:494
  273.5 0.6 broadcast_in_dim.33.g_ref
  274.1 88.9 %finish.1 = (bf16[192,1152]{1,0:T(8,128)(2,1)}, f32[192,1152]{1,0:T(8,128)}, f32[72,1920]{1,0:T(8,128)}, f32[72,1152]{1,0:T(8,128)}, f32[72,6144]{1,0:T(8,128)}, /*index=5*/f32[192,1152]{1,0:T(8,128)}, f32[8,128]{1,0:T(8,128)}) custom-call(bf16[768,384]{1,0:T(8,128)(2,1)} %get-tuple-element.54.q_ref, bf16[4,768,256]{2,1,0:T(8,128)(2,1)} %bitcast.35, ...), custom_call_target="tpu_custom_call" | custom-call | tf_op jit(solution)/shard_map/finish/pallas_call | solution.py:1134
  363.1 1.3 slice_bitcast_fusion
  364.3 1.8 copy.46
  366.1 2.3 copy.47
  368.4 0.8 copy.48
  369.2 0.0 copy-done.5
  369.2 0.7 copy.49
  370.0 1.2 copy.50
  371.2 0.6 copy-done.3
  371.8 0.9 copy.51
  (29 shorter events, 0.3 us)
Async XLA Ops:
  0.6 3.2 copy-start
  5.8 1.4 copy-start.8
  5.8 1.3 copy-start.9
  107.6 44.5 %copy-start.1 = (bf16[288,1152]{1,0:T(8,128)(2,1)S(1)}, bf16[288,1152]{1,0:T(8,128)(2,1)}, u32[]{:S(2)}) copy-start(bf16[288,1152]{1,0:T(8,128)(2,1)} %param.15) | copy-start | bytes 1990660
  152.3 1.1 copy-start.7
  224.8 48.7 %copy-start.6 = (f32[1152]{0:T(1024)S(1)}, f32[1152]{0:T(1024)}, u32[]{:S(2)}) copy-start(f32[1152]{0:T(1024)} %param.13) | copy-start | bytes 13828
  363.0 5.4 %copy-start.4 = (f32[72,1920]{1,0:T(8,128)S(1)}, f32[72,1920]{1,0:T(8,128)}, u32[]{:S(2)}) copy-start(f32[72,1920]{1,0:T(8,128)} %get-tuple-element.126) | copy-start | bytes 1658884
  366.1 3.1 copy-start.5
  366.1 3.8 %copy-start.2 = (f32[72,6144]{1,0:T(8,128)S(1)}, f32[72,6144]{1,0:T(8,128)}, u32[]{:S(2)}) copy-start(f32[72,6144]{1,0:T(8,128)} %get-tuple-element.128) | copy-start | bytes 5308420
  370.0 1.8 copy-start.3

commit v5 on v4

--- a/solution.py
+++ b/solution.py
@@ -44,137 +44,6 @@
     def offsets(self, axes):
         return list(itertools.product(*[range(self.sizes[axis]) for axis in axes]))
 
-    def gather(self, x, axes):
-        count = math.prod(self.sizes[axis] for axis in axes)
-        return ("peer", x, axes, lambda ref, p: ref, (count,) + x.shape, x.shape)
-
-    def swap(self, x, axes):
-        return ("peer", x, axes, lambda ref, p: ref.at[p], x.shape, x.shape[1:])
-
-    def columns(self, x, axes, start, width):
-        count = math.prod(self.sizes[axis] for axis in axes)
-        source = lambda ref, p: ref.at[
-            :, pl.ds(pl.multiple_of(lax.axis_index("grp") * start + p * width, 128), width)
-        ]
-        return ("peer", x, axes, source, (count, x.shape[0], width), (x.shape[0], width))
-
-    def turn_over(self, x):
-        return ("owner", x, None, None, x.shape, x.shape)
-
-    def run(self, name, number, ops):
-        ctx, wsh = self.sizes["ctx"], self.sizes["wsh"]
-        total = 0
-        for kind, x, axes, *_ in ops:
-            total += 1 if kind == "owner" else math.prod(self.sizes[a] for a in axes)
-        peers = {}
-        for kind, x, axes, *_ in ops:
-            for offset in self.offsets(axes if kind == "peer" else ("ctx", "wsh")):
-                axes_of = axes if kind == "peer" else ("ctx", "wsh")
-                key = tuple(sorted((a, o) for a, o in zip(axes_of, offset) if o))
-                if key:
-                    peers[key] = (axes_of, offset)
-        count = len(ops)
-
-        def kernel(*refs):
-            ins, outs = refs[:count], refs[count : 2 * count]
-            bounce = refs[2 * count : 3 * count]
-            send, recv, near = refs[3 * count :]
-            barrier = pltpu.get_barrier_semaphore()
-            for axes, offset in peers.values():
-                where, _ = self.place(axes, offset)
-                pl.semaphore_signal(barrier, 1, device_id=where, device_id_type=MESH)
-            pl.semaphore_wait(barrier, len(peers))
-            first, second, remote, late = [], [], [], []
-            slot = 0
-            for op, (kind, x, axes, source, _, _) in enumerate(ops):
-                if kind == "peer":
-                    none = tuple(0 for _ in axes)
-                    _, me = self.place(axes, none)
-                    for offset in self.offsets(axes):
-                        where, index = self.place(axes, offset)
-                        if any(offset):
-                            copy = pltpu.make_async_remote_copy(
-                                source(ins[op], index),
-                                outs[op].at[me],
-                                send.at[slot],
-                                recv.at[slot],
-                                device_id=where,
-                                device_id_type=MESH,
-                            )
-                            copy.start()
-                            remote.append(copy)
-                        else:
-                            copy = pltpu.make_async_copy(
-                                source(ins[op], me), bounce[op], near.at[op]
-                            )
-                            copy.start()
-                            first.append(copy)
-                            second.append(
-                                pltpu.make_async_copy(bounce[op], outs[op].at[me], near.at[op])
-                            )
-                        slot += 1
-                else:
-                    my_c, my_w = lax.axis_index("ctx"), lax.axis_index("wsh")
-                    shard = my_w * ctx + my_c
-                    to_c, to_w = shard // wsh, lax.rem(shard, wsh)
-                    own = jnp.logical_and(to_c == my_c, to_w == my_w)
-                    copy = pltpu.make_async_remote_copy(
-                        ins[op],
-                        outs[op],
-                        send.at[slot],
-                        recv.at[slot],
-                        device_id={"ctx": to_c, "wsh": to_w},
-                        device_id_type=MESH,
-                    )
-                    inward = pltpu.make_async_copy(ins[op], bounce[op], near.at[op])
-                    outward = pltpu.make_async_copy(bounce[op], outs[op], near.at[op])
-
-                    @pl.when(jnp.logical_not(own))
-                    def _():
-                        copy.start()
-
-                    late.append((own, copy, inward, outward))
-                    slot += 1
-            for one, two in zip(first, second):
-                one.wait()
-                two.start()
-            for own, copy, inward, outward in late:
-
-                @pl.when(own)
-                def _():
-                    inward.start()
-                    inward.wait()
-                    outward.start()
-                    outward.wait()
-
-            for copy in second:
-                copy.wait()
-            for own, copy, inward, outward in late:
-
-                @pl.when(jnp.logical_not(own))
-                def _():
-                    copy.wait()
-
-            for copy in remote:
-                copy.wait()
-
-        return pl.pallas_call(
-            kernel,
-            name=name,
-            out_shape=[jax.ShapeDtypeStruct(op[4], op[1].dtype) for op in ops],
-            in_specs=[pl.BlockSpec(memory_space=pl.ANY)] * count,
-            out_specs=[pl.BlockSpec(memory_space=pl.ANY)] * count,
-            scratch_shapes=[pltpu.VMEM(op[5], op[1].dtype) for op in ops]
-            + [
-                pltpu.SemaphoreType.DMA((total,)),
-                pltpu.SemaphoreType.DMA((total,)),
-                pltpu.SemaphoreType.DMA((count,)),
-            ],
-            compiler_params=pltpu.CompilerParams(
-                collective_id=number, has_side_effects=True, vmem_limit_bytes=VMEM_LIMIT
-            ),
-        )(*[op[1] for op in ops])
-
 
 def head_plan(w):
     pair, odd = w // 2, w % 2
@@ -187,22 +56,6 @@
         f_kv, h_kv = 3 * pair, 3 * pair + 1
     q_order = [f_heads[0], h_heads[0], f_heads[1], h_heads[1], f_heads[2], None]
     return q_order, [f_kv, h_kv]
-
-
-def qkv_columns(weight):
-    blank = jnp.zeros((weight.shape[0], HEAD_DIM), weight.dtype)
-    parts = []
-    for w in range(4):
-        q_order, kv_order = head_plan(w)
-        pieces = [
-            blank if h is None else weight[:, h * HEAD_DIM : (h + 1) * HEAD_DIM] for h in q_order
-        ]
-        for base in (QW, QW + KW):
-            pieces += [
-                weight[:, base + h * HEAD_DIM : base + (h + 1) * HEAD_DIM] for h in kv_order
-            ]
-        parts.append(jnp.concatenate(pieces, axis=1))
-    return jnp.stack(parts)
 
 
 def qkv_restore(parts):
@@ -243,42 +96,6 @@
     return x * cos + swapped * sin
 
 
-def project(normed, weight, cos, sin):
-    rows = normed.shape[0]
-    tile = 256
-
-    def kernel(n_ref, w_ref, c_ref, s_ref, q_ref, kv_ref):
-        full = jnp.dot(n_ref[...], w_ref[...], preferred_element_type=F32)
-        cos_t, sin_t = c_ref[...], s_ref[...]
-        low = lax.rem(lax.broadcasted_iota(jnp.int32, (tile, 128), 1), 64) < 32
-        for b in range(3):
-            block = turn(full[:, 128 * b : 128 * b + 128], cos_t, sin_t, low)
-            q_ref[:, 128 * b : 128 * b + 128] = (block.astype(BF).astype(F32) * 0.125).astype(BF)
-        kv_ref[:, :128] = turn(full[:, 384:512], cos_t, sin_t, low).astype(BF)
-        kv_ref[:, 128:] = full[:, 512:].astype(BF)
-
-    return pl.pallas_call(
-        kernel,
-        name="project",
-        grid=(rows // tile,),
-        in_specs=[
-            pl.BlockSpec((tile, D), lambda i: (i, 0)),
-            pl.BlockSpec((D, 640), lambda i: (0, 0)),
-            pl.BlockSpec((tile, 128), lambda i: (i, 0)),
-            pl.BlockSpec((tile, 128), lambda i: (i, 0)),
-        ],
-        out_specs=[
-            pl.BlockSpec((tile, 384), lambda i: (i, 0)),
-            pl.BlockSpec((tile, 256), lambda i: (i, 0)),
-        ],
-        out_shape=[
-            jax.ShapeDtypeStruct((rows, 384), BF),
-            jax.ShapeDtypeStruct((rows, 256), BF),
-        ],
-        compiler_params=pltpu.CompilerParams(vmem_limit_bytes=VMEM_LIMIT),
-    )(normed, weight, cos, sin)
-
-
 TQ = 256
 TK = 512
 
@@ -289,18 +106,48 @@
 
 
 def visible(kp_ref, ks_ref, qp_ref, qs_ref, start):
-    key_pos = kp_ref[pl.ds(start, TK), :]
-    key_seg = ks_ref[pl.ds(start, TK), :]
+    key_pos = jnp.tile(kp_ref[pl.ds(start, TK), :], (1, TQ // 128))
+    key_seg = jnp.tile(ks_ref[pl.ds(start, TK), :], (1, TQ // 128))
     return (key_pos <= qp_ref[...]) & ((key_seg == 0) | (key_seg == qs_ref[...]))
 
 
 HEAD_SLOTS = [(0, 0), (0, 1), (1, 0), (1, 1), (2, 0)]
 
 
-def attend_forward(q, kv, q_pos, q_seg, k_pos, k_seg):
+def attend_forward(link, q, kv, q_pos, q_seg, k_pos, k_seg, gate_up):
     rows, keys = q.shape[0], kv.shape[0]
-
-    def kernel(q_ref, kv_ref, qp_ref, qs_ref, kp_ref, ks_ref, a_ref, o_ref, lse_ref, acc, top, tot):
+    steps = rows // TQ
+    wsh = link.sizes["wsh"]
+    units = FF // wsh
+    peers = link.offsets(("wsh",))
+
+    def kernel(
+        q_ref, kv_ref, qp_ref, qs_ref, kp_ref, ks_ref, gu_ref,
+        a_ref, o_ref, lse_ref, wh_ref,
+        acc, top, tot, bounce, send, recv, near,
+    ):
+        def columns(p):
+            left = lax.axis_index("grp") * FF + p * units
+            return gu_ref.at[:, pl.ds(pl.multiple_of(left, 128), units)]
+
+        wires = Wires(send, recv)
+        _, me = link.place(("wsh",), peers[0])
+        copies = []
+        for offset in peers[1:]:
+            where, index = link.place(("wsh",), offset)
+            copies.append(wires.copy(columns(index), wh_ref.at[me], where))
+        inward = pltpu.make_async_copy(columns(me), bounce, near)
+        outward = pltpu.make_async_copy(bounce, wh_ref.at[me], near)
+
+        @pl.when(pl.program_id(0) == 0)
+        def _():
+            greet([link.place(("wsh",), offset)[0] for offset in peers[1:]])
+            for copy in copies:
+                copy.start()
+            inward.start()
+            inward.wait()
+            outward.start()
+
         acc[...] = jnp.zeros_like(acc)
         top[...] = jnp.full_like(top, -1e30)
         tot[...] = jnp.zeros_like(tot)
@@ -339,35 +186,50 @@
             o_ref[:, 128 * b : 128 * b + 128] = block
             a_ref[:, 128 * b : 128 * b + 128] = block.astype(BF)
 
+        @pl.when(pl.program_id(0) == steps - 1)
+        def _():
+            outward.wait()
+            for copy in copies:
+                copy.wait()
+
     return pl.pallas_call(
         kernel,
         name="attend_forward",
-        grid=(rows // TQ,),
+        grid=(steps,),
         in_specs=[
             pl.BlockSpec((TQ, 384), lambda i: (i, 0)),
             pl.BlockSpec((keys, 256), lambda i: (0, 0)),
             pl.BlockSpec((1, TQ), lambda i: (0, i)),
             pl.BlockSpec((1, TQ), lambda i: (0, i)),
-            pl.BlockSpec((keys, 1), lambda i: (0, 0)),
-            pl.BlockSpec((keys, 1), lambda i: (0, 0)),
+            pl.BlockSpec((keys, 128), lambda i: (0, 0)),
+            pl.BlockSpec((keys, 128), lambda i: (0, 0)),
+            pl.BlockSpec(memory_space=pl.ANY),
         ],
         out_specs=[
             pl.BlockSpec((TQ, 384), lambda i: (i, 0)),
             pl.BlockSpec((TQ, 384), lambda i: (i, 0)),
             pl.BlockSpec((8, TQ), lambda i: (0, i)),
+            pl.BlockSpec(memory_space=pl.ANY),
         ],
         out_shape=[
             jax.ShapeDtypeStruct((rows, 384), BF),
             jax.ShapeDtypeStruct((rows, 384), F32),
             jax.ShapeDtypeStruct((8, rows), F32),
+            jax.ShapeDtypeStruct((wsh, gate_up.shape[0], units), BF),
         ],
         scratch_shapes=[
             pltpu.VMEM((5, 128, TQ), F32),
             pltpu.VMEM((8, TQ), F32),
             pltpu.VMEM((8, TQ), F32),
+            pltpu.VMEM((gate_up.shape[0], units), BF),
+            pltpu.SemaphoreType.DMA((wsh,)),
+            pltpu.SemaphoreType.DMA((wsh,)),
+            pltpu.SemaphoreType.DMA,
         ],
-        compiler_params=pltpu.CompilerParams(vmem_limit_bytes=VMEM_LIMIT),
-    )(q, kv, q_pos, q_seg, k_pos, k_seg)
+        compiler_params=pltpu.CompilerParams(
+            collective_id=2, has_side_effects=True, vmem_limit_bytes=VMEM_LIMIT
+        ),
+    )(q, kv, q_pos, q_seg, k_pos, k_seg, gate_up)
 
 
 def owner_of(link):
@@ -500,8 +362,8 @@
             pl.BlockSpec((keys, 256), lambda i: (0, 0)),
             pl.BlockSpec((1, TQ), lambda i: (0, i)),
             pl.BlockSpec((1, TQ), lambda i: (0, i)),
-            pl.BlockSpec((keys, 1), lambda i: (0, 0)),
-            pl.BlockSpec((keys, 1), lambda i: (0, 0)),
+            pl.BlockSpec((keys, 128), lambda i: (0, 0)),
+            pl.BlockSpec((keys, 128), lambda i: (0, 0)),
             pl.BlockSpec((8, TQ), lambda i: (0, i)),
             pl.BlockSpec((TQ, 384), lambda i: (i, 0)),
             pl.BlockSpec((TQ, 384), lambda i: (i, 0)),
@@ -829,6 +691,165 @@
         ],
         compiler_params=pltpu.CompilerParams(
             collective_id=3, has_side_effects=True, vmem_limit_bytes=VMEM_LIMIT
+        ),
+    )(*operands)
+
+
+def head(link, tokens, gain, weight, marks, upstream):
+    ctx, wsh = link.sizes["ctx"], link.sizes["wsh"]
+    own_rows = tokens.shape[0]
+    plane, group = own_rows * wsh, own_rows * wsh * ctx
+    half = weight.shape[0] // 2
+
+    def kernel(
+        x_ref, g_ref, w_ref, m_ref, up_ref,
+        q_ref, kv_ref, n_ref, wq_ref, kpos_ref, kseg_ref, q_marks, dy_ref, c_ref, s_ref,
+        cols, marks_all, send, recv,
+    ):
+        wires = Wires(send, recv)
+        core = lax.axis_index("grp")
+        sibling = {"grp": 1 - core}
+        my_c = lax.axis_index("ctx")
+        own, x, y, z = square()
+        levels = [link.place(("ctx",), offset) for offset in link.offsets(("ctx",))[1:]]
+        greet(
+            [{"wsh": x}, {"wsh": y}, {"wsh": z}, sibling] + [where for where, _ in levels]
+        )
+        mark_copies = []
+        for p in (x, y, z):
+            mark_copies.append(
+                wires.start(m_ref, marks_all.at[my_c, own], {"wsh": p})
+            )
+        marks_all[my_c, own] = m_ref[...]
+        side = pl.ds(pl.multiple_of(core * half, 16), half)
+
+        for w in range(wsh):
+            q_order, kv_order = head_plan(w)
+            slots = [h for h in q_order] + [HEADS + h for h in kv_order]
+            slots += [HEADS + KV_HEADS + h for h in kv_order]
+            blank = jnp.zeros((w_ref.shape[0], HEAD_DIM), BF)
+            for pair in range(5):
+                two = [
+                    blank if h is None else w_ref[:, h * HEAD_DIM : h * HEAD_DIM + HEAD_DIM]
+                    for h in slots[2 * pair : 2 * pair + 2]
+                ]
+                cols[w, :, 128 * pair : 128 * pair + 128] = jnp.concatenate(two, axis=1)
+        w_copies = []
+        for p in (x, y, z):
+            w_copies.append(
+                wires.start(cols.at[p, side], wq_ref.at[own, side], {"wsh": p})
+            )
+        tokens_in = x_ref[...].astype(F32)
+        factor = lax.rsqrt(jnp.mean(tokens_in * tokens_in, axis=-1, keepdims=True) + EPSILON)
+        n_ref[own] = (tokens_in * factor * g_ref[...]).astype(BF)
+        gather = SquareGather(wires, n_ref)
+        gather.begin()
+        wq_ref[own] = cols[own]
+        dy_ref[own] = up_ref[...]
+
+        for copy in mark_copies:
+            copy.wait()
+        level_copies = []
+        for where, _ in levels:
+            level_copies.append(wires.start(marks_all.at[my_c], marks_all.at[my_c], where))
+        lane = lax.broadcasted_iota(jnp.int32, (1, 128), 1)
+        power = lax.rem(lane, 32).astype(F32) * (-math.log(10000.0) / 32)
+        frequency = jnp.exp(power)
+        sign = jnp.where(lax.rem(lane, 64) < 32, -1.0, 1.0)
+
+        def upright(row):
+            return jnp.broadcast_to(row, (128, row.shape[1])).T
+
+        for w in range(wsh):
+            at = slice(w * own_rows, w * own_rows + own_rows)
+            angles = upright(marks_all[my_c, w, 0:1, :])[:own_rows] * frequency
+            c_ref[at, :] = jnp.cos(angles)
+            s_ref[at, :] = jnp.sin(angles) * sign
+        gather.relay()
+        forward = []
+        for p, copy in zip((x, y, z), w_copies):
+            copy.wait()
+            forward.append(wires.start(wq_ref.at[p, side], wq_ref.at[p, side], sibling))
+        dy_gather = SquareGather(wires, dy_ref)
+        dy_gather.begin()
+        for copy in forward:
+            copy.wait()
+
+        low = lax.rem(lax.broadcasted_iota(jnp.int32, (own_rows, 128), 1), 64) < 32
+        kv_copies = []
+
+        def block(slot):
+            at = pl.ds(pl.multiple_of(slot * own_rows, 16), own_rows)
+            full = jnp.dot(
+                n_ref[slot], wq_ref[...].reshape(D, 640), preferred_element_type=F32
+            )
+            cos_t, sin_t = c_ref[at, :], s_ref[at, :]
+            for b in range(3):
+                turned = turn(full[:, 128 * b : 128 * b + 128], cos_t, sin_t, low)
+                q_ref[at, 128 * b : 128 * b + 128] = (
+                    turned.astype(BF).astype(F32) * 0.125
+                ).astype(BF)
+            kv_ref[my_c, at, :128] = turn(full[:, 384:512], cos_t, sin_t, low).astype(BF)
+            kv_ref[my_c, at, 128:] = full[:, 512:].astype(BF)
+            for where, _ in levels:
+                kv_copies.append(
+                    wires.start(kv_ref.at[my_c, at], kv_ref.at[my_c, at], where)
+                )
+
+        block(own)
+        gather.wait_x()
+        block(x)
+        gather.wait_y()
+        block(y)
+        gather.wait_z()
+        block(z)
+        dy_gather.relay()
+
+        for copy in level_copies:
+            copy.wait()
+        for w in range(wsh):
+            q_marks[:, w * own_rows : w * own_rows + own_rows] = marks_all[my_c, w, :, :own_rows]
+
+        @pl.loop(0, ctx)
+        def _(c):
+            for w in range(wsh):
+                at = pl.ds(pl.multiple_of(c * plane + w * own_rows, 16), own_rows)
+                kpos_ref[at, :] = upright(marks_all[c, w, 0:1, :])[:own_rows]
+                kseg_ref[at, :] = upright(marks_all[c, w, 1:2, :])[:own_rows]
+
+        dy_gather.wait_x()
+        dy_gather.wait_y()
+        dy_gather.wait_z()
+        for copy in kv_copies:
+            copy.wait()
+
+    operands = (tokens, gain, weight, marks, upstream)
+    vmem = pl.BlockSpec(memory_space=pltpu.VMEM)
+    return pl.pallas_call(
+        kernel,
+        name="head",
+        in_specs=[vmem] * len(operands),
+        out_specs=[vmem] * 10,
+        out_shape=[
+            jax.ShapeDtypeStruct((plane, 384), BF),
+            jax.ShapeDtypeStruct((ctx, plane, 256), BF),
+            jax.ShapeDtypeStruct((wsh, own_rows, D), BF),
+            jax.ShapeDtypeStruct((wsh, 2 * half, 640), BF),
+            jax.ShapeDtypeStruct((group, 128), F32),
+            jax.ShapeDtypeStruct((group, 128), F32),
+            jax.ShapeDtypeStruct((8, plane), F32),
+            jax.ShapeDtypeStruct((wsh, own_rows, D), BF),
+            jax.ShapeDtypeStruct((plane, 128), F32),
+            jax.ShapeDtypeStruct((plane, 128), F32),
+        ],
+        scratch_shapes=[
+            pltpu.VMEM((wsh, 2 * half, 640), BF),
+            pltpu.VMEM((ctx, wsh, 8, 256), F32),
+            pltpu.SemaphoreType.DMA((5 * ctx + 24,)),
+            pltpu.SemaphoreType.DMA((5 * ctx + 24,)),
+        ],
+        compiler_params=pltpu.CompilerParams(
+            collective_id=1, has_side_effects=True, vmem_limit_bytes=VMEM_LIMIT
         ),
     )(*operands)
 
@@ -1178,17 +1199,6 @@
     )(*operands)
 
 
-def rms_factor(values):
-    return lax.rsqrt(jnp.mean(values * values, axis=-1, keepdims=True) + EPSILON)
-
-
-def rope_tables(positions):
-    frequency = jnp.exp(jnp.arange(32, dtype=F32) * (-math.log(10000.0) / 32))
-    angles = positions.astype(F32)[:, None] * jnp.tile(frequency, 4)[None, :]
-    sign = jnp.where(jnp.arange(128) % 64 < 32, -1.0, 1.0).astype(F32)
-    return jnp.cos(angles), jnp.sin(angles) * sign[None, :]
-
-
 def build(sizes):
     ctx, wsh = sizes["ctx"], sizes["wsh"]
     shards = ctx * wsh
@@ -1209,47 +1219,30 @@
         own = tokens.shape[0]
         plane = own * wsh
         group = plane * ctx
-        core = lax.axis_index("grp")
         odd = lax.rem(lax.axis_index("wsh"), 2) == 1
-        inputs = tokens.astype(F32)
-        factor_one = rms_factor(inputs)
-        normed_one = (inputs * factor_one * attend_gain).astype(BF)
-        marks = jnp.pad(segment_ids * 65536 + positions, (0, 1024 - own)).reshape(8, 128)
-
-        normed_all, w_qkv, marks_plane = link.run(
-            "gather_one",
-            1,
-            [
-                link.gather(normed_one, ("wsh",)),
-                link.swap(qkv_columns(query_key_value), ("wsh",)),
-                link.gather(marks, ("wsh",)),
-            ],
-        )
-        normed_all = normed_all.reshape(plane, D)
+        marks = jnp.pad(
+            jnp.stack([positions, segment_ids]).astype(F32), ((0, 6), (0, 256 - own))
+        )
+        (
+            queries,
+            kv_all,
+            normed_all,
+            w_qkv,
+            k_pos,
+            k_seg,
+            q_marks,
+            dy_all,
+            cos,
+            sin,
+        ) = head(link, tokens, attend_gain[None, :], query_key_value, marks, upstream)
+        kv_all = kv_all.reshape(group, 256)
+        normed_all, dy_all = normed_all.reshape(plane, D), dy_all.reshape(plane, D)
         w_qkv = w_qkv.reshape(D, 640)
-        plane_marks = marks_plane.reshape(wsh, 1024)[:, :own].reshape(plane)
-        q_pos, q_seg = plane_marks % 65536, plane_marks // 65536
-        cos, sin = rope_tables(q_pos)
-        queries, kv_own = project(normed_all, w_qkv, cos, sin)
-
-        kv_all, marks_all, dy_all, w_half = link.run(
-            "gather_keys",
-            2,
-            [
-                link.gather(kv_own, ("ctx",)),
-                link.gather(marks_plane, ("ctx",)),
-                link.gather(upstream, ("wsh",)),
-                link.columns(gate_up, ("wsh",), FF, FF // wsh),
-            ],
-        )
-        kv_all = kv_all.reshape(group, 256)
-        dy_all = dy_all.reshape(plane, D)
+        q_pos, q_seg = q_marks[0:1], q_marks[1:2]
+        attended, attended_wide, lse, w_half = attend_forward(
+            link, queries, kv_all, q_pos, q_seg, k_pos, k_seg, gate_up
+        )
         w_half = w_half.reshape(D, FF // wsh)
-        marks_all = marks_all.reshape(shards, 1024)[:, :own].reshape(group, 1)
-        k_pos, k_seg = marks_all % 65536, marks_all // 65536
-        q_pos, q_seg = q_pos.reshape(1, plane), q_seg.reshape(1, plane)
-        attended, attended_wide, lse = attend_forward(queries, kv_all, q_pos, q_seg, k_pos, k_seg)
-
         w_out = spread_rows(attend_out, odd)
         (
             middle,

time: 380 us -> 339 us (0.89); the launches traced: 373 us -> 339 us
  Pallas kernels: 343 us -> 318 us
  other arithmetic: 12.3 us -> 1.79 us
    pallas_call x4 -> x2, Pallas kernels: 134 us -> 110 us  [the longest x1 63.9 us: head(): pl.pallas_call(kernel, name='head', in_specs=[vmem] * len(operands), out_...]
    select_n x4 -> x0, other arithmetic: 4.2 us -> none  [the longest x1 2.99 us: local(): k_pos, k_seg = (marks_all % 65536, marks_all // 65536)]
    unnamed x37 -> x25, local copies, waits for them, and re-layouts: 10.1 us -> 12.3 us
where the time goes in v5:
time: 339 us
  Pallas kernels  318 us (94%)
  local copies, waits for them, and re-layouts  18.2 us (5%)
    pallas_call x1, Pallas kernels, finish(): pl.pallas_call(kernel, name='finish', in_specs=[vmem] * len(operands), ou...  86.6 us
    pallas_call x1, Pallas kernels, feed(): pl.pallas_call(kernel, name='feed', in_specs=[vmem] * len(operands), out_...  72.9 us
    pallas_call x1, Pallas kernels, head(): pl.pallas_call(kernel, name='head', in_specs=[vmem] * len(operands), out_...  63.9 us
    pallas_call x1, Pallas kernels, attend_backward(): pl.pallas_call(kernel, name='attend_backward', grid=(steps,), in_specs=[p...  48.2 us
    pallas_call x1, Pallas kernels, attend_forward(): pl.pallas_call(kernel, name='attend_forward', grid=(steps,), in_specs=[pl...  46.5 us
    unnamed x25, local copies, waits for them, and re-layouts  12.3 us

profile of v5, /device:TPU:0, one launch (start us, length us, event | category | flops | bytes accessed | tf_op | source)
XLA Modules:
  0.0 338.7 jit_solution(17318262204369286026)
XLA Ops:
  0.6 0.0 copy-start
  0.6 0.8 add_convert_fusion
  1.4 1.3 broadcast_in_dim.13.g_ref
  2.7 1.3 broadcast_in_dim.16.g_ref
  4.0 0.6 pad.4.m_ref
  4.6 0.9 slice_dynamic-update-slice_fusion.3
  5.5 0.9 slice_dynamic-update-slice_fusion.2
  6.5 1.0 slice_dynamic-update-slice_fusion.1
  7.5 0.9 slice_dynamic-update-slice_fusion.8
  8.5 0.0 copy-done
  8.6 1.0 broadcast_select_fusion.wo_ref
  9.6 63.9 %head.1 = (bf16[768,384]{1,0:T(8,128)(2,1)}, bf16[4,768,256]{2,1,0:T(8,128)(2,1)}, bf16[4,192,1152]{2,1,0:T(8,128)(2,1)}, bf16[4,288,640]{2,1,0:T(8,128)(2,1)}, ...) custom-call(bf16[192,1152]{1,0:T(8,128)(2,1)} %x_ref.5, ...), custom_call_target="tpu_custom_call" | custom-call | tf_op jit(solution)/shard_map/head/pallas_call | solution.py:828
  73.5 1.4 fusion
  74.9 46.5 %attend_forward.1 = (bf16[768,384]{1,0:T(8,128)(2,1)}, f32[768,384]{1,0:T(8,128)}, f32[8,768]{1,0:T(8,128)}, bf16[4,288,768]{2,1,0:T(8,128)(2,1)}) custom-call(bf16[768,384]{1,0:T(8,128)(2,1)} %get-tuple-element.41.q_ref, bf16[3072,256]{1,0:T(8,128)(2,1)} %bitcast.13, f32[1,768]{1,0:T(1,128)} %get-tuple-element.81.qp_ref, ...), custom_call_target="tpu_custom_call" | custom-call | tf_op jit(solution)/shard_map/attend_forward/pallas_call | solution.py:195
  121.4 72.9 %feed.1 = (f32[192,1152]{1,0:T(8,128)}, f32[192,1152]{1,0:T(8,128)}, bf16[4,192,1152]{2,1,0:T(8,128)(2,1)}, bf16[768,384]{1,0:T(8,128)(2,1)}, f32[1,1152]{1,0:T(...) custom-call(bf16[768,384]{1,0:T(8,128)(2,1)} %get-tuple-element.48.at_ref, ...), custom_call_target="tpu_custom_call" | custom-call | tf_op jit(solution)/shard_map/feed/pallas_call | solution.py:661
  194.3 48.2 %attend_backward.1 = (bf16[768,384]{1,0:T(8,128)(2,1)}, bf16[3072,256]{1,0:T(8,128)(2,1)}, bf16[4,288,768]{2,1,0:T(8,128)(2,1)}, bf16[96,1152]{1,0:T(8,128)(2,1)}) custom-call(bf16[768,384]{1,0:T(8,128)(2,1)} %get-tuple-element.41.q_ref, bf16[3072,256]{1,0:T(8,128)(2,1)} %bitcast.14, f32[1,768]{1,0:T(1,128)} %get-tuple-element.81.qp_ref, ...), custom_call_target="tpu_custom_call" | custom-call | tf_op jit(solution)/shard_map/attend_backward/pallas_call | solution.py:356
  242.5 86.6 %finish.1 = (bf16[192,1152]{1,0:T(8,128)(2,1)}, f32[192,1152]{1,0:T(8,128)}, f32[72,1920]{1,0:T(8,128)}, f32[72,1152]{1,0:T(8,128)}, f32[72,6144]{1,0:T(8,128)}, /*index=5*/f32[192,1152]{1,0:T(8,128)}, f32[8,128]{1,0:T(8,128)}) custom-call(bf16[768,384]{1,0:T(8,128)(2,1)} %get-tuple-element.54.q_ref, bf16[4,768,256]{2,1,0:T(8,128)(2,1)} %bitcast.19, ...), custom_call_target="tpu_custom_call" | custom-call | tf_op jit(solution)/shard_map/finish/pallas_call | solution.py:1155
  329.1 0.0 copy-start.3
  329.1 1.3 slice_bitcast_fusion
  330.4 0.0 copy-start.4
  330.4 1.9 copy.36
  332.2 0.0 copy-start.1
  332.2 2.3 copy.37
  334.5 0.0 copy-done.3
  334.5 0.8 copy.38
  335.3 0.0 copy-done.4
  335.3 0.7 copy.39
  336.0 0.0 copy-done.1
  336.0 0.0 copy-start.2
  336.0 1.2 copy.40
  337.3 0.6 copy-done.2
  337.8 0.9 copy.41
  (6 shorter events, 0.1 us)
Async XLA Ops:
  0.6 7.8 %copy-start = (bf16[288,1152]{1,0:T(8,128)(2,1)S(1)}, bf16[288,1152]{1,0:T(8,128)(2,1)}, u32[]{:S(2)}) copy-start(bf16[288,1152]{1,0:T(8,128)(2,1)} %param.15) | copy-start | bytes 1990660
  329.1 5.4 %copy-start.3 = (f32[72,1920]{1,0:T(8,128)S(1)}, f32[72,1920]{1,0:T(8,128)}, u32[]{:S(2)}) copy-start(f32[72,1920]{1,0:T(8,128)} %get-tuple-element.96) | copy-start | bytes 1658884
  330.4 4.9 %copy-start.4 = (f32[72,1152]{1,0:T(8,128)S(1)}, f32[72,1152]{1,0:T(8,128)}, u32[]{:S(2)}) copy-start(f32[72,1152]{1,0:T(8,128)} %get-tuple-element.97) | copy-start | bytes 995332
  332.2 3.8 %copy-start.1 = (f32[72,6144]{1,0:T(8,128)S(1)}, f32[72,6144]{1,0:T(8,128)}, u32[]{:S(2)}) copy-start(f32[72,6144]{1,0:T(8,128)} %get-tuple-element.98) | copy-start | bytes 5308420
  336.0 1.8 copy-start.2

commit v6 on v5

--- a/solution.py
+++ b/solution.py
@@ -78,19 +78,6 @@
     return jnp.concatenate(pieces, axis=1)
 
 
-def spread_rows(rows, odd):
-    n = rows.shape[1]
-    half = jnp.zeros((32, n), rows.dtype)
-    blank = jnp.zeros((64, n), rows.dtype)
-    even_rows = jnp.concatenate(
-        [rows[0:64], rows[192:256], rows[64:128], rows[256:288], half, rows[128:192], blank]
-    )
-    odd_rows = jnp.concatenate(
-        [rows[96:160], half, rows[0:32], rows[160:224], rows[32:96], rows[224:288], blank]
-    )
-    return jnp.where(odd, odd_rows, even_rows)
-
-
 def turn(x, cos, sin, lanes):
     swapped = jnp.where(lanes, pltpu.roll(x, 96, 1), pltpu.roll(x, 32, 1))
     return x * cos + swapped * sin
@@ -105,16 +92,18 @@
     return jnp.where(low if head == 0 else jnp.logical_not(low), block, jnp.zeros_like(block))
 
 
-def visible(kp_ref, ks_ref, qp_ref, qs_ref, start):
+def visible(kp_ref, ks_ref, qm_ref, start):
     key_pos = jnp.tile(kp_ref[pl.ds(start, TK), :], (1, TQ // 128))
     key_seg = jnp.tile(ks_ref[pl.ds(start, TK), :], (1, TQ // 128))
-    return (key_pos <= qp_ref[...]) & ((key_seg == 0) | (key_seg == qs_ref[...]))
-
-
+    return (key_pos <= qm_ref[0:1, :]) & ((key_seg == 0) | (key_seg == qm_ref[1:2, :]))
+
+
+ODD_ROWS = [(96, 32), (192, 64), (0, 64), (128, 64), (256, 64)]
+EVEN_ROWS = [(0, 64), (128, 64), (256, 64), (64, 64), (192, 32)]
 HEAD_SLOTS = [(0, 0), (0, 1), (1, 0), (1, 1), (2, 0)]
 
 
-def attend_forward(link, q, kv, q_pos, q_seg, k_pos, k_seg, gate_up):
+def attend_forward(link, q, kv, q_marks, k_pos, k_seg, gate_up):
     rows, keys = q.shape[0], kv.shape[0]
     steps = rows // TQ
     wsh = link.sizes["wsh"]
@@ -122,7 +111,7 @@
     peers = link.offsets(("wsh",))
 
     def kernel(
-        q_ref, kv_ref, qp_ref, qs_ref, kp_ref, ks_ref, gu_ref,
+        q_ref, kv_ref, qm_ref, kp_ref, ks_ref, gu_ref,
         a_ref, o_ref, lse_ref, wh_ref,
         acc, top, tot, bounce, send, recv, near,
     ):
@@ -158,7 +147,7 @@
             start = pl.multiple_of(t * TK, TK)
             k_tile = kv_ref[pl.ds(start, TK), :128]
             v_tile = kv_ref[pl.ds(start, TK), 128:]
-            seen = visible(kp_ref, ks_ref, qp_ref, qs_ref, start)
+            seen = visible(kp_ref, ks_ref, qm_ref, start)
             for j in range(5):
                 scores = dot_general(k_tile, heads[j], 1, 1)
                 scores = jnp.where(seen, scores, -1e30)
@@ -199,8 +188,7 @@
         in_specs=[
             pl.BlockSpec((TQ, 384), lambda i: (i, 0)),
             pl.BlockSpec((keys, 256), lambda i: (0, 0)),
-            pl.BlockSpec((1, TQ), lambda i: (0, i)),
-            pl.BlockSpec((1, TQ), lambda i: (0, i)),
+            pl.BlockSpec((8, TQ), lambda i: (0, i)),
             pl.BlockSpec((keys, 128), lambda i: (0, 0)),
             pl.BlockSpec((keys, 128), lambda i: (0, 0)),
             pl.BlockSpec(memory_space=pl.ANY),
@@ -229,7 +217,7 @@
         compiler_params=pltpu.CompilerParams(
             collective_id=2, has_side_effects=True, vmem_limit_bytes=VMEM_LIMIT
         ),
-    )(q, kv, q_pos, q_seg, k_pos, k_seg, gate_up)
+    )(q, kv, q_marks, k_pos, k_seg, gate_up)
 
 
 def owner_of(link):
@@ -240,161 +228,146 @@
     return {"ctx": to_c, "wsh": to_w}, jnp.logical_and(to_c == my_c, to_w == my_w)
 
 
+BK = 384
+
+
 def attend_backward(
-    link, q, kv, q_pos, q_seg, k_pos, k_seg, lse, out, out_grad, send_rows, send_down
+    link, q, kv, q_marks, k_pos, k_seg, lse, out, out_grad, send_rows
 ):
+    ctx = link.sizes["ctx"]
     rows, keys = q.shape[0], kv.shape[0]
     steps = rows // TQ
-    axes = ("ctx",)
-    peers = link.offsets(axes)
-    everyone = link.offsets(("ctx", "wsh"))
+    span = keys // ctx
+    levels = link.offsets(("ctx",))[1:]
 
     def kernel(
-        q_ref, kv_ref, qp_ref, qs_ref, kp_ref, ks_ref, lse_ref, o_ref, do_ref, rows_ref, down_ref,
-        dq_ref, dkv_ref, got_ref, down_got, acc, kv_acc, bounce, bounce_two, send, recv, near,
+        q_ref, kv_ref, qm_ref, kp_ref, ks_ref, lse_ref, o_ref, do_ref, rows_ref,
+        dq_ref, got_kv, got_rows,
+        acc, heads, grads, delta, kv_send, bounce, send, recv, kv_out, kv_in, near,
     ):
-        _, me = link.place(axes, peers[0])
+        wires = Wires(send, recv)
+        my_c = lax.axis_index("ctx")
+        greet([link.place(("ctx",), offset)[0] for offset in levels])
         copies = []
-        for at, offset in enumerate(peers[1:]):
-            where, index = link.place(axes, offset)
-            copies.append(
+        for offset in levels:
+            where, index = link.place(("ctx",), offset)
+            copies.append(wires.start(rows_ref.at[index], got_rows.at[my_c], where))
+        inward = pltpu.make_async_copy(rows_ref.at[my_c], bounce, near.at[0])
+        outward = pltpu.make_async_copy(bounce, got_rows.at[my_c], near.at[0])
+        inward.start()
+        acc[...] = jnp.zeros_like(acc)
+        delta[...] = jnp.zeros_like(delta)
+        for i in range(steps):
+            at = slice(i * TQ, i * TQ + TQ)
+            for j, (b, h) in enumerate(HEAD_SLOTS):
+                lanes = slice(128 * b, 128 * b + 128)
+                heads[i, j] = head_block(q_ref[at, lanes], h)
+                grad = head_block(do_ref[at, lanes], h)
+                grads[i, j] = grad
+                product = grad.astype(F32) * o_ref[at, lanes]
+                delta[i, j : j + 1, :] = jnp.sum(product.T, axis=0, keepdims=True)
+        inward.wait()
+        outward.start()
+
+        @pl.loop(0, ctx)
+        def _(d):
+            chunk = lax.rem(my_c + 1 + d, ctx)
+
+            @pl.loop(0, span // BK)
+            def _(t):
+                inner = pl.multiple_of(t * BK, 128)
+                at = pl.ds(pl.multiple_of(chunk * span + t * BK, 128), BK)
+                k_tile = kv_ref[at, :128]
+                v_tile = kv_ref[at, 128:]
+                key_pos = jnp.tile(kp_ref[at, :], (1, TQ // 128))
+                key_seg = jnp.tile(ks_ref[at, :], (1, TQ // 128))
+                k_sum = jnp.zeros((BK, 128), F32)
+                v_sum = jnp.zeros((BK, 128), F32)
+                for i in range(steps):
+                    cols = slice(i * TQ, i * TQ + TQ)
+                    seen = (key_pos <= qm_ref[0:1, cols]) & (
+                        (key_seg == 0) | (key_seg == qm_ref[1:2, cols])
+                    )
+                    for j in range(5):
+                        scores = dot_general(k_tile, heads[i, j], 1, 1)
+                        probs = jnp.where(seen, jnp.exp(scores - lse_ref[j : j + 1, cols]), 0.0)
+                        prob_grad = dot_general(v_tile, grads[i, j], 1, 1)
+                        score_grad = (probs * (prob_grad - delta[i, j : j + 1, :])).astype(BF)
+                        v_sum += jnp.dot(
+                            probs.astype(BF), grads[i, j], preferred_element_type=F32
+                        )
+                        k_sum += jnp.dot(score_grad, heads[i, j], preferred_element_type=F32)
+                        acc[i, j] += dot_general(k_tile, score_grad, 0, 0)
+                kv_send[chunk, pl.ds(inner, BK), :128] = k_sum.astype(BF)
+                kv_send[chunk, pl.ds(inner, BK), 128:] = v_sum.astype(BF)
+
+            @pl.when(d < ctx - 1)
+            def _():
                 pltpu.make_async_remote_copy(
-                    rows_ref.at[index],
-                    got_ref.at[me],
-                    send.at[at],
-                    recv.at[at],
-                    device_id=where,
+                    kv_send.at[chunk],
+                    got_kv.at[my_c],
+                    kv_out.at[d],
+                    kv_in.at[d],
+                    device_id={"ctx": chunk},
                     device_id_type=MESH,
-                )
-            )
-        owner, stays = owner_of(link)
-        move = pltpu.make_async_remote_copy(
-            down_ref,
-            down_got,
-            send.at[len(peers)],
-            recv.at[len(peers)],
-            device_id=owner,
-            device_id_type=MESH,
-        )
-        inward = pltpu.make_async_copy(rows_ref.at[me], bounce, near.at[0])
-        outward = pltpu.make_async_copy(bounce, got_ref.at[me], near.at[0])
-        stay_in = pltpu.make_async_copy(down_ref, bounce_two, near.at[1])
-        stay_out = pltpu.make_async_copy(bounce_two, down_got, near.at[1])
-
-        @pl.when(pl.program_id(0) == 0)
-        def _():
-            greet([link.place(("ctx", "wsh"), offset)[0] for offset in everyone[1:]])
-            for copy in copies:
-                copy.start()
-
-            @pl.when(jnp.logical_not(stays))
-            def _():
-                move.start()
-
-            @pl.when(stays)
-            def _():
-                stay_in.start()
-                stay_in.wait()
-                stay_out.start()
-
-            inward.start()
-            inward.wait()
-            outward.start()
-            kv_acc[...] = jnp.zeros_like(kv_acc)
-
-        acc[...] = jnp.zeros_like(acc)
-        heads = [head_block(q_ref[:, 128 * b : 128 * b + 128], h) for b, h in HEAD_SLOTS]
-        grads = [head_block(do_ref[:, 128 * b : 128 * b + 128], h) for b, h in HEAD_SLOTS]
-        delta = []
-        for j, (b, h) in enumerate(HEAD_SLOTS):
-            product = grads[j].astype(F32) * o_ref[:, 128 * b : 128 * b + 128]
-            delta.append(jnp.sum(product.T, axis=0, keepdims=True))
-
-        @pl.loop(0, keys // TK)
-        def _(t):
-            start = pl.multiple_of(t * TK, TK)
-            k_tile = kv_ref[pl.ds(start, TK), :128]
-            v_tile = kv_ref[pl.ds(start, TK), 128:]
-            seen = visible(kp_ref, ks_ref, qp_ref, qs_ref, start)
-            k_sum = jnp.zeros((TK, 128), F32)
-            v_sum = jnp.zeros((TK, 128), F32)
-            for j in range(5):
-                scores = dot_general(k_tile, heads[j], 1, 1)
-                probs = jnp.where(seen, jnp.exp(scores - lse_ref[j : j + 1, :]), 0.0)
-                prob_grad = dot_general(v_tile, grads[j], 1, 1)
-                score_grad = (probs * (prob_grad - delta[j])).astype(BF)
-                v_sum += jnp.dot(probs.astype(BF), grads[j], preferred_element_type=F32)
-                k_sum += jnp.dot(score_grad, heads[j], preferred_element_type=F32)
-                acc[j] += dot_general(k_tile, score_grad, 0, 0)
-            kv_acc[pl.ds(start, TK), :128] += k_sum
-            kv_acc[pl.ds(start, TK), 128:] += v_sum
-
+                ).start()
+
+        near_kv = pltpu.make_async_copy(kv_send.at[my_c], got_kv.at[my_c], near.at[1])
+        near_kv.start()
         low = lax.broadcasted_iota(jnp.int32, (TQ, 128), 1) < 64
-        for b in range(3):
-            first = acc[2 * b].T * 0.125
-            if b < 2:
-                block = jnp.where(low, first, acc[2 * b + 1].T * 0.125)
-            else:
-                block = jnp.where(low, first, 0.0)
-            dq_ref[:, 128 * b : 128 * b + 128] = block.astype(BF)
-
-        @pl.when(pl.program_id(0) == steps - 1)
-        def _():
-            dkv_ref[...] = kv_acc[...].astype(BF)
-            outward.wait()
-            for copy in copies:
-                copy.wait()
-
-            @pl.when(jnp.logical_not(stays))
-            def _():
-                move.wait()
-
-            @pl.when(stays)
-            def _():
-                stay_out.wait()
-
+        for i in range(steps):
+            for b in range(3):
+                first = acc[i, 2 * b].T * 0.125
+                if b < 2:
+                    block = jnp.where(low, first, acc[i, 2 * b + 1].T * 0.125)
+                else:
+                    block = jnp.where(low, first, 0.0)
+                dq_ref[i * TQ : i * TQ + TQ, 128 * b : 128 * b + 128] = block.astype(BF)
+
+        near_kv.wait()
+        outward.wait()
+        for copy in copies:
+            copy.wait()
+
+        for d in range(ctx - 1):
+            pltpu.make_async_remote_copy(
+                kv_send.at[0],
+                got_kv.at[0],
+                kv_out.at[d],
+                kv_in.at[d],
+                device_id={"ctx": my_c},
+                device_id_type=MESH,
+            ).wait()
+
+    vmem = pl.BlockSpec(memory_space=pltpu.VMEM)
+    anywhere = pl.BlockSpec(memory_space=pl.ANY)
     return pl.pallas_call(
         kernel,
         name="attend_backward",
-        grid=(steps,),
-        in_specs=[
-            pl.BlockSpec((TQ, 384), lambda i: (i, 0)),
-            pl.BlockSpec((keys, 256), lambda i: (0, 0)),
-            pl.BlockSpec((1, TQ), lambda i: (0, i)),
-            pl.BlockSpec((1, TQ), lambda i: (0, i)),
-            pl.BlockSpec((keys, 128), lambda i: (0, 0)),
-            pl.BlockSpec((keys, 128), lambda i: (0, 0)),
-            pl.BlockSpec((8, TQ), lambda i: (0, i)),
-            pl.BlockSpec((TQ, 384), lambda i: (i, 0)),
-            pl.BlockSpec((TQ, 384), lambda i: (i, 0)),
-            pl.BlockSpec(memory_space=pl.ANY),
-            pl.BlockSpec(memory_space=pl.ANY),
-        ],
-        out_specs=[
-            pl.BlockSpec((TQ, 384), lambda i: (i, 0)),
-            pl.BlockSpec((keys, 256), lambda i: (0, 0)),
-            pl.BlockSpec(memory_space=pl.ANY),
-            pl.BlockSpec(memory_space=pl.ANY),
-        ],
+        in_specs=[vmem] * 8 + [anywhere],
+        out_specs=[vmem] + [anywhere] * 2,
         out_shape=[
             jax.ShapeDtypeStruct((rows, 384), BF),
-            jax.ShapeDtypeStruct((keys, 256), BF),
+            jax.ShapeDtypeStruct((ctx, span, 256), BF),
             jax.ShapeDtypeStruct(send_rows.shape, BF),
-            jax.ShapeDtypeStruct(send_down.shape, BF),
         ],
         scratch_shapes=[
-            pltpu.VMEM((5, 128, TQ), F32),
-            pltpu.VMEM((keys, 256), F32),
+            pltpu.VMEM((steps, 5, 128, TQ), F32),
+            pltpu.VMEM((steps, 5, TQ, 128), BF),
+            pltpu.VMEM((steps, 5, TQ, 128), BF),
+            pltpu.VMEM((steps, 8, TQ), F32),
+            pltpu.VMEM((ctx, span, 256), BF),
             pltpu.VMEM(send_rows.shape[1:], BF),
-            pltpu.VMEM(send_down.shape, BF),
-            pltpu.SemaphoreType.DMA((len(peers) + 1,)),
-            pltpu.SemaphoreType.DMA((len(peers) + 1,)),
+            pltpu.SemaphoreType.DMA((ctx,)),
+            pltpu.SemaphoreType.DMA((ctx,)),
+            pltpu.SemaphoreType.DMA((ctx,)),
+            pltpu.SemaphoreType.DMA((ctx,)),
             pltpu.SemaphoreType.DMA((2,)),
         ],
         compiler_params=pltpu.CompilerParams(
             collective_id=11, has_side_effects=True, vmem_limit_bytes=VMEM_LIMIT
         ),
-    )(q, kv, q_pos, q_seg, k_pos, k_seg, lse, out, out_grad, send_rows, send_down)
+    )(q, kv, q_marks, k_pos, k_seg, lse, out, out_grad, send_rows)
 
 
 class Wires:
@@ -527,9 +500,9 @@
     pick = units // ctx // 2
 
     def kernel(
-        at_ref, wo_ref, x_ref, g_ref, wh_ref, dw_ref, dy_ref,
-        mid_ref, mg_ref, br_ref, ag_ref, fs_ref, dp_ref, gs_ref, ds_ref,
-        w_both, parts, near, total, near2, total2, n2, hgrad, hidden, gate_g, up_g,
+        at_ref, ao_ref, x_ref, g_ref, wh_ref, dw_ref, dy_ref,
+        mid_ref, mg_ref, br_ref, ag_ref, fs_ref, dp_ref, gs_ref, gl_ref, ds_ref,
+        wo_ref, w_both, parts, near, total, near2, total2, n2, hgrad, hidden, gate_g, up_g,
         down_h, down_pair, down_send, down_got, gate_h, gate_pair, send, recv, local,
     ):
         wires = Wires(send, recv)
@@ -545,6 +518,23 @@
 
         w_copy = pltpu.make_async_copy(wh_ref, w_both.at[core], local)
         w_copy.start()
+
+        odd = lax.rem(own, 2) == 1
+        wo_ref[...] = jnp.zeros_like(wo_ref)
+
+        def spread(pieces):
+            at = 0
+            for start, size in pieces:
+                wo_ref[start : start + size, :] = ao_ref[at : at + size, :]
+                at += size
+
+        @pl.when(odd)
+        def _():
+            spread(ODD_ROWS)
+
+        @pl.when(jnp.logical_not(odd))
+        def _():
+            spread(EVEN_ROWS)
 
         first = SquareScatter(wires, parts, near, total)
         for slot in (z, x, y, own):
@@ -563,7 +553,7 @@
         middle = x_ref[...].astype(F32) + first.result()
         mid_ref[...] = middle
         factor = lax.rsqrt(jnp.mean(middle * middle, axis=-1, keepdims=True) + EPSILON)
-        n2[own] = (middle * factor * g_ref[...]).astype(BF)
+        n2[own] = (middle * factor * g_ref[1:2, :]).astype(BF)
         gather = SquareGather(wires, n2)
         gather.begin()
         w_copy.wait()
@@ -620,7 +610,7 @@
         grad = second.result()
         middle = mid_ref[...]
         factor = lax.rsqrt(jnp.mean(middle * middle, axis=-1, keepdims=True) + EPSILON)
-        weighted = grad * g_ref[...]
+        weighted = grad * g_ref[1:2, :]
         inner = jnp.mean(weighted * middle, axis=-1, keepdims=True)
         middle_grad = (
             dy_ref[rows_of(own), :].astype(F32)
@@ -639,7 +629,9 @@
         outward(own)
         gate_swap.wait()
         for c in range(ctx):
-            gs_ref[c] = (gate_h[core, c].astype(F32) + gate_pair[c].astype(F32)).astype(BF)
+            both = (gate_h[core, c].astype(F32) + gate_pair[c].astype(F32)).astype(BF)
+            gs_ref[c] = both[:, : units // 2]
+            gl_ref[c] = both[:, units // 2 :]
         branch.relay()
         for slot in range(wsh):
             at = slice(slot * own_rows, slot * own_rows + own_rows)
@@ -662,7 +654,7 @@
         kernel,
         name="feed",
         in_specs=[vmem] * len(operands),
-        out_specs=[vmem] * 8,
+        out_specs=[vmem] * 9,
         out_shape=[
             jax.ShapeDtypeStruct((own_rows, D), F32),
             jax.ShapeDtypeStruct((own_rows, D), F32),
@@ -670,10 +662,12 @@
             jax.ShapeDtypeStruct((plane, 384), BF),
             jax.ShapeDtypeStruct((1, D), F32),
             jax.ShapeDtypeStruct((wsh, own_rows, D), BF),
-            jax.ShapeDtypeStruct((ctx, chunk, units), BF),
+            jax.ShapeDtypeStruct((ctx, chunk, units // 2), BF),
+            jax.ShapeDtypeStruct((ctx, chunk, units // 2), BF),
             jax.ShapeDtypeStruct((pick, D), BF),
         ],
         scratch_shapes=[
+            pltpu.VMEM((384, D), BF),
             pltpu.VMEM((2, D, units), BF),
             pltpu.VMEM((4, own_rows, D), BF),
             *square_scratch(own_rows),
@@ -704,7 +698,7 @@
     def kernel(
         x_ref, g_ref, w_ref, m_ref, up_ref,
         q_ref, kv_ref, n_ref, wq_ref, kpos_ref, kseg_ref, q_marks, dy_ref, c_ref, s_ref,
-        cols, marks_all, send, recv,
+        cols, mine, marks_all, send, recv,
     ):
         wires = Wires(send, recv)
         core = lax.axis_index("grp")
@@ -715,12 +709,12 @@
         greet(
             [{"wsh": x}, {"wsh": y}, {"wsh": z}, sibling] + [where for where, _ in levels]
         )
+        mine[...] = jnp.zeros_like(mine)
+        mine[:2, :own_rows] = m_ref[...]
         mark_copies = []
         for p in (x, y, z):
-            mark_copies.append(
-                wires.start(m_ref, marks_all.at[my_c, own], {"wsh": p})
-            )
-        marks_all[my_c, own] = m_ref[...]
+            mark_copies.append(wires.start(mine, marks_all.at[my_c, own], {"wsh": p}))
+        marks_all[my_c, own] = mine[...]
         side = pl.ds(pl.multiple_of(core * half, 16), half)
 
         for w in range(wsh):
@@ -741,7 +735,7 @@
             )
         tokens_in = x_ref[...].astype(F32)
         factor = lax.rsqrt(jnp.mean(tokens_in * tokens_in, axis=-1, keepdims=True) + EPSILON)
-        n_ref[own] = (tokens_in * factor * g_ref[...]).astype(BF)
+        n_ref[own] = (tokens_in * factor * g_ref[0:1, :]).astype(BF)
         gather = SquareGather(wires, n_ref)
         gather.begin()
         wq_ref[own] = cols[own]
@@ -844,6 +838,7 @@
         ],
         scratch_shapes=[
             pltpu.VMEM((wsh, 2 * half, 640), BF),
+            pltpu.VMEM((8, 256), F32),
             pltpu.VMEM((ctx, wsh, 8, 256), F32),
             pltpu.SemaphoreType.DMA((5 * ctx + 24,)),
             pltpu.SemaphoreType.DMA((5 * ctx + 24,)),
@@ -856,7 +851,7 @@
 
 def finish(
     link, q_grad, kv_grad, weight, cos, sin, normed, tokens, gain, middle_grad, gate_got, down_got,
-    attended, branch, feed_sum, down_part, middle,
+    attended, branch, feed_sum, down_part, middle, gate_late,
 ):
     ctx, wsh = link.sizes["ctx"], link.sizes["wsh"]
     shards = ctx * wsh
@@ -871,12 +866,13 @@
     down_rows = down_got.shape[0]
 
     def kernel(
-        q_ref, kv_send, w_ref, c_ref, s_ref, n_ref, x_ref, g_ref, mg_ref, gate_ref, down_ref,
-        at_ref, br_ref, fs_ref, dp_ref, mid_ref,
-        act_ref, ig_ref, qkv_ref, out_ref, gate_out, down_out, gains_out,
-        kv_ref, pg, parts, near, total, near2, total2, acc, wide, q_own, q_pair, q_send, q_got,
-        q_mid, q_fin, kv_own, kv_pair, kv_go, kv_got, kv_mid, kv_fin, gate_mid, gate_fin, down_fin, out_halves,
-        out_pair, out_send, out_mid, out_got, out_fin, gains, gains_got, gains_fin,
+        q_ref, kv_ref, w_ref, c_ref, s_ref, n_ref, x_ref, g_ref, mg_ref, gate_ref, down_ref,
+        at_ref, br_ref, fs_ref, dp_ref, mid_ref, late_ref,
+        act_ref, ig_ref, q_fin, kv_fin, out_fin, gate_fin, late_fin, down_fin, gains_out,
+        pg, parts, near, total, near2, total2, wide, q_own, q_pair, q_send, q_got,
+        q_mid, kv_own, kv_pair, kv_go, kv_got, kv_mid, gate_mid, late_got,
+        late_mid, out_halves,
+        out_pair, out_send, out_mid, out_got, gains, gains_got, gains_fin,
         send, recv,
     ):
         wires = Wires(send, recv)
@@ -908,16 +904,60 @@
                 for copy in copies:
                     copy.start()
 
-        kv_copies = []
-        for offset in link.offsets(("ctx",))[1:]:
-            where, index = link.place(("ctx",), offset)
-            kv_copies.append(wires.start(kv_send.at[index], kv_ref.at[my_c], where))
+        levels = [link.place(("ctx",), offset) for offset in link.offsets(("ctx",))[1:]]
+        late_copies = []
+        for where, index in levels:
+            late_copies.append(wires.start(late_ref.at[index], late_got.at[my_c], where))
+
+        owner, stays = owner_of(link)
+        moves = jnp.logical_not(stays)
+        down_move = wires.copy(down_ref, down_fin.at[core], owner)
+        begin(moves, down_move)
+
+        @pl.when(stays)
+        def _():
+            down_fin[core] = down_ref[...]
+
+        low = lax.rem(lax.broadcasted_iota(jnp.int32, (own_rows, 128), 1), 64) < 32
+        scatter = SquareScatter(wires, parts, near, total)
+        gain_sum = jnp.zeros((1, D), F32)
+        for slot in (scatter.z, scatter.x, scatter.y, scatter.own):
+            at = pl.ds(pl.multiple_of(slot * own_rows, 16), own_rows)
+            cos_t, sin_t = c_ref[at, :], -s_ref[at, :]
+            for b in range(3):
+                block = q_ref[at, 128 * b : 128 * b + 128].astype(F32)
+                pg[at, 128 * b : 128 * b + 128] = turn(block, cos_t, sin_t, low).astype(BF)
+            summed = kv_ref[0, at, :].astype(F32)
+            for c in range(1, ctx):
+                summed += kv_ref[c, at, :].astype(F32)
+            block = summed[:, :128].astype(BF).astype(F32)
+            pg[at, 384:512] = turn(block, cos_t, sin_t, low).astype(BF)
+            pg[at, 512:] = summed[:, 128:].astype(BF)
+            part = dot_general(pg[at, :], w_ref[...], 1, 1)
+            parts[slot] = part.astype(BF)
+            gain_sum += jnp.sum(part * n_ref[at, :].astype(F32), axis=0, keepdims=True)
+            if slot is scatter.z:
+                scatter.send_diagonal()
+            elif slot is scatter.x:
+                scatter.send_x()
+            elif slot is scatter.y:
+                scatter.send_y()
+
+        strip = dot_general(n_ref[...], pg[:, 384:], 0, 0).astype(BF)
+        for c in range(ctx):
+            kv_own[c] = strip[c * chunk : c * chunk + chunk, :]
+        kv_swap = wires.copy(kv_own, kv_pair, sibling)
+        begin(first, kv_swap)
+        scatter.relay()
+        strip = dot_general(n_ref[...], pg[:, :384], 0, 0).astype(BF)
+        for c in range(ctx):
+            q_own[c] = strip[c * chunk : c * chunk + chunk, :]
+        q_swap = wires.copy(q_own, q_pair, sibling)
+        begin(second, q_swap)
         layer = SquareScatter(wires, dp_ref, near2, total2)
         layer.send_diagonal()
         layer.send_x()
         layer.send_y()
-        kv_ref[my_c] = kv_send[my_c]
-
         wide[...] = dot_general(at_ref[...], br_ref[...], 0, 0)
 
         def out_strips(pieces):
@@ -932,44 +972,55 @@
 
         @pl.when(odd)
         def _():
-            out_strips([(96, 32), (192, 64), (0, 64), (128, 64), (256, 64)])
+            out_strips(ODD_ROWS)
 
         @pl.when(jnp.logical_not(odd))
         def _():
-            out_strips([(0, 64), (128, 64), (256, 64), (64, 64), (192, 32)])
+            out_strips(EVEN_ROWS)
 
         out_swap = wires.start(out_halves.at[1 - core], out_pair, sibling)
-        low = lax.rem(lax.broadcasted_iota(jnp.int32, (own_rows, 128), 1), 64) < 32
-
-        @pl.loop(0, wsh)
-        def _(slot):
-            at = pl.ds(pl.multiple_of(slot * own_rows, 16), own_rows)
-            for b in range(3):
-                block = q_ref[at, 128 * b : 128 * b + 128].astype(F32)
-                pg[at, 128 * b : 128 * b + 128] = turn(
-                    block, c_ref[at, :], -s_ref[at, :], low
-                ).astype(BF)
-
+        q_copies, kvg_copies, out_copies = [], [], []
+        for where, index in levels:
+            q_copies.append(wires.copy(q_send.at[index], q_got.at[my_c], where))
+            kvg_copies.append(wires.copy(kv_go.at[index], kv_got.at[my_c], where))
+
+        @pl.when(first)
+        def _():
+            q_swap.wait_recv()
+
+            @pl.loop(0, ctx)
+            def _(c):
+                q_send[c] = (q_own[c].astype(F32) + q_pair[c].astype(F32)).astype(BF)
+
+            for copy in q_copies:
+                copy.start()
+            q_got[my_c] = q_send[my_c]
+            kv_swap.wait_send()
+
+        @pl.when(second)
+        def _():
+            kv_swap.wait_recv()
+
+            @pl.loop(0, ctx)
+            def _(c):
+                kv_go[c] = (kv_own[c].astype(F32) + kv_pair[c].astype(F32)).astype(BF)
+
+            for copy in kvg_copies:
+                copy.start()
+            kv_got[my_c] = kv_go[my_c]
+            q_swap.wait_send()
+
+        both = jnp.concatenate([gain_sum / g_ref[0:1, :], fs_ref[...]], axis=0)
+        gains[...] = jnp.zeros_like(gains)
+        for s in range(shards):
+            gains[s, :2, :rows] = both[:, rows * s : rows * s + rows]
+        gain_copies = []
+        for offset in peers[1:]:
+            where, index = link.place(axes, offset)
+            gain_copies.append(wires.start(gains.at[index], gains_got.at[me], where))
+        gains_got[me] = gains[me]
         layer.relay()
-        for b in range(3):
-            acc[384 * b : 384 * b + 384, :] = dot_general(
-                n_ref[:, 384 * b : 384 * b + 384], pg[:, :384], 0, 0
-            )
-
-        for c in range(ctx):
-            q_own[c] = acc[c * chunk : c * chunk + chunk, :].astype(BF)
-        q_swap = wires.copy(q_own, q_pair, sibling)
-        begin(second, q_swap)
-
-        down_fin[core] = down_ref[...]
-        down_copy = wires.start(down_fin.at[core], down_fin.at[core], sibling)
-
-        over_ctx(gate_ref, gate_mid)
-        gate_moves = in_plane(gate_mid, lambda w: gate_fin.at[core, w])
-        for copy in gate_moves:
-            copy.start()
-        gate_fin[core, my_w] = gate_mid[my_w]
-        act_ref[...] = (mid_ref[...] + layer.result()).astype(BF)
+
         out_swap.wait()
         for k in range(ctx):
             strip = slice(k * rows, k * rows + rows)
@@ -981,131 +1032,51 @@
             copy.start()
         out_mid[my_w] = out_send[my_w]
 
-        @pl.when(first)
-        def _():
-            q_swap.wait_recv()
-
-            @pl.loop(0, ctx)
-            def _(c):
-                q_send[c] = (q_own[c].astype(F32) + q_pair[c].astype(F32)).astype(BF)
-
-        @pl.when(second)
-        def _():
-            q_swap.wait_send()
-
-        for copy in gate_moves:
-            copy.wait()
-        gate_copy = wires.start(gate_fin.at[core], gate_fin.at[core], sibling)
-        down_copy.wait()
-        down_out[:down_rows, :] = down_fin[0].astype(F32)
-        down_out[down_rows:, :] = down_fin[1].astype(F32)
-        gate_copy.wait()
-        for half in range(2):
-            for w in range(wsh):
-                left = (half * wsh + w) * gate_width
-                gate_out[:, left : left + gate_width] = gate_fin[half, w].astype(F32)
-
+        grad = scatter.result()
+        x = x_ref[...].astype(F32)
+        factor = lax.rsqrt(jnp.mean(x * x, axis=-1, keepdims=True) + EPSILON)
+        weighted = grad * g_ref[0:1, :]
+        inner = jnp.mean(weighted * x, axis=-1, keepdims=True)
+        ig_ref[...] = mg_ref[...] + factor * weighted - x * (factor * factor * factor) * inner
         for copy in out_moves:
             copy.wait()
-
-        for copy in kv_copies:
-            copy.wait()
-        q_copies, kvg_copies, out_copies = [], [], []
-        for offset in link.offsets(("ctx",))[1:]:
-            where, index = link.place(("ctx",), offset)
-            q_copies.append(wires.copy(q_send.at[index], q_got.at[my_c], where))
-            kvg_copies.append(wires.copy(kv_go.at[index], kv_got.at[my_c], where))
-        begin(first, *q_copies)
-        for offset in link.offsets(("ctx",))[1:]:
-            where, index = link.place(("ctx",), offset)
+        for where, index in levels:
             part = out_mid.at[index // fold, lax.rem(index, fold)]
             out_copies.append(wires.start(part, out_got.at[my_c], where))
         out_got[my_c] = out_mid[my_c // fold, lax.rem(my_c, fold)]
-        scatter = SquareScatter(wires, parts, near, total)
-        gain_sum = jnp.zeros((1, D), F32)
-        for slot in (scatter.z, scatter.x, scatter.y, scatter.own):
-            at = pl.ds(pl.multiple_of(slot * own_rows, 16), own_rows)
-            summed = kv_ref[0, at, :].astype(F32)
-            for c in range(1, ctx):
-                summed += kv_ref[c, at, :].astype(F32)
-            block = summed[:, :128].astype(BF).astype(F32)
-            pg[at, 384:512] = turn(block, c_ref[at, :], -s_ref[at, :], low).astype(BF)
-            pg[at, 512:] = summed[:, 128:].astype(BF)
-            part = dot_general(pg[at, :], w_ref[...], 1, 1)
-            parts[slot] = part.astype(BF)
-            gain_sum += jnp.sum(part * n_ref[at, :].astype(F32), axis=0, keepdims=True)
-            if slot is scatter.z:
-                scatter.send_diagonal()
-            elif slot is scatter.x:
-                scatter.send_x()
-            elif slot is scatter.y:
-                scatter.send_y()
-
-        for b in range(3):
-            acc[384 * b : 384 * b + 384, :256] = dot_general(
-                n_ref[:, 384 * b : 384 * b + 384], pg[:, 384:], 0, 0
-            )
-
-        for c in range(ctx):
-            kv_own[c] = acc[c * chunk : c * chunk + chunk, :256].astype(BF)
-        kv_swap = wires.copy(kv_own, kv_pair, sibling)
-        begin(first, kv_swap)
-        both = jnp.concatenate([gain_sum / g_ref[...], fs_ref[...]], axis=0)
-        gains[...] = jnp.zeros_like(gains)
-        for s in range(shards):
-            gains[s, :2, :rows] = both[:, rows * s : rows * s + rows]
-        gain_copies = []
-        for offset in peers[1:]:
-            where, index = link.place(axes, offset)
-            gain_copies.append(wires.start(gains.at[index], gains_got.at[me], where))
-        gains_got[me] = gains[me]
-        scatter.relay()
-
-        @pl.when(second)
-        def _():
-            kv_swap.wait_recv()
-
-            @pl.loop(0, ctx)
-            def _(c):
-                kv_go[c] = (kv_own[c].astype(F32) + kv_pair[c].astype(F32)).astype(BF)
-
-            for copy in kvg_copies:
-                copy.start()
-            kv_got[my_c] = kv_go[my_c]
+
+
+        @pl.when(moves)
+        def _():
+            down_move.wait()
+
+        down_copy = wires.start(down_fin.at[core], down_fin.at[core], sibling)
+        over_ctx(gate_ref, gate_mid)
+        gate_moves = in_plane(gate_mid, lambda w: gate_fin.at[core, w])
+        for copy in gate_moves:
+            copy.start()
+        gate_fin[core, my_w] = gate_mid[my_w]
+        for copy in late_copies:
+            copy.wait()
+        late_got[my_c] = late_ref[my_c]
+        over_ctx(late_got, late_mid)
+        late_moves = in_plane(late_mid, lambda w: late_fin.at[core, w])
+        for copy in late_moves:
+            copy.start()
+        late_fin[core, my_w] = late_mid[my_w]
+        act_ref[...] = (mid_ref[...] + layer.result()).astype(BF)
+
+        q_moves = in_plane(q_mid, lambda w: q_fin.at[w])
+        kv_moves = in_plane(kv_mid, lambda w: kv_fin.at[w])
 
         @pl.when(first)
         def _():
-            kv_swap.wait_send()
-            q_got[my_c] = q_send[my_c]
             for copy in q_copies:
                 copy.wait()
             over_ctx(q_got, q_mid)
-
-        q_moves = in_plane(q_mid, lambda w: q_fin.at[w])
-        begin(first, *q_moves)
-        for copy in out_copies:
-            copy.wait()
-        out_fin[core] = jnp.sum(out_got[...].astype(F32), axis=0).astype(BF)
-
-        out_copy = wires.start(out_fin.at[core], out_fin.at[core], sibling)
-
-        grad = scatter.result()
-        x = x_ref[...].astype(F32)
-        factor = lax.rsqrt(jnp.mean(x * x, axis=-1, keepdims=True) + EPSILON)
-        weighted = grad * g_ref[...]
-        inner = jnp.mean(weighted * x, axis=-1, keepdims=True)
-        ig_ref[...] = mg_ref[...] + factor * weighted - x * (factor * factor * factor) * inner
-        q_final = wires.copy(q_fin, q_fin, sibling)
-        kv_final = wires.copy(kv_fin, kv_fin, sibling)
-
-        kv_moves = in_plane(kv_mid, lambda w: kv_fin.at[w])
-
-        @pl.when(first)
-        def _():
             for copy in q_moves:
-                copy.wait()
+                copy.start()
             q_fin[my_w] = q_mid[my_w]
-            q_final.start()
 
         @pl.when(second)
         def _():
@@ -1114,19 +1085,39 @@
             over_ctx(kv_got, kv_mid)
             for copy in kv_moves:
                 copy.start()
-            for copy in kv_moves:
-                copy.wait()
             kv_fin[my_w] = kv_mid[my_w]
-            kv_final.start()
-
+
+        for copy in gate_moves + late_moves:
+            copy.wait()
+        gate_copy = wires.start(gate_fin.at[core], gate_fin.at[core], sibling)
+        late_copy = wires.start(late_fin.at[core], late_fin.at[core], sibling)
+        for copy in out_copies:
+            copy.wait()
+        out_fin[core] = jnp.sum(out_got[...].astype(F32), axis=0).astype(BF)
+        out_copy = wires.start(out_fin.at[core], out_fin.at[core], sibling)
         for copy in gain_copies:
             copy.wait()
         gains_fin[core] = jnp.sum(gains_got[...], axis=0)
         gain_copy = wires.start(gains_fin.at[core], gains_fin.at[core], sibling)
+        q_final = wires.copy(q_fin, q_fin, sibling)
+        kv_final = wires.copy(kv_fin, kv_fin, sibling)
+
+        @pl.when(first)
+        def _():
+            for copy in q_moves:
+                copy.wait()
+            q_final.start()
+
+        @pl.when(second)
+        def _():
+            for copy in kv_moves:
+                copy.wait()
+            kv_final.start()
+
+        down_copy.wait()
+        gate_copy.wait()
+        late_copy.wait()
         out_copy.wait()
-        out_ref[...] = jnp.concatenate(
-            [out_fin[0, :, :576].astype(F32), out_fin[1, :, :576].astype(F32)], axis=1
-        )
 
         @pl.when(first)
         def _():
@@ -1138,65 +1129,106 @@
             kv_final.wait_send()
             q_final.wait_recv()
 
-        qkv_ref[...] = qkv_restore(
-            [
-                jnp.concatenate([q_fin[w].astype(F32), kv_fin[w].astype(F32)], axis=1)
-                for w in range(wsh)
-            ]
-        )
         gain_copy.wait()
         gains_out[...] = gains_fin[0] + gains_fin[1]
 
     operands = (
         q_grad, kv_grad, weight, cos, sin, normed, tokens, gain, middle_grad, gate_got, down_got,
-        attended, branch, feed_sum, down_part, middle,
+        attended, branch, feed_sum, down_part, middle, gate_late,
     )
     vmem = pl.BlockSpec(memory_space=pltpu.VMEM)
     return pl.pallas_call(
         kernel,
         name="finish",
         in_specs=[vmem] * len(operands),
-        out_specs=[vmem] * 7,
+        out_specs=[vmem] * 9,
         out_shape=[
             jax.ShapeDtypeStruct((own_rows, D), BF),
             jax.ShapeDtypeStruct((own_rows, D), F32),
-            jax.ShapeDtypeStruct((rows, QW + 2 * KW), F32),
-            jax.ShapeDtypeStruct((rows, D), F32),
-            jax.ShapeDtypeStruct((rows, 2 * FF), F32),
-            jax.ShapeDtypeStruct((2 * down_rows, D), F32),
+            jax.ShapeDtypeStruct((wsh, rows, 384), BF),
+            jax.ShapeDtypeStruct((wsh, rows, 256), BF),
+            jax.ShapeDtypeStruct((2, rows, 640), BF),
+            jax.ShapeDtypeStruct((2, wsh, rows, gate_width), BF),
+            jax.ShapeDtypeStruct((2, wsh, rows, gate_width), BF),
+            jax.ShapeDtypeStruct((2, down_rows, D), BF),
             jax.ShapeDtypeStruct((8, 128), F32),
         ],
         scratch_shapes=[
-            pltpu.VMEM((ctx, plane, 256), BF),
             pltpu.VMEM((plane, 640), BF),
             pltpu.VMEM((4, own_rows, D), BF),
             *square_scratch(own_rows),
             *square_scratch(own_rows),
-            pltpu.VMEM((D, 384), F32),
             pltpu.VMEM((384, D), F32),
             *[pltpu.VMEM((ctx, chunk, 384), BF)] * 4,
-            *[pltpu.VMEM((wsh, rows, 384), BF)] * 2,
+            pltpu.VMEM((wsh, rows, 384), BF),
             *[pltpu.VMEM((ctx, chunk, 256), BF)] * 4,
-            *[pltpu.VMEM((wsh, rows, 256), BF)] * 2,
+            pltpu.VMEM((wsh, rows, 256), BF),
             pltpu.VMEM((wsh, rows, gate_width), BF),
-            pltpu.VMEM((2, wsh, rows, gate_width), BF),
-            pltpu.VMEM((2, down_rows, D), BF),
+            pltpu.VMEM((ctx, chunk, gate_width), BF),
+            pltpu.VMEM((wsh, rows, gate_width), BF),
             pltpu.VMEM((2, 288, 640), BF),
             pltpu.VMEM((288, 640), BF),
             pltpu.VMEM((wsh, fold, rows, 640), BF),
             pltpu.VMEM((wsh, fold, rows, 640), BF),
             pltpu.VMEM((ctx, rows, 640), BF),
-            pltpu.VMEM((2, rows, 640), BF),
             pltpu.VMEM((shards, 8, 128), F32),
             pltpu.VMEM((shards, 8, 128), F32),
             pltpu.VMEM((2, 8, 128), F32),
-            pltpu.SemaphoreType.DMA((3 * shards + 2 * ctx + 32,)),
-            pltpu.SemaphoreType.DMA((3 * shards + 2 * ctx + 32,)),
+            pltpu.SemaphoreType.DMA((shards + 5 * ctx + 48,)),
+            pltpu.SemaphoreType.DMA((shards + 5 * ctx + 48,)),
         ],
         compiler_params=pltpu.CompilerParams(
             collective_id=8, has_side_effects=True, vmem_limit_bytes=VMEM_LIMIT
         ),
     )(*operands)
+
+
+def wrap(act, input_grad, q_sum, kv_sum, out_sum, gate_sum, late_sum, down_sum):
+    wsh, rows, _ = q_sum.shape
+    down_rows = down_sum.shape[1]
+    width = gate_sum.shape[3]
+
+    def kernel(
+        act_in, ig_in, q_in, kv_in, out_in, gate_in, late_in, down_in,
+        act_ref, ig_ref, qkv_ref, out_ref, gate_ref, down_ref,
+    ):
+        act_ref[...] = act_in[...]
+        ig_ref[...] = ig_in[...]
+        qkv_ref[...] = qkv_restore(
+            [
+                jnp.concatenate([q_in[w].astype(F32), kv_in[w].astype(F32)], axis=1)
+                for w in range(wsh)
+            ]
+        )
+        out_ref[...] = jnp.concatenate(
+            [out_in[0, :, :576].astype(F32), out_in[1, :, :576].astype(F32)], axis=1
+        )
+        for half in range(2):
+            for w in range(wsh):
+                left = (half * wsh + w) * 2 * width
+                gate_ref[:, left : left + width] = gate_in[half, w].astype(F32)
+                left += width
+                gate_ref[:, left : left + width] = late_in[half, w].astype(F32)
+            down_ref[half * down_rows : half * down_rows + down_rows, :] = down_in[half].astype(
+                F32
+            )
+
+    vmem = pl.BlockSpec(memory_space=pltpu.VMEM)
+    return pl.pallas_call(
+        kernel,
+        name="wrap",
+        in_specs=[vmem] * 8,
+        out_specs=[vmem] * 6,
+        out_shape=[
+            jax.ShapeDtypeStruct(act.shape, BF),
+            jax.ShapeDtypeStruct(act.shape, F32),
+            jax.ShapeDtypeStruct((rows, QW + 2 * KW), F32),
+            jax.ShapeDtypeStruct((rows, D), F32),
+            jax.ShapeDtypeStruct((rows, 2 * FF), F32),
+            jax.ShapeDtypeStruct((2 * down_rows, D), F32),
+        ],
+        compiler_params=pltpu.CompilerParams(vmem_limit_bytes=VMEM_LIMIT),
+    )(act, input_grad, q_sum, kv_sum, out_sum, gate_sum, late_sum, down_sum)
 
 
 def build(sizes):
@@ -1219,10 +1251,8 @@
         own = tokens.shape[0]
         plane = own * wsh
         group = plane * ctx
-        odd = lax.rem(lax.axis_index("wsh"), 2) == 1
-        marks = jnp.pad(
-            jnp.stack([positions, segment_ids]).astype(F32), ((0, 6), (0, 256 - own))
-        )
+        marks = jnp.stack([positions, segment_ids]).astype(F32)
+        both_gains = jnp.stack([attend_gain, feed_gain])
         (
             queries,
             kv_all,
@@ -1234,16 +1264,14 @@
             dy_all,
             cos,
             sin,
-        ) = head(link, tokens, attend_gain[None, :], query_key_value, marks, upstream)
+        ) = head(link, tokens, both_gains, query_key_value, marks, upstream)
         kv_all = kv_all.reshape(group, 256)
         normed_all, dy_all = normed_all.reshape(plane, D), dy_all.reshape(plane, D)
         w_qkv = w_qkv.reshape(D, 640)
-        q_pos, q_seg = q_marks[0:1], q_marks[1:2]
         attended, attended_wide, lse, w_half = attend_forward(
-            link, queries, kv_all, q_pos, q_seg, k_pos, k_seg, gate_up
+            link, queries, kv_all, q_marks, k_pos, k_seg, gate_up
         )
         w_half = w_half.reshape(D, FF // wsh)
-        w_out = spread_rows(attend_out, odd)
         (
             middle,
             middle_grad,
@@ -1252,17 +1280,19 @@
             feed_sum,
             down_part,
             gate_send,
+            gate_late,
             down_sum,
-        ) = feed(link, attended, w_out, tokens, feed_gain[None, :], w_half, down_weight, dy_all)
-        q_grad, kv_grad, gate_got, down_got = attend_backward(
-            link, queries, kv_all, q_pos, q_seg, k_pos, k_seg, lse, attended_wide, attended_grad,
-            gate_send, down_sum,
+        ) = feed(link, attended, attend_out, tokens, both_gains, w_half, down_weight, dy_all)
+        q_grad, kv_grad, gate_got = attend_backward(
+            link, queries, kv_all, q_marks, k_pos, k_seg, lse, attended_wide, attended_grad,
+            gate_send,
         )
-        (activations, input_grad, qkv_out, out_out, gate_out, down_out, gain_out) = finish(
-            link, q_grad, kv_grad.reshape(ctx, plane, 256), w_qkv, cos, sin, normed_all, tokens,
-            attend_gain[None, :], middle_grad, gate_got, down_got, attended,
-            branch_all.reshape(plane, D), feed_sum, down_part, middle,
+        *sums, gain_out = finish(
+            link, q_grad, kv_grad, w_qkv, cos, sin, normed_all, tokens,
+            both_gains, middle_grad, gate_got, down_sum, attended,
+            branch_all.reshape(plane, D), feed_sum, down_part, middle, gate_late,
         )
+        activations, input_grad, qkv_out, out_out, gate_out, down_out = wrap(*sums)
         width = D // shards
         return (
             activations,

time: 339 us -> 323 us (0.953); the launches traced: 339 us -> 317 us
  local copies, waits for them, and re-layouts: 18.2 us -> 2.67 us
  Pallas kernels: 318 us -> 311 us
    pallas_call x1, Pallas kernels: 86.6 us -> 72.3 us  [finish(): pl.pallas_call(kernel, name='finish', in_specs=[vmem] * len(operands), ou...]
    unnamed x25 -> x0, local copies, waits for them, and re-layouts: 12.3 us -> none
    pallas_call x1 -> x2, Pallas kernels: 48.2 us -> 55.3 us  [the longest x1 51.1 us: attend_backward(): pl.pallas_call(kernel, name='attend_backward', in_specs=[vmem] * 8 + [any...]
where the time goes in v6:
time: 323 us; the launch traced here: 317 us
  Pallas kernels  311 us (96%)
    pallas_call x1, Pallas kernels, feed(): pl.pallas_call(kernel, name='feed', in_specs=[vmem] * len(operands), out_...  73.3 us
    pallas_call x1, Pallas kernels, finish(): pl.pallas_call(kernel, name='finish', in_specs=[vmem] * len(operands), ou...  72.3 us
    pallas_call x1, Pallas kernels, head(): pl.pallas_call(kernel, name='head', in_specs=[vmem] * len(operands), out_...  63.9 us
    pallas_call x1, Pallas kernels, attend_backward(): pl.pallas_call(kernel, name='attend_backward', in_specs=[vmem] * 8 + [any...  51.1 us
    pallas_call x1, Pallas kernels, attend_forward(): pl.pallas_call(kernel, name='attend_forward', grid=(steps,), in_specs=[pl...  46.5 us

profile of v6, /device:TPU:0, one launch (start us, length us, event | category | flops | bytes accessed | tf_op | source)
XLA Modules:
  0.0 316.8 jit_solution(7258965815629683592)
XLA Ops:
  0.6 1.3 add_convert_fusion.m_ref
  1.9 0.7 stack.18
  2.6 0.7 stack.19
  3.3 0.6 pad_maximum_fusion.g_ref
  3.9 63.9 %head.1 = (bf16[768,384]{1,0:T(8,128)(2,1)}, bf16[4,768,256]{2,1,0:T(8,128)(2,1)}, bf16[4,192,1152]{2,1,0:T(8,128)(2,1)}, bf16[4,288,640]{2,1,0:T(8,128)(2,1)}, ...) custom-call(bf16[192,1152]{1,0:T(8,128)(2,1)} %x_ref.5, ...), custom_call_target="tpu_custom_call" | custom-call | tf_op jit(solution)/shard_map/head/pallas_call | solution.py:822
  67.8 46.5 %attend_forward.1 = (bf16[768,384]{1,0:T(8,128)(2,1)}, f32[768,384]{1,0:T(8,128)}, f32[8,768]{1,0:T(8,128)}, bf16[4,288,768]{2,1,0:T(8,128)(2,1)}) custom-call(bf16[768,384]{1,0:T(8,128)(2,1)} %get-tuple-element.49.q_ref, bf16[3072,256]{1,0:T(8,128)(2,1)} %bitcast.12, f32[8,768]{1,0:T(8,128)} %get-tuple-element.51.qm_ref, ...), custom_call_target="tpu_custom_call" | custom-call | tf_op jit(solution)/shard_map/attend_forward/pallas_call | solution.py:184
  114.3 73.3 %feed.1 = (f32[192,1152]{1,0:T(8,128)}, f32[192,1152]{1,0:T(8,128)}, bf16[4,192,1152]{2,1,0:T(8,128)(2,1)}, bf16[768,384]{1,0:T(8,128)(2,1)}, f32[1,1152]{1,0:T(...) custom-call(bf16[768,384]{1,0:T(8,128)(2,1)} %get-tuple-element.56.a, ...), custom_call_target="tpu_custom_call" | custom-call | tf_op jit(solution)/shard_map/feed/pallas_call | solution.py:653
  187.6 51.1 %attend_backward.1 = (bf16[768,384]{1,0:T(8,128)(2,1)}, bf16[4,768,256]{2,1,0:T(8,128)(2,1)}, bf16[4,288,384]{2,1,0:T(8,128)(2,1)}) custom-call(bf16[768,384]{1,0:T(8,128)(2,1)} %get-tuple-element.49.q_ref, bf16[3072,256]{1,0:T(8,128)(2,1)} %bitcast.13, f32[8,768]{1,0:T(8,128)} %get-tuple-element.51.qm_ref, f32[3072,128]{1,0:T(8,128)} %get-tuple-element.52.kp_ref, ...), custom_call_target="tpu_custom_call" | custom-call | tf_op jit(solution)/shard_map/attend_backward/pallas_call | solution.py:344
  238.7 72.3 %finish.1 = (bf16[192,1152]{1,0:T(8,128)(2,1)}, f32[192,1152]{1,0:T(8,128)}, bf16[4,72,384]{2,1,0:T(8,128)(2,1)}, bf16[4,72,256]{2,1,0:T(8,128)(2,1)}, bf16[2,72...) custom-call(bf16[768,384]{1,0:T(8,128)(2,1)} %get-tuple-element.61.q, ...), custom_call_target="tpu_custom_call" | custom-call | tf_op jit(solution)/shard_map/finish/pallas_call | solution.py:1140
  311.1 1.3 slice_bitcast_fusion
  312.3 4.2 %wrap.1 = (bf16[192,1152]{1,0:T(8,128)(2,1)}, f32[192,1152]{1,0:T(8,128)}, f32[72,1920]{1,0:T(8,128)}, f32[72,1152]{1,0:T(8,128)}, f32[72,6144]{1,0:T(8,128)}, /*index=5*/f32[192,1152]{1,0:T(8,128)}) custom-call(bf16[192,1152]{1,0:T(8,128)(2,1)} %get-tuple-element.75.act_in, f32[192,1152]{1,0:T(8,128)} %get-tuple-element.76.ig_in, ...), custom_call_target="tpu_custom_call" | custom-call | tf_op jit(solution)/shard_map/wrap/pallas_call | solution.py:1217

commit v7 on v6

--- a/solution.py
+++ b/solution.py
@@ -148,18 +148,22 @@
             k_tile = kv_ref[pl.ds(start, TK), :128]
             v_tile = kv_ref[pl.ds(start, TK), 128:]
             seen = visible(kp_ref, ks_ref, qm_ref, start)
+            scores = [
+                jnp.where(seen, dot_general(k_tile, heads[j], 1, 1), -1e30) for j in range(5)
+            ]
+            old = [top[j : j + 1, :] for j in range(5)]
+            new = [
+                jnp.maximum(old[j], jnp.max(scores[j], axis=0, keepdims=True)) for j in range(5)
+            ]
+            expons = [jnp.exp(scores[j] - new[j]) for j in range(5)]
+            shrink = [jnp.exp(old[j] - new[j]) for j in range(5)]
+            mixed = [dot_general(v_tile, expons[j].astype(BF), 0, 0) for j in range(5)]
             for j in range(5):
-                scores = dot_general(k_tile, heads[j], 1, 1)
-                scores = jnp.where(seen, scores, -1e30)
-                old = top[j : j + 1, :]
-                new = jnp.maximum(old, jnp.max(scores, axis=0, keepdims=True))
-                expons = jnp.exp(scores - new)
-                shrink = jnp.exp(old - new)
-                tot[j : j + 1, :] = tot[j : j + 1, :] * shrink + jnp.sum(
-                    expons, axis=0, keepdims=True
+                tot[j : j + 1, :] = tot[j : j + 1, :] * shrink[j] + jnp.sum(
+                    expons[j], axis=0, keepdims=True
                 )
-                acc[j] = acc[j] * shrink + dot_general(v_tile, expons.astype(BF), 0, 0)
-                top[j : j + 1, :] = new
+                acc[j] = acc[j] * shrink[j] + mixed[j]
+                top[j : j + 1, :] = new[j]
 
         for j, (b, h) in enumerate(HEAD_SLOTS):
             out = acc[j] / tot[j : j + 1, :]
@@ -243,7 +247,7 @@
     def kernel(
         q_ref, kv_ref, qm_ref, kp_ref, ks_ref, lse_ref, o_ref, do_ref, rows_ref,
         dq_ref, got_kv, got_rows,
-        acc, heads, grads, delta, kv_send, bounce, send, recv, kv_out, kv_in, near,
+        acc, heads, grads, delta, marks, lses, k_sum, v_sum, kv_send, bounce, send, recv, kv_out, kv_in, near,
     ):
         wires = Wires(send, recv)
         my_c = lax.axis_index("ctx")
@@ -259,6 +263,8 @@
         delta[...] = jnp.zeros_like(delta)
         for i in range(steps):
             at = slice(i * TQ, i * TQ + TQ)
+            marks[i] = qm_ref[:, at]
+            lses[i] = lse_ref[:, at]
             for j, (b, h) in enumerate(HEAD_SLOTS):
                 lanes = slice(128 * b, 128 * b + 128)
                 heads[i, j] = head_block(q_ref[at, lanes], h)
@@ -281,25 +287,31 @@
                 v_tile = kv_ref[at, 128:]
                 key_pos = jnp.tile(kp_ref[at, :], (1, TQ // 128))
                 key_seg = jnp.tile(ks_ref[at, :], (1, TQ // 128))
-                k_sum = jnp.zeros((BK, 128), F32)
-                v_sum = jnp.zeros((BK, 128), F32)
-                for i in range(steps):
-                    cols = slice(i * TQ, i * TQ + TQ)
-                    seen = (key_pos <= qm_ref[0:1, cols]) & (
-                        (key_seg == 0) | (key_seg == qm_ref[1:2, cols])
+                k_sum[...] = jnp.zeros_like(k_sum)
+                v_sum[...] = jnp.zeros_like(v_sum)
+
+                @pl.loop(0, steps)
+                def _(i):
+                    seen = (key_pos <= marks[i, 0:1, :]) & (
+                        (key_seg == 0) | (key_seg == marks[i, 1:2, :])
                     )
+                    k_part = jnp.zeros((BK, 128), F32)
+                    v_part = jnp.zeros((BK, 128), F32)
                     for j in range(5):
                         scores = dot_general(k_tile, heads[i, j], 1, 1)
-                        probs = jnp.where(seen, jnp.exp(scores - lse_ref[j : j + 1, cols]), 0.0)
+                        probs = jnp.where(seen, jnp.exp(scores - lses[i, j : j + 1, :]), 0.0)
                         prob_grad = dot_general(v_tile, grads[i, j], 1, 1)
                         score_grad = (probs * (prob_grad - delta[i, j : j + 1, :])).astype(BF)
-                        v_sum += jnp.dot(
+                        v_part += jnp.dot(
                             probs.astype(BF), grads[i, j], preferred_element_type=F32
                         )
-                        k_sum += jnp.dot(score_grad, heads[i, j], preferred_element_type=F32)
+                        k_part += jnp.dot(score_grad, heads[i, j], preferred_element_type=F32)
                         acc[i, j] += dot_general(k_tile, score_grad, 0, 0)
-                kv_send[chunk, pl.ds(inner, BK), :128] = k_sum.astype(BF)
-                kv_send[chunk, pl.ds(inner, BK), 128:] = v_sum.astype(BF)
+                    k_sum[...] += k_part
+                    v_sum[...] += v_part
+
+                kv_send[chunk, pl.ds(inner, BK), :128] = k_sum[...].astype(BF)
+                kv_send[chunk, pl.ds(inner, BK), 128:] = v_sum[...].astype(BF)
 
             @pl.when(d < ctx - 1)
             def _():
@@ -356,6 +368,10 @@
             pltpu.VMEM((steps, 5, TQ, 128), BF),
             pltpu.VMEM((steps, 5, TQ, 128), BF),
             pltpu.VMEM((steps, 8, TQ), F32),
+            pltpu.VMEM((steps, 8, TQ), F32),
+            pltpu.VMEM((steps, 8, TQ), F32),
+            pltpu.VMEM((BK, 128), F32),
+            pltpu.VMEM((BK, 128), F32),
             pltpu.VMEM((ctx, span, 256), BF),
             pltpu.VMEM(send_rows.shape[1:], BF),
             pltpu.SemaphoreType.DMA((ctx,)),
@@ -736,8 +752,6 @@
         tokens_in = x_ref[...].astype(F32)
         factor = lax.rsqrt(jnp.mean(tokens_in * tokens_in, axis=-1, keepdims=True) + EPSILON)
         n_ref[own] = (tokens_in * factor * g_ref[0:1, :]).astype(BF)
-        gather = SquareGather(wires, n_ref)
-        gather.begin()
         wq_ref[own] = cols[own]
         dy_ref[own] = up_ref[...]
 
@@ -759,13 +773,12 @@
             angles = upright(marks_all[my_c, w, 0:1, :])[:own_rows] * frequency
             c_ref[at, :] = jnp.cos(angles)
             s_ref[at, :] = jnp.sin(angles) * sign
-        gather.relay()
         forward = []
         for p, copy in zip((x, y, z), w_copies):
             copy.wait()
             forward.append(wires.start(wq_ref.at[p, side], wq_ref.at[p, side], sibling))
-        dy_gather = SquareGather(wires, dy_ref)
-        dy_gather.begin()
+        gather = SquareGather(wires, n_ref)
+        gather.begin()
         for copy in forward:
             copy.wait()
 
@@ -791,6 +804,9 @@
                 )
 
         block(own)
+        gather.relay()
+        dy_gather = SquareGather(wires, dy_ref)
+        dy_gather.begin()
         gather.wait_x()
         block(x)
         gather.wait_y()

time: 323 us -> 297 us (0.920); the launches traced: 317 us -> 296 us
  Pallas kernels: 311 us -> 290 us
    pallas_call x1, Pallas kernels: 46.5 us -> 31.4 us  [attend_forward(): pl.pallas_call(kernel, name='attend_forward', grid=(steps,), in_specs=[pl...]
    pallas_call x1, Pallas kernels: 63.9 us -> 58.6 us  [head(): pl.pallas_call(kernel, name='head', in_specs=[vmem] * len(operands), out_...]
where the time goes in v7:
time: 297 us; the launch traced here: 296 us
  Pallas kernels  290 us (98%)
    pallas_call x1, Pallas kernels, feed(): pl.pallas_call(kernel, name='feed', in_specs=[vmem] * len(operands), out_...  71.7 us
    pallas_call x1, Pallas kernels, finish(): pl.pallas_call(kernel, name='finish', in_specs=[vmem] * len(operands), ou...  70.3 us
    pallas_call x1, Pallas kernels, head(): pl.pallas_call(kernel, name='head', in_specs=[vmem] * len(operands), out_...  58.6 us
    pallas_call x1, Pallas kernels, attend_backward(): pl.pallas_call(kernel, name='attend_backward', in_specs=[vmem] * 8 + [any...  54 us
    pallas_call x1, Pallas kernels, attend_forward(): pl.pallas_call(kernel, name='attend_forward', grid=(steps,), in_specs=[pl...  31.4 us

profile of v7, /device:TPU:0, one launch (start us, length us, event | category | flops | bytes accessed | tf_op | source)
XLA Modules:
  0.0 295.5 jit_solution(14430273585000922741)
XLA Ops:
  0.6 1.3 add_convert_fusion.m_ref
  1.9 0.7 stack.18
  2.6 0.7 stack.19
  3.3 0.6 pad_maximum_fusion.g_ref
  3.9 58.6 %head.1 = (bf16[768,384]{1,0:T(8,128)(2,1)}, bf16[4,768,256]{2,1,0:T(8,128)(2,1)}, bf16[4,192,1152]{2,1,0:T(8,128)(2,1)}, bf16[4,288,640]{2,1,0:T(8,128)(2,1)}, ...) custom-call(bf16[192,1152]{1,0:T(8,128)(2,1)} %x_ref.5, ...), custom_call_target="tpu_custom_call" | custom-call | tf_op jit(solution)/shard_map/head/pallas_call | solution.py:838
  62.5 31.4 %attend_forward.1 = (bf16[768,384]{1,0:T(8,128)(2,1)}, f32[768,384]{1,0:T(8,128)}, f32[8,768]{1,0:T(8,128)}, bf16[4,288,768]{2,1,0:T(8,128)(2,1)}) custom-call(bf16[768,384]{1,0:T(8,128)(2,1)} %get-tuple-element.49.q_ref, bf16[3072,256]{1,0:T(8,128)(2,1)} %bitcast.12, f32[8,768]{1,0:T(8,128)} %get-tuple-element.51.qm_ref, ...), custom_call_target="tpu_custom_call" | custom-call | tf_op jit(solution)/shard_map/attend_forward/pallas_call | solution.py:188
  93.9 71.7 %feed.1 = (f32[192,1152]{1,0:T(8,128)}, f32[192,1152]{1,0:T(8,128)}, bf16[4,192,1152]{2,1,0:T(8,128)(2,1)}, bf16[768,384]{1,0:T(8,128)(2,1)}, f32[1,1152]{1,0:T(...) custom-call(bf16[768,384]{1,0:T(8,128)(2,1)} %get-tuple-element.56.a, ...), custom_call_target="tpu_custom_call" | custom-call | tf_op jit(solution)/shard_map/feed/pallas_call | solution.py:669
  165.7 54.0 %attend_backward.1 = (bf16[768,384]{1,0:T(8,128)(2,1)}, bf16[4,768,256]{2,1,0:T(8,128)(2,1)}, bf16[4,288,384]{2,1,0:T(8,128)(2,1)}) custom-call(bf16[768,384]{1,0:T(8,128)(2,1)} %get-tuple-element.49.q_ref, bf16[3072,256]{1,0:T(8,128)(2,1)} %bitcast.13, f32[8,768]{1,0:T(8,128)} %get-tuple-element.51.qm_ref, f32[3072,128]{1,0:T(8,128)} %get-tuple-element.52.kp_ref, ...), custom_call_target="tpu_custom_call" | custom-call | tf_op jit(solution)/shard_map/attend_backward/pallas_call | solution.py:356
  219.6 70.3 %finish.1 = (bf16[192,1152]{1,0:T(8,128)(2,1)}, f32[192,1152]{1,0:T(8,128)}, bf16[4,72,384]{2,1,0:T(8,128)(2,1)}, bf16[4,72,256]{2,1,0:T(8,128)(2,1)}, bf16[2,72...) custom-call(bf16[768,384]{1,0:T(8,128)(2,1)} %get-tuple-element.61.q, ...), custom_call_target="tpu_custom_call" | custom-call | tf_op jit(solution)/shard_map/finish/pallas_call | solution.py:1156
  290.0 1.3 slice_bitcast_fusion
  291.3 4.2 %wrap.1 = (bf16[192,1152]{1,0:T(8,128)(2,1)}, f32[192,1152]{1,0:T(8,128)}, f32[72,1920]{1,0:T(8,128)}, f32[72,1152]{1,0:T(8,128)}, f32[72,6144]{1,0:T(8,128)}, /*index=5*/f32[192,1152]{1,0:T(8,128)}) custom-call(bf16[192,1152]{1,0:T(8,128)(2,1)} %get-tuple-element.75.act_in, f32[192,1152]{1,0:T(8,128)} %get-tuple-element.76.ig_in, ...), custom_call_target="tpu_custom_call" | custom-call | tf_op jit(solution)/shard_map/wrap/pallas_call | solution.py:1233

commit v8 on v7

--- a/solution.py
+++ b/solution.py
@@ -84,7 +84,6 @@
 
 
 TQ = 256
-TK = 512
 
 
 def head_block(block, head):
@@ -92,144 +91,9 @@
     return jnp.where(low if head == 0 else jnp.logical_not(low), block, jnp.zeros_like(block))
 
 
-def visible(kp_ref, ks_ref, qm_ref, start):
-    key_pos = jnp.tile(kp_ref[pl.ds(start, TK), :], (1, TQ // 128))
-    key_seg = jnp.tile(ks_ref[pl.ds(start, TK), :], (1, TQ // 128))
-    return (key_pos <= qm_ref[0:1, :]) & ((key_seg == 0) | (key_seg == qm_ref[1:2, :]))
-
-
 ODD_ROWS = [(96, 32), (192, 64), (0, 64), (128, 64), (256, 64)]
 EVEN_ROWS = [(0, 64), (128, 64), (256, 64), (64, 64), (192, 32)]
 HEAD_SLOTS = [(0, 0), (0, 1), (1, 0), (1, 1), (2, 0)]
-
-
-def attend_forward(link, q, kv, q_marks, k_pos, k_seg, gate_up):
-    rows, keys = q.shape[0], kv.shape[0]
-    steps = rows // TQ
-    wsh = link.sizes["wsh"]
-    units = FF // wsh
-    peers = link.offsets(("wsh",))
-
-    def kernel(
-        q_ref, kv_ref, qm_ref, kp_ref, ks_ref, gu_ref,
-        a_ref, o_ref, lse_ref, wh_ref,
-        acc, top, tot, bounce, send, recv, near,
-    ):
-        def columns(p):
-            left = lax.axis_index("grp") * FF + p * units
-            return gu_ref.at[:, pl.ds(pl.multiple_of(left, 128), units)]
-
-        wires = Wires(send, recv)
-        _, me = link.place(("wsh",), peers[0])
-        copies = []
-        for offset in peers[1:]:
-            where, index = link.place(("wsh",), offset)
-            copies.append(wires.copy(columns(index), wh_ref.at[me], where))
-        inward = pltpu.make_async_copy(columns(me), bounce, near)
-        outward = pltpu.make_async_copy(bounce, wh_ref.at[me], near)
-
-        @pl.when(pl.program_id(0) == 0)
-        def _():
-            greet([link.place(("wsh",), offset)[0] for offset in peers[1:]])
-            for copy in copies:
-                copy.start()
-            inward.start()
-            inward.wait()
-            outward.start()
-
-        acc[...] = jnp.zeros_like(acc)
-        top[...] = jnp.full_like(top, -1e30)
-        tot[...] = jnp.zeros_like(tot)
-        heads = [head_block(q_ref[:, 128 * b : 128 * b + 128], h) for b, h in HEAD_SLOTS]
-
-        @pl.loop(0, keys // TK)
-        def _(t):
-            start = pl.multiple_of(t * TK, TK)
-            k_tile = kv_ref[pl.ds(start, TK), :128]
-            v_tile = kv_ref[pl.ds(start, TK), 128:]
-            seen = visible(kp_ref, ks_ref, qm_ref, start)
-            scores = [
-                jnp.where(seen, dot_general(k_tile, heads[j], 1, 1), -1e30) for j in range(5)
-            ]
-            old = [top[j : j + 1, :] for j in range(5)]
-            new = [
-                jnp.maximum(old[j], jnp.max(scores[j], axis=0, keepdims=True)) for j in range(5)
-            ]
-            expons = [jnp.exp(scores[j] - new[j]) for j in range(5)]
-            shrink = [jnp.exp(old[j] - new[j]) for j in range(5)]
-            mixed = [dot_general(v_tile, expons[j].astype(BF), 0, 0) for j in range(5)]
-            for j in range(5):
-                tot[j : j + 1, :] = tot[j : j + 1, :] * shrink[j] + jnp.sum(
-                    expons[j], axis=0, keepdims=True
-                )
-                acc[j] = acc[j] * shrink[j] + mixed[j]
-                top[j : j + 1, :] = new[j]
-
-        for j, (b, h) in enumerate(HEAD_SLOTS):
-            out = acc[j] / tot[j : j + 1, :]
-            acc[j] = out
-        lse_ref[...] = top[...] + jnp.log(jnp.maximum(tot[...], 1e-37))
-        low = lax.broadcasted_iota(jnp.int32, (TQ, 128), 1) < 64
-        for b in range(3):
-            first = acc[2 * b].T
-            if b < 2:
-                block = jnp.where(low, first, acc[2 * b + 1].T)
-            else:
-                block = jnp.where(low, first, 0.0)
-            o_ref[:, 128 * b : 128 * b + 128] = block
-            a_ref[:, 128 * b : 128 * b + 128] = block.astype(BF)
-
-        @pl.when(pl.program_id(0) == steps - 1)
-        def _():
-            outward.wait()
-            for copy in copies:
-                copy.wait()
-
-    return pl.pallas_call(
-        kernel,
-        name="attend_forward",
-        grid=(steps,),
-        in_specs=[
-            pl.BlockSpec((TQ, 384), lambda i: (i, 0)),
-            pl.BlockSpec((keys, 256), lambda i: (0, 0)),
-            pl.BlockSpec((8, TQ), lambda i: (0, i)),
-            pl.BlockSpec((keys, 128), lambda i: (0, 0)),
-            pl.BlockSpec((keys, 128), lambda i: (0, 0)),
-            pl.BlockSpec(memory_space=pl.ANY),
-        ],
-        out_specs=[
-            pl.BlockSpec((TQ, 384), lambda i: (i, 0)),
-            pl.BlockSpec((TQ, 384), lambda i: (i, 0)),
-            pl.BlockSpec((8, TQ), lambda i: (0, i)),
-            pl.BlockSpec(memory_space=pl.ANY),
-        ],
-        out_shape=[
-            jax.ShapeDtypeStruct((rows, 384), BF),
-            jax.ShapeDtypeStruct((rows, 384), F32),
-            jax.ShapeDtypeStruct((8, rows), F32),
-            jax.ShapeDtypeStruct((wsh, gate_up.shape[0], units), BF),
-        ],
-        scratch_shapes=[
-            pltpu.VMEM((5, 128, TQ), F32),
-            pltpu.VMEM((8, TQ), F32),
-            pltpu.VMEM((8, TQ), F32),
-            pltpu.VMEM((gate_up.shape[0], units), BF),
-            pltpu.SemaphoreType.DMA((wsh,)),
-            pltpu.SemaphoreType.DMA((wsh,)),
-            pltpu.SemaphoreType.DMA,
-        ],
-        compiler_params=pltpu.CompilerParams(
-            collective_id=2, has_side_effects=True, vmem_limit_bytes=VMEM_LIMIT
-        ),
-    )(q, kv, q_marks, k_pos, k_seg, gate_up)
-
-
-def owner_of(link):
-    ctx, wsh = link.sizes["ctx"], link.sizes["wsh"]
-    my_c, my_w = lax.axis_index("ctx"), lax.axis_index("wsh")
-    shard = my_w * ctx + my_c
-    to_c, to_w = shard // wsh, lax.rem(shard, wsh)
-    return {"ctx": to_c, "wsh": to_w}, jnp.logical_and(to_c == my_c, to_w == my_w)
 
 
 BK = 384
@@ -649,11 +513,13 @@
             gs_ref[c] = both[:, : units // 2]
             gl_ref[c] = both[:, units // 2 :]
         branch.relay()
-        for slot in range(wsh):
-            at = slice(slot * own_rows, slot * own_rows + own_rows)
+
+        @pl.loop(0, wsh)
+        def _(slot):
             dp_ref[slot] = jnp.dot(
-                hidden[at, :], dw_ref[...], preferred_element_type=F32
+                hidden[rows_of(slot), :], dw_ref[...], preferred_element_type=F32
             ).astype(BF)
+
         branch.wait_x()
         outward(x)
         branch.wait_y()
@@ -705,16 +571,20 @@
     )(*operands)
 
 
-def head(link, tokens, gain, weight, marks, upstream):
+def head(link, tokens, gain, weight, marks, upstream, gate_up):
     ctx, wsh = link.sizes["ctx"], link.sizes["wsh"]
     own_rows = tokens.shape[0]
     plane, group = own_rows * wsh, own_rows * wsh * ctx
     half = weight.shape[0] // 2
+    units = FF // wsh
+    steps = plane // TQ
 
     def kernel(
-        x_ref, g_ref, w_ref, m_ref, up_ref,
+        x_ref, g_ref, w_ref, m_ref, up_ref, gu_ref,
         q_ref, kv_ref, n_ref, wq_ref, kpos_ref, kseg_ref, q_marks, dy_ref, c_ref, s_ref,
-        cols, mine, marks_all, send, recv,
+        a_ref, o_ref, lse_ref, wh_ref,
+        cols, mine, marks_all, heads, tile_marks, acc, top, tot, bounce, send, recv, kv_out, kv_in,
+        near,
     ):
         wires = Wires(send, recv)
         core = lax.axis_index("grp")
@@ -783,9 +653,19 @@
             copy.wait()
 
         low = lax.rem(lax.broadcasted_iota(jnp.int32, (own_rows, 128), 1), 64) < 32
-        kv_copies = []
-
-        def block(slot):
+
+        def kv_copy(slot, order, d, to):
+            at = pl.ds(pl.multiple_of(slot * own_rows, 16), own_rows)
+            return pltpu.make_async_remote_copy(
+                kv_ref.at[my_c, at],
+                kv_ref.at[my_c, at],
+                kv_out.at[order, d],
+                kv_in.at[order, d],
+                device_id={"ctx": to},
+                device_id_type=MESH,
+            )
+
+        def block(slot, order):
             at = pl.ds(pl.multiple_of(slot * own_rows, 16), own_rows)
             full = jnp.dot(
                 n_ref[slot], wq_ref[...].reshape(D, 640), preferred_element_type=F32
@@ -798,27 +678,37 @@
                 ).astype(BF)
             kv_ref[my_c, at, :128] = turn(full[:, 384:512], cos_t, sin_t, low).astype(BF)
             kv_ref[my_c, at, 128:] = full[:, 512:].astype(BF)
-            for where, _ in levels:
-                kv_copies.append(
-                    wires.start(kv_ref.at[my_c, at], kv_ref.at[my_c, at], where)
-                )
-
-        block(own)
+            for d, (_, index) in enumerate(levels):
+                kv_copy(slot, order, d, index).start()
+
+        block(own, 0)
         gather.relay()
         dy_gather = SquareGather(wires, dy_ref)
         dy_gather.begin()
         gather.wait_x()
-        block(x)
+        block(x, 1)
         gather.wait_y()
-        block(y)
+        block(y, 2)
         gather.wait_z()
-        block(z)
+        block(z, 3)
         dy_gather.relay()
 
-        for copy in level_copies:
-            copy.wait()
+        def columns(p):
+            left = core * FF + p * units
+            return gu_ref.at[:, pl.ds(pl.multiple_of(left, 128), units)]
+
+        gate_copies = []
+        for p in (x, y, z):
+            gate_copies.append(wires.start(columns(p), wh_ref.at[own], {"wsh": p}))
+        inward = pltpu.make_async_copy(columns(own), bounce, near)
+        outward = pltpu.make_async_copy(bounce, wh_ref.at[own], near)
+        inward.start()
+
         for w in range(wsh):
             q_marks[:, w * own_rows : w * own_rows + own_rows] = marks_all[my_c, w, :, :own_rows]
+
+        for copy in level_copies:
+            copy.wait()
 
         @pl.loop(0, ctx)
         def _(c):
@@ -827,19 +717,81 @@
                 kpos_ref[at, :] = upright(marks_all[c, w, 0:1, :])[:own_rows]
                 kseg_ref[at, :] = upright(marks_all[c, w, 1:2, :])[:own_rows]
 
+        inward.wait()
+        outward.start()
+
+        acc[...] = jnp.zeros_like(acc)
+        top[...] = jnp.full_like(top, -1e30)
+        tot[...] = jnp.zeros_like(tot)
+        for i in range(steps):
+            at = slice(i * TQ, i * TQ + TQ)
+            tile_marks[i] = q_marks[:, at]
+            for j, (b, side_of) in enumerate(HEAD_SLOTS):
+                heads[i, j] = head_block(q_ref[at, 128 * b : 128 * b + 128], side_of)
+
+        @pl.loop(0, ctx)
+        def _(d):
+            chunk = lax.rem(my_c + ctx - d, ctx)
+
+            @pl.when(d > 0)
+            def _():
+                for order in range(wsh):
+                    kv_copy(0, order, d - 1, my_c).wait()
+
+            at = pl.ds(pl.multiple_of(chunk * plane, 128), plane)
+            k_tile = kv_ref[chunk, :, :128]
+            v_tile = kv_ref[chunk, :, 128:]
+            key_pos = jnp.tile(kpos_ref[at, :], (1, TQ // 128))
+            key_seg = jnp.tile(kseg_ref[at, :], (1, TQ // 128))
+
+            @pl.loop(0, steps)
+            def _(i):
+                seen = (key_pos <= tile_marks[i, 0:1, :]) & (
+                    (key_seg == 0) | (key_seg == tile_marks[i, 1:2, :])
+                )
+                scores = [
+                    jnp.where(seen, dot_general(k_tile, heads[i, j], 1, 1), -1e30)
+                    for j in range(5)
+                ]
+                old = [top[i, j : j + 1, :] for j in range(5)]
+                new = [
+                    jnp.maximum(old[j], jnp.max(scores[j], axis=0, keepdims=True))
+                    for j in range(5)
+                ]
+                expons = [jnp.exp(scores[j] - new[j]) for j in range(5)]
+                shrink = [jnp.exp(old[j] - new[j]) for j in range(5)]
+                mixed = [dot_general(v_tile, expons[j].astype(BF), 0, 0) for j in range(5)]
+                for j in range(5):
+                    tot[i, j : j + 1, :] = tot[i, j : j + 1, :] * shrink[j] + jnp.sum(
+                        expons[j], axis=0, keepdims=True
+                    )
+                    acc[i, j] = acc[i, j] * shrink[j] + mixed[j]
+                    top[i, j : j + 1, :] = new[j]
+
+        half_lanes = lax.broadcasted_iota(jnp.int32, (TQ, 128), 1) < 64
+        for i in range(steps):
+            at = slice(i * TQ, i * TQ + TQ)
+            lse_ref[:, at] = top[i] + jnp.log(jnp.maximum(tot[i], 1e-37))
+            outs = [(acc[i, j] / tot[i, j : j + 1, :]).T for j in range(5)] + [0.0]
+            for b in range(3):
+                block_out = jnp.where(half_lanes, outs[2 * b], outs[2 * b + 1])
+                o_ref[at, 128 * b : 128 * b + 128] = block_out
+                a_ref[at, 128 * b : 128 * b + 128] = block_out.astype(BF)
+
         dy_gather.wait_x()
         dy_gather.wait_y()
         dy_gather.wait_z()
-        for copy in kv_copies:
-            copy.wait()
-
-    operands = (tokens, gain, weight, marks, upstream)
+        for copy in gate_copies:
+            copy.wait()
+        outward.wait()
+
+    operands = (tokens, gain, weight, marks, upstream, gate_up)
     vmem = pl.BlockSpec(memory_space=pltpu.VMEM)
     return pl.pallas_call(
         kernel,
         name="head",
-        in_specs=[vmem] * len(operands),
-        out_specs=[vmem] * 10,
+        in_specs=[vmem] * 5 + [pl.BlockSpec(memory_space=pl.ANY)],
+        out_specs=[vmem] * 13 + [pl.BlockSpec(memory_space=pl.ANY)],
         out_shape=[
             jax.ShapeDtypeStruct((plane, 384), BF),
             jax.ShapeDtypeStruct((ctx, plane, 256), BF),
@@ -851,13 +803,26 @@
             jax.ShapeDtypeStruct((wsh, own_rows, D), BF),
             jax.ShapeDtypeStruct((plane, 128), F32),
             jax.ShapeDtypeStruct((plane, 128), F32),
+            jax.ShapeDtypeStruct((plane, 384), BF),
+            jax.ShapeDtypeStruct((plane, 384), F32),
+            jax.ShapeDtypeStruct((8, plane), F32),
+            jax.ShapeDtypeStruct((wsh, 2 * half, units), BF),
         ],
         scratch_shapes=[
             pltpu.VMEM((wsh, 2 * half, 640), BF),
             pltpu.VMEM((8, 256), F32),
             pltpu.VMEM((ctx, wsh, 8, 256), F32),
-            pltpu.SemaphoreType.DMA((5 * ctx + 24,)),
-            pltpu.SemaphoreType.DMA((5 * ctx + 24,)),
+            pltpu.VMEM((steps, 5, TQ, 128), BF),
+            pltpu.VMEM((steps, 8, TQ), F32),
+            pltpu.VMEM((steps, 5, 128, TQ), F32),
+            pltpu.VMEM((steps, 8, TQ), F32),
+            pltpu.VMEM((steps, 8, TQ), F32),
+            pltpu.VMEM((2 * half, units), BF),
+            pltpu.SemaphoreType.DMA((ctx + 28,)),
+            pltpu.SemaphoreType.DMA((ctx + 28,)),
+            pltpu.SemaphoreType.DMA((wsh, ctx)),
+            pltpu.SemaphoreType.DMA((wsh, ctx)),
+            pltpu.SemaphoreType.DMA,
         ],
         compiler_params=pltpu.CompilerParams(
             collective_id=1, has_side_effects=True, vmem_limit_bytes=VMEM_LIMIT
@@ -880,6 +845,7 @@
     peers = link.offsets(axes)
     gate_width = gate_got.shape[2]
     down_rows = down_got.shape[0]
+    piece = down_rows // wsh
 
     def kernel(
         q_ref, kv_ref, w_ref, c_ref, s_ref, n_ref, x_ref, g_ref, mg_ref, gate_ref, down_ref,
@@ -887,7 +853,7 @@
         act_ref, ig_ref, q_fin, kv_fin, out_fin, gate_fin, late_fin, down_fin, gains_out,
         pg, parts, near, total, near2, total2, wide, q_own, q_pair, q_send, q_got,
         q_mid, kv_own, kv_pair, kv_go, kv_got, kv_mid, gate_mid, late_got,
-        late_mid, out_halves,
+        late_mid, spread, spread_got, risen, landed, out_halves,
         out_pair, out_send, out_mid, out_got, gains, gains_got, gains_fin,
         send, recv,
     ):
@@ -925,14 +891,12 @@
         for where, index in levels:
             late_copies.append(wires.start(late_ref.at[index], late_got.at[my_c], where))
 
-        owner, stays = owner_of(link)
-        moves = jnp.logical_not(stays)
-        down_move = wires.copy(down_ref, down_fin.at[core], owner)
-        begin(moves, down_move)
-
-        @pl.when(stays)
-        def _():
-            down_fin[core] = down_ref[...]
+        for p in range(wsh):
+            spread[p] = down_ref[p * piece : p * piece + piece, :]
+        spread_moves = in_plane(spread, lambda w: spread_got.at[w])
+        for copy in spread_moves:
+            copy.start()
+        spread_got[my_w] = spread[my_w]
 
         low = lax.rem(lax.broadcasted_iota(jnp.int32, (own_rows, 128), 1), 64) < 32
         scatter = SquareScatter(wires, parts, near, total)
@@ -959,6 +923,41 @@
             elif slot is scatter.y:
                 scatter.send_y()
 
+        for copy in spread_moves:
+            copy.wait()
+        lane = lax.rem(my_c, wsh)
+        rise, arrive = wires.used, []
+        wires.used += wsh
+        for p in range(wsh):
+            to = (p * ctx + my_c) // wsh
+            out_copy_p = pltpu.make_async_remote_copy(
+                spread_got.at[p],
+                risen.at[lane],
+                send.at[rise + p],
+                recv.at[rise + lane],
+                device_id={"ctx": to},
+                device_id_type=MESH,
+            )
+
+            @pl.when(to != my_c)
+            def _():
+                out_copy_p.start()
+
+            @pl.when(to == my_c)
+            def _():
+                risen[lane] = spread_got[p]
+
+            from_c = lax.rem(my_c, fold) * wsh + p
+            in_copy_p = pltpu.make_async_remote_copy(
+                spread_got.at[p],
+                risen.at[p],
+                send.at[rise + p],
+                recv.at[rise + p],
+                device_id={"ctx": to},
+                device_id_type=MESH,
+            )
+            arrive.append((out_copy_p, to != my_c, in_copy_p, from_c != my_c))
+
         strip = dot_general(n_ref[...], pg[:, 384:], 0, 0).astype(BF)
         for c in range(ctx):
             kv_own[c] = strip[c * chunk : c * chunk + chunk, :]
@@ -1062,11 +1061,20 @@
         out_got[my_c] = out_mid[my_c // fold, lax.rem(my_c, fold)]
 
 
-        @pl.when(moves)
-        def _():
-            down_move.wait()
-
-        down_copy = wires.start(down_fin.at[core], down_fin.at[core], sibling)
+        for out_copy_p, goes, in_copy_p, comes in arrive:
+
+            @pl.when(goes)
+            def _():
+                out_copy_p.wait_send()
+
+            @pl.when(comes)
+            def _():
+                in_copy_p.wait_recv()
+
+        land_moves = in_plane(risen, lambda w: landed.at[w])
+        for copy in land_moves:
+            copy.start()
+        landed[my_w] = risen[my_w]
         over_ctx(gate_ref, gate_mid)
         gate_moves = in_plane(gate_mid, lambda w: gate_fin.at[core, w])
         for copy in gate_moves:
@@ -1103,6 +1111,11 @@
                 copy.start()
             kv_fin[my_w] = kv_mid[my_w]
 
+        for copy in land_moves:
+            copy.wait()
+        for p in range(wsh):
+            down_fin[core, p * piece : p * piece + piece, :] = landed[p]
+        down_copy = wires.start(down_fin.at[core], down_fin.at[core], sibling)
         for copy in gate_moves + late_moves:
             copy.wait()
         gate_copy = wires.start(gate_fin.at[core], gate_fin.at[core], sibling)
@@ -1182,6 +1195,7 @@
             pltpu.VMEM((wsh, rows, gate_width), BF),
             pltpu.VMEM((ctx, chunk, gate_width), BF),
             pltpu.VMEM((wsh, rows, gate_width), BF),
+            *[pltpu.VMEM((wsh, piece, D), BF)] * 4,
             pltpu.VMEM((2, 288, 640), BF),
             pltpu.VMEM((288, 640), BF),
             pltpu.VMEM((wsh, fold, rows, 640), BF),
@@ -1280,13 +1294,14 @@
             dy_all,
             cos,
             sin,
-        ) = head(link, tokens, both_gains, query_key_value, marks, upstream)
+            attended,
+            attended_wide,
+            lse,
+            w_half,
+        ) = head(link, tokens, both_gains, query_key_value, marks, upstream, gate_up)
         kv_all = kv_all.reshape(group, 256)
         normed_all, dy_all = normed_all.reshape(plane, D), dy_all.reshape(plane, D)
         w_qkv = w_qkv.reshape(D, 640)
-        attended, attended_wide, lse, w_half = attend_forward(
-            link, queries, kv_all, q_marks, k_pos, k_seg, gate_up
-        )
         w_half = w_half.reshape(D, FF // wsh)
         (
             middle,

time: 297 us -> 277 us (0.933)
  Pallas kernels: 290 us -> 271 us
    pallas_call x2 -> x1, Pallas kernels: 90 us -> 71.5 us  [head(): pl.pallas_call(kernel, name='head', in_specs=[vmem] * 5 + [pl.BlockSpec(m...]
    pallas_call x1, Pallas kernels: 70.3 us -> 66 us  [finish(): pl.pallas_call(kernel, name='finish', in_specs=[vmem] * len(operands), ou...]
    pallas_call x1, Pallas kernels: 71.7 us -> 75.8 us  [feed(): pl.pallas_call(kernel, name='feed', in_specs=[vmem] * len(operands), out_...]
where the time goes in v8:
time: 277 us; the launch traced here: 276 us
  Pallas kernels  271 us (98%)
    pallas_call x1, Pallas kernels, feed(): pl.pallas_call(kernel, name='feed', in_specs=[vmem] * len(operands), out_...  75.8 us
    pallas_call x1, Pallas kernels, head(): pl.pallas_call(kernel, name='head', in_specs=[vmem] * 5 + [pl.BlockSpec(m...  71.5 us
    pallas_call x1, Pallas kernels, finish(): pl.pallas_call(kernel, name='finish', in_specs=[vmem] * len(operands), ou...  66 us
    pallas_call x1, Pallas kernels, attend_backward(): pl.pallas_call(kernel, name='attend_backward', in_specs=[vmem] * 8 + [any...  53 us

profile of v8, /device:TPU:0, one launch (start us, length us, event | category | flops | bytes accessed | tf_op | source)
XLA Modules:
  0.0 275.8 jit_solution(18336587037460724003)
XLA Ops:
  0.6 1.3 add_convert_fusion.m_ref
  1.9 0.7 stack.18
  2.6 0.7 stack.19
  3.3 0.6 pad_maximum_fusion.g_ref
  3.9 71.5 %head.1 = (bf16[768,384]{1,0:T(8,128)(2,1)}, bf16[4,768,256]{2,1,0:T(8,128)(2,1)}, bf16[4,192,1152]{2,1,0:T(8,128)(2,1)}, bf16[4,288,640]{2,1,0:T(8,128)(2,1)}, ...) custom-call(bf16[192,1152]{1,0:T(8,128)(2,1)} %x_ref.5, ...), custom_call_target="tpu_custom_call" | custom-call | tf_op jit(solution)/shard_map/head/pallas_call | solution.py:790
  75.4 75.8 %feed.1 = (f32[192,1152]{1,0:T(8,128)}, f32[192,1152]{1,0:T(8,128)}, bf16[4,192,1152]{2,1,0:T(8,128)(2,1)}, bf16[768,384]{1,0:T(8,128)(2,1)}, f32[1,1152]{1,0:T(...) custom-call(bf16[768,384]{1,0:T(8,128)(2,1)} %get-tuple-element.56.a, ...), custom_call_target="tpu_custom_call" | custom-call | tf_op jit(solution)/shard_map/feed/pallas_call | solution.py:535
  151.2 53.0 %attend_backward.1 = (bf16[768,384]{1,0:T(8,128)(2,1)}, bf16[4,768,256]{2,1,0:T(8,128)(2,1)}, bf16[4,288,384]{2,1,0:T(8,128)(2,1)}) custom-call(bf16[768,384]{1,0:T(8,128)(2,1)} %get-tuple-element.49.q_ref, bf16[3072,256]{1,0:T(8,128)(2,1)} %bitcast.16, f32[8,768]{1,0:T(8,128)} %get-tuple-element.51.qm_ref, f32[3072,128]{1,0:T(8,128)} %get-tuple-element.52.kp_ref, ...), custom_call_target="tpu_custom_call" | custom-call | tf_op jit(solution)/shard_map/attend_backward/pallas_call | solution.py:220
  204.3 66.0 %finish.1 = (bf16[192,1152]{1,0:T(8,128)(2,1)}, f32[192,1152]{1,0:T(8,128)}, bf16[4,72,384]{2,1,0:T(8,128)(2,1)}, bf16[4,72,256]{2,1,0:T(8,128)(2,1)}, bf16[2,72...) custom-call(bf16[768,384]{1,0:T(8,128)(2,1)} %get-tuple-element.61.q, ...), custom_call_target="tpu_custom_call" | custom-call | tf_op jit(solution)/shard_map/finish/pallas_call | solution.py:1169
  270.3 1.3 slice_bitcast_fusion
  271.6 4.2 %wrap.1 = (bf16[192,1152]{1,0:T(8,128)(2,1)}, f32[192,1152]{1,0:T(8,128)}, f32[72,1920]{1,0:T(8,128)}, f32[72,1152]{1,0:T(8,128)}, f32[72,6144]{1,0:T(8,128)}, /*index=5*/f32[192,1152]{1,0:T(8,128)}) custom-call(bf16[192,1152]{1,0:T(8,128)(2,1)} %get-tuple-element.75.act_in, f32[192,1152]{1,0:T(8,128)} %get-tuple-element.76.ig_in, ...), custom_call_target="tpu_custom_call" | custom-call | tf_op jit(solution)/shard_map/wrap/pallas_call | solution.py:1247

commit v9 on v8

--- a/solution.py
+++ b/solution.py
@@ -97,6 +97,7 @@
 
 
 BK = 384
+EARLY = 384
 
 
 def attend_backward(
@@ -161,16 +162,24 @@
                     )
                     k_part = jnp.zeros((BK, 128), F32)
                     v_part = jnp.zeros((BK, 128), F32)
+                    scores = [dot_general(k_tile, heads[i, j], 1, 1) for j in range(5)]
+                    back = [dot_general(v_tile, grads[i, j], 1, 1) for j in range(5)]
+                    probs = [
+                        jnp.where(seen, jnp.exp(scores[j] - lses[i, j : j + 1, :]), 0.0)
+                        for j in range(5)
+                    ]
+                    score_grad = [
+                        (probs[j] * (back[j] - delta[i, j : j + 1, :])).astype(BF)
+                        for j in range(5)
+                    ]
                     for j in range(5):
-                        scores = dot_general(k_tile, heads[i, j], 1, 1)
-                        probs = jnp.where(seen, jnp.exp(scores - lses[i, j : j + 1, :]), 0.0)
-                        prob_grad = dot_general(v_tile, grads[i, j], 1, 1)
-                        score_grad = (probs * (prob_grad - delta[i, j : j + 1, :])).astype(BF)
                         v_part += jnp.dot(
-                            probs.astype(BF), grads[i, j], preferred_element_type=F32
+                            probs[j].astype(BF), grads[i, j], preferred_element_type=F32
                         )
-                        k_part += jnp.dot(score_grad, heads[i, j], preferred_element_type=F32)
-                        acc[i, j] += dot_general(k_tile, score_grad, 0, 0)
+                        k_part += jnp.dot(
+                            score_grad[j], heads[i, j], preferred_element_type=F32
+                        )
+                        acc[i, j] += dot_general(k_tile, score_grad[j], 0, 0)
                     k_sum[...] += k_part
                     v_sum[...] += v_part
 
@@ -378,6 +387,7 @@
     units = down.shape[0]
     chunk = D // ctx
     pick = units // ctx // 2
+    early = EARLY
 
     def kernel(
         at_ref, ao_ref, x_ref, g_ref, wh_ref, dw_ref, dy_ref,
@@ -433,7 +443,7 @@
         middle = x_ref[...].astype(F32) + first.result()
         mid_ref[...] = middle
         factor = lax.rsqrt(jnp.mean(middle * middle, axis=-1, keepdims=True) + EPSILON)
-        n2[own] = (middle * factor * g_ref[1:2, :]).astype(BF)
+        n2[own] = (middle * factor * g_ref[...].reshape(1, D)).astype(BF)
         gather = SquareGather(wires, n2)
         gather.begin()
         w_copy.wait()
@@ -490,7 +500,7 @@
         grad = second.result()
         middle = mid_ref[...]
         factor = lax.rsqrt(jnp.mean(middle * middle, axis=-1, keepdims=True) + EPSILON)
-        weighted = grad * g_ref[1:2, :]
+        weighted = grad * g_ref[...].reshape(1, D)
         inner = jnp.mean(weighted * middle, axis=-1, keepdims=True)
         middle_grad = (
             dy_ref[rows_of(own), :].astype(F32)
@@ -510,8 +520,8 @@
         gate_swap.wait()
         for c in range(ctx):
             both = (gate_h[core, c].astype(F32) + gate_pair[c].astype(F32)).astype(BF)
-            gs_ref[c] = both[:, : units // 2]
-            gl_ref[c] = both[:, units // 2 :]
+            gs_ref[c] = both[:, :early]
+            gl_ref[c] = both[:, early:]
         branch.relay()
 
         @pl.loop(0, wsh)
@@ -544,8 +554,8 @@
             jax.ShapeDtypeStruct((plane, 384), BF),
             jax.ShapeDtypeStruct((1, D), F32),
             jax.ShapeDtypeStruct((wsh, own_rows, D), BF),
-            jax.ShapeDtypeStruct((ctx, chunk, units // 2), BF),
-            jax.ShapeDtypeStruct((ctx, chunk, units // 2), BF),
+            jax.ShapeDtypeStruct((ctx, chunk, early), BF),
+            jax.ShapeDtypeStruct((ctx, chunk, units - early), BF),
             jax.ShapeDtypeStruct((pick, D), BF),
         ],
         scratch_shapes=[
@@ -571,7 +581,7 @@
     )(*operands)
 
 
-def head(link, tokens, gain, weight, marks, upstream, gate_up):
+def head(link, tokens, gain, weight, positions, segments, upstream, gate_up):
     ctx, wsh = link.sizes["ctx"], link.sizes["wsh"]
     own_rows = tokens.shape[0]
     plane, group = own_rows * wsh, own_rows * wsh * ctx
@@ -580,7 +590,7 @@
     steps = plane // TQ
 
     def kernel(
-        x_ref, g_ref, w_ref, m_ref, up_ref, gu_ref,
+        x_ref, g_ref, w_ref, pos_ref, seg_ref, up_ref, gu_ref,
         q_ref, kv_ref, n_ref, wq_ref, kpos_ref, kseg_ref, q_marks, dy_ref, c_ref, s_ref,
         a_ref, o_ref, lse_ref, wh_ref,
         cols, mine, marks_all, heads, tile_marks, acc, top, tot, bounce, send, recv, kv_out, kv_in,
@@ -596,7 +606,8 @@
             [{"wsh": x}, {"wsh": y}, {"wsh": z}, sibling] + [where for where, _ in levels]
         )
         mine[...] = jnp.zeros_like(mine)
-        mine[:2, :own_rows] = m_ref[...]
+        mine[0:1, :own_rows] = pos_ref[...].reshape(1, own_rows).astype(F32)
+        mine[1:2, :own_rows] = seg_ref[...].reshape(1, own_rows).astype(F32)
         mark_copies = []
         for p in (x, y, z):
             mark_copies.append(wires.start(mine, marks_all.at[my_c, own], {"wsh": p}))
@@ -621,7 +632,7 @@
             )
         tokens_in = x_ref[...].astype(F32)
         factor = lax.rsqrt(jnp.mean(tokens_in * tokens_in, axis=-1, keepdims=True) + EPSILON)
-        n_ref[own] = (tokens_in * factor * g_ref[0:1, :]).astype(BF)
+        n_ref[own] = (tokens_in * factor * g_ref[...].reshape(1, D)).astype(BF)
         wq_ref[own] = cols[own]
         dy_ref[own] = up_ref[...]
 
@@ -785,12 +796,12 @@
             copy.wait()
         outward.wait()
 
-    operands = (tokens, gain, weight, marks, upstream, gate_up)
+    operands = (tokens, gain, weight, positions, segments, upstream, gate_up)
     vmem = pl.BlockSpec(memory_space=pltpu.VMEM)
     return pl.pallas_call(
         kernel,
         name="head",
-        in_specs=[vmem] * 5 + [pl.BlockSpec(memory_space=pl.ANY)],
+        in_specs=[vmem] * 6 + [pl.BlockSpec(memory_space=pl.ANY)],
         out_specs=[vmem] * 13 + [pl.BlockSpec(memory_space=pl.ANY)],
         out_shape=[
             jax.ShapeDtypeStruct((plane, 384), BF),
@@ -843,7 +854,7 @@
     plane = normed.shape[0]
     axes = ("ctx", "wsh")
     peers = link.offsets(axes)
-    gate_width = gate_got.shape[2]
+    gate_width, late_width = gate_got.shape[2], gate_late.shape[2]
     down_rows = down_got.shape[0]
     piece = down_rows // wsh
 
@@ -1025,7 +1036,7 @@
             kv_got[my_c] = kv_go[my_c]
             q_swap.wait_send()
 
-        both = jnp.concatenate([gain_sum / g_ref[0:1, :], fs_ref[...]], axis=0)
+        both = jnp.concatenate([gain_sum / g_ref[...].reshape(1, D), fs_ref[...]], axis=0)
         gains[...] = jnp.zeros_like(gains)
         for s in range(shards):
             gains[s, :2, :rows] = both[:, rows * s : rows * s + rows]
@@ -1050,7 +1061,7 @@
         grad = scatter.result()
         x = x_ref[...].astype(F32)
         factor = lax.rsqrt(jnp.mean(x * x, axis=-1, keepdims=True) + EPSILON)
-        weighted = grad * g_ref[0:1, :]
+        weighted = grad * g_ref[...].reshape(1, D)
         inner = jnp.mean(weighted * x, axis=-1, keepdims=True)
         ig_ref[...] = mg_ref[...] + factor * weighted - x * (factor * factor * factor) * inner
         for copy in out_moves:
@@ -1178,7 +1189,7 @@
             jax.ShapeDtypeStruct((wsh, rows, 256), BF),
             jax.ShapeDtypeStruct((2, rows, 640), BF),
             jax.ShapeDtypeStruct((2, wsh, rows, gate_width), BF),
-            jax.ShapeDtypeStruct((2, wsh, rows, gate_width), BF),
+            jax.ShapeDtypeStruct((2, wsh, rows, late_width), BF),
             jax.ShapeDtypeStruct((2, down_rows, D), BF),
             jax.ShapeDtypeStruct((8, 128), F32),
         ],
@@ -1193,8 +1204,8 @@
             *[pltpu.VMEM((ctx, chunk, 256), BF)] * 4,
             pltpu.VMEM((wsh, rows, 256), BF),
             pltpu.VMEM((wsh, rows, gate_width), BF),
-            pltpu.VMEM((ctx, chunk, gate_width), BF),
-            pltpu.VMEM((wsh, rows, gate_width), BF),
+            pltpu.VMEM((ctx, chunk, late_width), BF),
+            pltpu.VMEM((wsh, rows, late_width), BF),
             *[pltpu.VMEM((wsh, piece, D), BF)] * 4,
             pltpu.VMEM((2, 288, 640), BF),
             pltpu.VMEM((288, 640), BF),
@@ -1213,15 +1224,17 @@
     )(*operands)
 
 
-def wrap(act, input_grad, q_sum, kv_sum, out_sum, gate_sum, late_sum, down_sum):
+def wrap(act, input_grad, q_sum, kv_sum, out_sum, gate_sum, late_sum, down_sum, gain_sum):
     wsh, rows, _ = q_sum.shape
     down_rows = down_sum.shape[1]
-    width = gate_sum.shape[3]
+    width, wide = gate_sum.shape[3], late_sum.shape[3]
 
     def kernel(
-        act_in, ig_in, q_in, kv_in, out_in, gate_in, late_in, down_in,
-        act_ref, ig_ref, qkv_ref, out_ref, gate_ref, down_ref,
+        act_in, ig_in, q_in, kv_in, out_in, gate_in, late_in, down_in, gain_in,
+        act_ref, ig_ref, qkv_ref, out_ref, gate_ref, down_ref, one_ref, two_ref,
     ):
+        one_ref[...] = gain_in[0:1, :rows].reshape(rows)
+        two_ref[...] = gain_in[1:2, :rows].reshape(rows)
         act_ref[...] = act_in[...]
         ig_ref[...] = ig_in[...]
         qkv_ref[...] = qkv_restore(
@@ -1235,10 +1248,10 @@
         )
         for half in range(2):
             for w in range(wsh):
-                left = (half * wsh + w) * 2 * width
+                left = (half * wsh + w) * (width + wide)
                 gate_ref[:, left : left + width] = gate_in[half, w].astype(F32)
                 left += width
-                gate_ref[:, left : left + width] = late_in[half, w].astype(F32)
+                gate_ref[:, left : left + wide] = late_in[half, w].astype(F32)
             down_ref[half * down_rows : half * down_rows + down_rows, :] = down_in[half].astype(
                 F32
             )
@@ -1247,8 +1260,8 @@
     return pl.pallas_call(
         kernel,
         name="wrap",
-        in_specs=[vmem] * 8,
-        out_specs=[vmem] * 6,
+        in_specs=[vmem] * 9,
+        out_specs=[vmem] * 8,
         out_shape=[
             jax.ShapeDtypeStruct(act.shape, BF),
             jax.ShapeDtypeStruct(act.shape, F32),
@@ -1256,9 +1269,11 @@
             jax.ShapeDtypeStruct((rows, D), F32),
             jax.ShapeDtypeStruct((rows, 2 * FF), F32),
             jax.ShapeDtypeStruct((2 * down_rows, D), F32),
+            jax.ShapeDtypeStruct((rows,), F32),
+            jax.ShapeDtypeStruct((rows,), F32),
         ],
         compiler_params=pltpu.CompilerParams(vmem_limit_bytes=VMEM_LIMIT),
-    )(act, input_grad, q_sum, kv_sum, out_sum, gate_sum, late_sum, down_sum)
+    )(act, input_grad, q_sum, kv_sum, out_sum, gate_sum, late_sum, down_sum, gain_sum)
 
 
 def build(sizes):
@@ -1281,8 +1296,6 @@
         own = tokens.shape[0]
         plane = own * wsh
         group = plane * ctx
-        marks = jnp.stack([positions, segment_ids]).astype(F32)
-        both_gains = jnp.stack([attend_gain, feed_gain])
         (
             queries,
             kv_all,
@@ -1298,7 +1311,9 @@
             attended_wide,
             lse,
             w_half,
-        ) = head(link, tokens, both_gains, query_key_value, marks, upstream, gate_up)
+        ) = head(
+            link, tokens, attend_gain, query_key_value, positions, segment_ids, upstream, gate_up
+        )
         kv_all = kv_all.reshape(group, 256)
         normed_all, dy_all = normed_all.reshape(plane, D), dy_all.reshape(plane, D)
         w_qkv = w_qkv.reshape(D, 640)
@@ -1313,28 +1328,17 @@
             gate_send,
             gate_late,
             down_sum,
-        ) = feed(link, attended, attend_out, tokens, both_gains, w_half, down_weight, dy_all)
+        ) = feed(link, attended, attend_out, tokens, feed_gain, w_half, down_weight, dy_all)
         q_grad, kv_grad, gate_got = attend_backward(
             link, queries, kv_all, q_marks, k_pos, k_seg, lse, attended_wide, attended_grad,
             gate_send,
         )
-        *sums, gain_out = finish(
+        sums = finish(
             link, q_grad, kv_grad, w_qkv, cos, sin, normed_all, tokens,
-            both_gains, middle_grad, gate_got, down_sum, attended,
+            attend_gain, middle_grad, gate_got, down_sum, attended,
             branch_all.reshape(plane, D), feed_sum, down_part, middle, gate_late,
         )
-        activations, input_grad, qkv_out, out_out, gate_out, down_out = wrap(*sums)
-        width = D // shards
-        return (
-            activations,
-            input_grad,
-            qkv_out,
-            out_out,
-            gate_out,
-            down_out,
-            gain_out[0, :width],
-            gain_out[1, :width],
-        )
+        return wrap(*sums)
 
     return local
 

time: 277 us -> 272 us (0.982)
  no operation moved by 1% of the time
where the time goes in v9:
time: 272 us; the launch traced here: 271 us
  Pallas kernels  271 us (100%)
    pallas_call x1, Pallas kernels, feed(): pl.pallas_call(kernel, name='feed', in_specs=[vmem] * len(operands), out_...  75.9 us
    pallas_call x1, Pallas kernels, head(): pl.pallas_call(kernel, name='head', in_specs=[vmem] * 6 + [pl.BlockSpec(m...  71.5 us
    pallas_call x1, Pallas kernels, finish(): pl.pallas_call(kernel, name='finish', in_specs=[vmem] * len(operands), ou...  67.6 us
    pallas_call x1, Pallas kernels, attend_backward(): pl.pallas_call(kernel, name='attend_backward', in_specs=[vmem] * 8 + [any...  51.3 us

profile of v9, /device:TPU:0, one launch (start us, length us, event | category | flops | bytes accessed | tf_op | source)
XLA Modules:
  0.0 271.2 jit_solution(6348005263633578217)
XLA Ops:
  0.6 71.5 %head.1 = (bf16[768,384]{1,0:T(8,128)(2,1)}, bf16[4,768,256]{2,1,0:T(8,128)(2,1)}, bf16[4,192,1152]{2,1,0:T(8,128)(2,1)}, bf16[4,288,640]{2,1,0:T(8,128)(2,1)}, ...) custom-call(bf16[192,1152]{1,0:T(8,128)(2,1)} %x_ref.5, ...), custom_call_target="tpu_custom_call" | custom-call | tf_op jit(solution)/shard_map/head/pallas_call | solution.py:801
  72.2 75.9 %feed.1 = (f32[192,1152]{1,0:T(8,128)}, f32[192,1152]{1,0:T(8,128)}, bf16[4,192,1152]{2,1,0:T(8,128)(2,1)}, bf16[768,384]{1,0:T(8,128)(2,1)}, f32[1,1152]{1,0:T(...) custom-call(bf16[768,384]{1,0:T(8,128)(2,1)} %get-tuple-element.50.a, ...), custom_call_target="tpu_custom_call" | custom-call | tf_op jit(solution)/shard_map/feed/pallas_call | solution.py:545
  148.0 51.3 %attend_backward.1 = (bf16[768,384]{1,0:T(8,128)(2,1)}, bf16[4,768,256]{2,1,0:T(8,128)(2,1)}, bf16[4,288,384]{2,1,0:T(8,128)(2,1)}) custom-call(bf16[768,384]{1,0:T(8,128)(2,1)} %get-tuple-element.43.q_ref, bf16[3072,256]{1,0:T(8,128)(2,1)} %bitcast.10, f32[8,768]{1,0:T(8,128)} %get-tuple-element.45.qm_ref, f32[3072,128]{1,0:T(8,128)} %get-tuple-element.46.kp_ref, ...), custom_call_target="tpu_custom_call" | custom-call | tf_op jit(solution)/shard_map/attend_backward/pallas_call | solution.py:229
  199.3 67.6 %finish.1 = (bf16[192,1152]{1,0:T(8,128)(2,1)}, f32[192,1152]{1,0:T(8,128)}, bf16[4,72,384]{2,1,0:T(8,128)(2,1)}, bf16[4,72,256]{2,1,0:T(8,128)(2,1)}, bf16[2,72...) custom-call(bf16[768,384]{1,0:T(8,128)(2,1)} %get-tuple-element.55.q, ...), custom_call_target="tpu_custom_call" | custom-call | tf_op jit(solution)/shard_map/finish/pallas_call | solution.py:1180
  266.9 4.3 %wrap.1 = (bf16[192,1152]{1,0:T(8,128)(2,1)}, f32[192,1152]{1,0:T(8,128)}, f32[72,1920]{1,0:T(8,128)}, f32[72,1152]{1,0:T(8,128)}, f32[72,6144]{1,0:T(8,128)}, /...) custom-call(bf16[192,1152]{1,0:T(8,128)(2,1)} %get-tuple-element.69.act_in, f32[192,1152]{1,0:T(8,128)} %get-tuple-element.70.ig_in, ...), custom_call_target="tpu_custom_call" | custom-call | tf_op jit(solution)/shard_map/wrap/pallas_call | solution.py:1260

commit v10 on v9

--- a/solution.py
+++ b/solution.py
@@ -701,9 +701,6 @@
         gather.wait_y()
         block(y, 2)
         gather.wait_z()
-        block(z, 3)
-        dy_gather.relay()
-
         def columns(p):
             left = core * FF + p * units
             return gu_ref.at[:, pl.ds(pl.multiple_of(left, 128), units)]
@@ -714,6 +711,9 @@
         inward = pltpu.make_async_copy(columns(own), bounce, near)
         outward = pltpu.make_async_copy(bounce, wh_ref.at[own], near)
         inward.start()
+
+        block(z, 3)
+        dy_gather.relay()
 
         for w in range(wsh):
             q_marks[:, w * own_rows : w * own_rows + own_rows] = marks_all[my_c, w, :, :own_rows]

time: 272 us -> 272 us (level)
  no operation moved by 1% of the time
where the time goes in v10:
time: 272 us; the launch traced here: 271 us
  Pallas kernels  270 us (99%)
    pallas_call x1, Pallas kernels, feed(): pl.pallas_call(kernel, name='feed', in_specs=[vmem] * len(operands), out_...  75.9 us
    pallas_call x1, Pallas kernels, head(): pl.pallas_call(kernel, name='head', in_specs=[vmem] * 6 + [pl.BlockSpec(m...  71.5 us
    pallas_call x1, Pallas kernels, finish(): pl.pallas_call(kernel, name='finish', in_specs=[vmem] * len(operands), ou...  67.6 us
    pallas_call x1, Pallas kernels, attend_backward(): pl.pallas_call(kernel, name='attend_backward', in_specs=[vmem] * 8 + [any...  51.3 us

profile of v10, /device:TPU:0, one launch (start us, length us, event | category | flops | bytes accessed | tf_op | source)
XLA Modules:
  0.0 271.1 jit_solution(4609725525053485268)
XLA Ops:
  0.6 71.5 %head.1 = (bf16[768,384]{1,0:T(8,128)(2,1)}, bf16[4,768,256]{2,1,0:T(8,128)(2,1)}, bf16[4,192,1152]{2,1,0:T(8,128)(2,1)}, bf16[4,288,640]{2,1,0:T(8,128)(2,1)}, ...) custom-call(bf16[192,1152]{1,0:T(8,128)(2,1)} %x_ref.5, ...), custom_call_target="tpu_custom_call" | custom-call | tf_op jit(solution)/shard_map/head/pallas_call | solution.py:801
  72.1 75.9 %feed.1 = (f32[192,1152]{1,0:T(8,128)}, f32[192,1152]{1,0:T(8,128)}, bf16[4,192,1152]{2,1,0:T(8,128)(2,1)}, bf16[768,384]{1,0:T(8,128)(2,1)}, f32[1,1152]{1,0:T(...) custom-call(bf16[768,384]{1,0:T(8,128)(2,1)} %get-tuple-element.50.a, ...), custom_call_target="tpu_custom_call" | custom-call | tf_op jit(solution)/shard_map/feed/pallas_call | solution.py:545
  148.0 51.3 %attend_backward.1 = (bf16[768,384]{1,0:T(8,128)(2,1)}, bf16[4,768,256]{2,1,0:T(8,128)(2,1)}, bf16[4,288,384]{2,1,0:T(8,128)(2,1)}) custom-call(bf16[768,384]{1,0:T(8,128)(2,1)} %get-tuple-element.43.q_ref, bf16[3072,256]{1,0:T(8,128)(2,1)} %bitcast.10, f32[8,768]{1,0:T(8,128)} %get-tuple-element.45.qm_ref, f32[3072,128]{1,0:T(8,128)} %get-tuple-element.46.kp_ref, ...), custom_call_target="tpu_custom_call" | custom-call | tf_op jit(solution)/shard_map/attend_backward/pallas_call | solution.py:229
  199.3 67.6 %finish.1 = (bf16[192,1152]{1,0:T(8,128)(2,1)}, f32[192,1152]{1,0:T(8,128)}, bf16[4,72,384]{2,1,0:T(8,128)(2,1)}, bf16[4,72,256]{2,1,0:T(8,128)(2,1)}, bf16[2,72...) custom-call(bf16[768,384]{1,0:T(8,128)(2,1)} %get-tuple-element.55.q, ...), custom_call_target="tpu_custom_call" | custom-call | tf_op jit(solution)/shard_map/finish/pallas_call | solution.py:1180
  266.9 4.3 %wrap.1 = (bf16[192,1152]{1,0:T(8,128)(2,1)}, f32[192,1152]{1,0:T(8,128)}, f32[72,1920]{1,0:T(8,128)}, f32[72,1152]{1,0:T(8,128)}, f32[72,6144]{1,0:T(8,128)}, /...) custom-call(bf16[192,1152]{1,0:T(8,128)(2,1)} %get-tuple-element.69.act_in, f32[192,1152]{1,0:T(8,128)} %get-tuple-element.70.ig_in, ...), custom_call_target="tpu_custom_call" | custom-call | tf_op jit(solution)/shard_map/wrap/pallas_call | solution.py:1260
